TPU v7x, 512 devices: a whole 4x8x8 slice. The times are simulated.
512 devices in a mesh: region: 32 (over x, z), tm: 16 (over y, core).
Axes of the slice: x: 4, y: 8, z: 8, core: 2. Of those that a mesh axis runs over, the one named last changes fastest.
Arguments:
- right_side: float32 [1024, 65536], P('tm', 'region'), may hold values from -9 to 9
- initial: float32 [1024, 65536], P('tm', 'region'), may hold values from -1.5 to 1.5
- blocks: bfloat16 [512, 9, 128, 128], P(('region', 'tm')), may hold values from -2.5 to 3.1, as said below
- neighbour_blocks: int32 [512, 8], P('region'), may hold values from 0 to 511, as said below
- temporal_cov: bfloat16 [1024, 1024], P('tm'), may hold values from -2.5 to 2.8, as said below
Outputs:
- solution: float32 [1024, 65536], P('tm', 'region')
- residual: float32 [1024, 65536], P('tm', 'region')
Inputs may be any that keep to these rules, and one draw needn't show every extreme that they name: blocks[i, 0] is symmetric positive definite. `neighbour_blocks`: each column names every block exactly once. Blocks fall into cyclic windows of 16 consecutive blocks starting at 8 + m * 16, and every block listed for row i lies in the window of i. temporal_cov is symmetric positive definite.
All inputs are finite; a program needn't handle non-finite values.
Results may differ from a plain program's by a relative error of at most 0.012.
The roundings to bfloat16 on the way count: a program that leaves them out, or rounds other values in their place, can miss the bound.
Values may be sent and summed in bfloat16 or wider, within the bound.
No kernel may reach another device: no remote copies, remote signals or barrier semaphores. Data moves between devices by JAX's collectives and lax.ppermute only.
A program may use at most 64 MiB of HBM per device.

v0:
```python
import jax
import jax.numpy as jnp
from jax import lax
from jax.sharding import Mesh
from jax.sharding import PartitionSpec as P

ITERS = 2
REGION = ("region_0", "region_1")
TM = ("tm_0", "tm_1")
REGION_TM = ("region_0", "region_1", "tm_0", "tm_1")


def with_halo(value, sides, width):
    for axis, dim in sides:
        peers, length = (lax.axis_size(axis), value.shape[dim])
        up = [(i, (i + 1) % peers) for i in range(peers)]
        down = [(j, i) for i, j in up]
        last = lax.slice_in_dim(value, length - width, length, axis=dim)
        initial = lax.slice_in_dim(value, 0, width, axis=dim)
        before = lax.ppermute(last, axis, up)
        after = lax.ppermute(initial, axis, down)
        value = jnp.concatenate([before, value, after], axis=dim)
    return value


def gather_axes(value, axes, dim):
    for axis in reversed(axes):
        value = lax.all_gather(value, axis, axis=dim, tiled=True)
    return value


def one_axis_at_a_time(value, axes):
    for axis in axes:
        value = lax.psum(value, axis)
    return value


def local_tiles(lowered, neighbour_blocks):
    row_count = neighbour_blocks.shape[0]
    tile_width = lowered.shape[1] // row_count
    widened = with_halo(lowered, ((REGION, 1),), row_count // 2 * tile_width)
    region = lax.axis_index(REGION)
    block_total = row_count * lax.axis_size(REGION)
    offset = jnp.mod(neighbour_blocks - region * row_count + row_count // 2, block_total)
    itself = (jnp.arange(row_count, dtype=jnp.int32) + row_count // 2)[:, None]
    places = jnp.concatenate([itself, offset], axis=1)
    cell_tiles = widened.reshape(widened.shape[0], 2 * row_count, tile_width)
    return jnp.take(cell_tiles, places, axis=1)


def local(right_side, initial, blocks, neighbour_blocks, temporal_cov):
    hour_matrix = gather_axes(temporal_cov, TM, 0)
    region_blocks = lax.all_gather(blocks, TM, axis=0, tiled=True)
    tm_count = lax.axis_size(TM)
    hour_slice = right_side.shape[0]
    site_count = right_side.shape[1]
    tile_width = blocks.shape[2]
    own_rows = blocks.shape[0]

    def temporal(arrived):
        item_count = arrived.shape[2]
        flattened = arrived.reshape(arrived.shape[0], item_count * tile_width)
        blended = jnp.dot(hour_matrix, flattened, preferred_element_type=jnp.float32).astype(
            jnp.bfloat16
        )
        return blended.reshape(arrived.shape[0], 1, item_count, tile_width)

    def operate(current):
        lowered = current.astype(jnp.bfloat16)
        tile_stack = local_tiles(lowered, neighbour_blocks)
        spatial = jnp.einsum(
            "hrkb,rkab->hra", tile_stack, region_blocks, preferred_element_type=jnp.float32
        )
        spatial = spatial.astype(jnp.bfloat16).reshape(hour_slice, tm_count, own_rows, tile_width)
        blended = temporal(lax.all_to_all(spatial, TM, split_axis=1, concat_axis=0, tiled=True))
        returned = lax.all_to_all(blended, TM, split_axis=0, concat_axis=1, tiled=True)
        return current + returned.reshape(hour_slice, site_count).astype(jnp.float32)

    solution = initial
    residual = right_side - operate(initial)
    direction = residual
    norm_now = one_axis_at_a_time(jnp.sum(residual * residual), REGION_TM)
    for iteration in range(ITERS):
        applied = operate(direction)
        curvature, cross_term, square = (
            one_axis_at_a_time(jnp.sum(direction * applied), REGION_TM),
            one_axis_at_a_time(jnp.sum(residual * applied), REGION_TM),
            one_axis_at_a_time(jnp.sum(applied * applied), REGION_TM),
        )
        step_size = norm_now / curvature
        solution = solution + step_size * direction
        norm_next = norm_now - 2.0 * step_size * cross_term + step_size * step_size * square
        residual = residual - step_size * applied
        if iteration + 1 < ITERS:
            direction = residual + norm_next / norm_now * direction
        norm_now = norm_next
    return (solution, residual)


def solution(mesh):
    split = Mesh(mesh.devices.reshape(4, 8, 8, 2), ("region_0", "region_1", "tm_0", "tm_1"))
    return jax.shard_map(
        local,
        mesh=split,
        in_specs=(
            P(TM, REGION),
            P(TM, REGION),
            P(REGION_TM, None, None, None),
            P(REGION, None),
            P(TM, None),
        ),
        out_specs=(P(TM, REGION), P(TM, REGION)),
        check_vma=False,
    )
```

profile of v0, /device:TPU:1, one launch (start us, length us, event | category | flops | bytes accessed | tf_op | source)
XLA Modules:
  0.0 342.4 jit_solution(12038400127978279072)
XLA Ops:
  7.9 10.2 %all_gather.10 = bf16[128,1024]{1,0:T(8,128)(2,1)} all-gather(bf16[64,1024]{1,0:T(8,128)(2,1)} %param.11), channel_id=1, replica_groups=mesh['region_0'=4,'region_1'=8,'tm_0'=8,'tm_1'=2] {'tm_1'}, dimensions={0}, use_global_device_ids=true | all-gather | bytes 393216 | tf_op jit(solution)/shard_map/all_gather | solution.py:28
  19.3 1.9 collective-permute-start
  21.2 7.5 %collective-permute-start.1 = (bf16[64,1024]{1,0:T(8,128)(2,1)S(1)}, bf16[64,1024]{1,0:T(8,128)(2,1)S(1)}, u32[]{:S(2)}, u32[]{:S(2)}) collective-permute-start(bf16[64,1024]{1,0:T(8,128)(2,1)S(1)} %get-tuple-element.27), channel_id=1, source_target_pairs={{16,0},{32,16},{48,32},{64,48},{80,64},{96,80},{112,96},{128,112},... | collective-permute-start | bytes 393224 | tf_op jit(solution)/shard_map/ppermute | solution.py:21
  32.6 27.8 %all-gather.3.cloned.1.call-done = bf16[16,9,128,128]{3,2,1,0:T(8,128)(2,1)} async-done(((bf16[1,9,128,128]{3,2,1,0:T(8,128)(2,1)}), bf16[16,9,128,128]{3,2,1,0:T(8,128)(2,1)}) %all-gather.3.cloned.1.call-update) | async-done | bytes 4718608 | tf_op jit(solution)/shard_map/all_gather | solution.py:53
  60.5 5.0 %fusion.36 = bf16[64,16,1,128]{3,0,2,1:T(8,128)(2,1)} fusion(bf16[16,9,128,128]{3,2,1,0:T(8,128)(2,1)} %all-gather.3.cloned.1.call-done, bf16[16,9,64,128]{3,2,1,0:T(8,128)(2,1)S(1)} %bitcast.174, pred[16,9]{1,0:T(8,128)(4,1)S(1)} %copy.40), kind=kOutput, calls=%fused_computation.30 | convolution fusion | flops 303300608 | bytes 7340176 | tf_op jit(solution)/shard_map/hrkb,rkab->hra/dot_general | solution.py:71
  65.5 5.0 %all-to-all-start = ((bf16[64,16,1,128]{3,0,2,1:T(8,128)(2,1)}), bf16[64,16,1,128]{3,0,2,1:T(8,128)(2,1)S(1)}, u32[]{:S(2)}, u32[]{:S(2)}) async-start(bf16[64,16,1,128]{3,0,2,1:T(8,128)(2,1)} %fusion.36), calls=%async_computation | async-start | bytes 524288 | tf_op jit(solution)/shard_map/all_to_all | solution.py:75
  70.5 31.9 %all-gather.5.cloned.1.call-done = bf16[1024,1024]{1,0:T(8,128)(2,1)} async-done(((bf16[128,1024]{1,0:T(8,128)(2,1)}), bf16[1024,1024]{1,0:T(8,128)(2,1)}) %all-gather.5.cloned.1.call-update) | async-done | bytes 2097168 | tf_op jit(solution)/shard_map/all_gather | solution.py:28
  102.3 2.4 fusion.33
  106.3 20.0 %all_to_all.72 = bf16[16,2,4096]{2,1,0:T(2,128)(2,1)S(1)} all-to-all(bf16[16,2,4096]{2,1,0:T(2,128)(2,1)S(1)} %reshape.136), channel_id=1, replica_groups=mesh['region_0'=4,'region_1'=8,'tm_0'=8,'tm_1'=2] {'tm_0','tm_1'}, dimensions={0} | all-to-all | bytes 524288 | tf_op jit(solution)/shard_map/all_to_all | solution.py:76
  127.3 3.3 collective-permute-start.2
  130.6 6.4 %collective-permute-start.3 = (bf16[64,1024]{1,0:T(8,128)(2,1)S(1)}, bf16[64,1024]{1,0:T(8,128)(2,1)S(1)}, u32[]{:S(2)}, u32[]{:S(2)}) collective-permute-start(bf16[64,1024]{1,0:T(8,128)(2,1)S(1)} %get-tuple-element.25), channel_id=1, source_target_pairs={{16,0},{32,16},{48,32},{64,48},{80,64},{96,80},{112,96},{128,112},... | collective-permute-start | bytes 393224 | tf_op jit(solution)/shard_map/ppermute | solution.py:21
  136.9 1.8 collective-permute-done.2
  138.7 1.4 collective-permute-done.3
  140.3 2.5 gather_fusion.1
  142.7 5.1 %fusion.39 = bf16[64,16,1,128]{3,0,2,1:T(8,128)(2,1)S(1)} fusion(bf16[16,9,128,128]{3,2,1,0:T(8,128)(2,1)} %all-gather.3.cloned.1.call-done, bf16[16,9,64,128]{3,2,1,0:T(8,128)(2,1)} %bitcast.176, pred[16,9]{1,0:T(8,128)(4,1)S(1)} %copy.40), kind=kOutput, calls=%fused_computation.31 | convolution fusion | flops 303300608 | bytes 7340176 | tf_op jit(solution)/shard_map/hrkb,rkab->hra/dot_general | solution.py:71
  147.9 14.7 %all_to_all.73 = bf16[64,16,1,128]{3,0,2,1:T(8,128)(2,1)S(1)} all-to-all(bf16[64,16,1,128]{3,0,2,1:T(8,128)(2,1)S(1)} %fusion.39), channel_id=1, replica_groups=mesh['region_0'=4,'region_1'=8,'tm_0'=8,'tm_1'=2] {'tm_0','tm_1'}, dimensions={1} | all-to-all | bytes 524288 | tf_op jit(solution)/shard_map/all_to_all | solution.py:75
  164.5 14.2 %all_to_all.74 = bf16[16,2,4096]{2,1,0:T(2,128)(2,1)S(1)} all-to-all(bf16[16,2,4096]{2,1,0:T(2,128)(2,1)S(1)} %reshape.138), channel_id=1, replica_groups=mesh['region_0'=4,'region_1'=8,'tm_0'=8,'tm_1'=2] {'tm_0','tm_1'}, dimensions={0} | all-to-all | bytes 524288 | tf_op jit(solution)/shard_map/all_to_all | solution.py:76
  180.3 7.2 %all-reduce.2 = (f32[]{:T(128)}, f32[]{:T(128)}, f32[]{:T(128)}) all-reduce(f32[]{:T(128)} %get-tuple-element.5, f32[]{:T(128)} %get-tuple-element.4, f32[]{:T(128)} %get-tuple-element.3), channel_id=1, replica_groups=mesh['region_0'=4,'region_1'=8,'tm_0'=8,'tm_1'=2] {'region_0'}, use_global_device_ids=true, to_apply=%region_1.3 | all-reduce | flops 3 | bytes 24 | tf_op jit(solution)/shard_map/psum | solution.py:34
  187.5 16.8 %all-reduce.1 = (f32[]{:T(128)}, f32[]{:T(128)}, f32[]{:T(128)}) all-reduce(f32[]{:T(128)} %get-tuple-element.12, f32[]{:T(128)} %get-tuple-element.13, f32[]{:T(128)} %get-tuple-element.14), channel_id=1, replica_groups=mesh['region_0'=4,'region_1'=8,'tm_0'=8,'tm_1'=2] {'region_1'}, use_global_device_ids=true, to_apply=%region_2.4 | all-reduce | flops 3 | bytes 24 | tf_op jit(solution)/shard_map/psum | solution.py:34
  204.3 11.7 %all-reduce = (f32[]{:T(128)}, f32[]{:T(128)}, f32[]{:T(128)}) all-reduce(f32[]{:T(128)} %get-tuple-element.9, f32[]{:T(128)} %get-tuple-element.10, f32[]{:T(128)} %get-tuple-element.11), channel_id=1, replica_groups=mesh['region_0'=4,'region_1'=8,'tm_0'=8,'tm_1'=2] {'tm_0'}, use_global_device_ids=true, to_apply=%region_3.5 | all-reduce | flops 3 | bytes 24 | tf_op jit(solution)/shard_map/psum | solution.py:34
  216.0 11.5 %all-reduce.3 = (f32[]{:T(128)}, f32[]{:T(128)}, f32[]{:T(128)}) all-reduce(f32[]{:T(128)} %get-tuple-element.6, f32[]{:T(128)} %get-tuple-element.7, f32[]{:T(128)} %get-tuple-element.8), channel_id=1, replica_groups=mesh['region_0'=4,'region_1'=8,'tm_0'=8,'tm_1'=2] {'tm_1'}, use_global_device_ids=true, to_apply=%region_4.6 | all-reduce | flops 3 | bytes 24 | tf_op jit(solution)/shard_map/psum | solution.py:34
  231.4 1.9 collective-permute-start.4
  233.3 6.7 %collective-permute-start.5 = (bf16[64,1024]{1,0:T(8,128)(2,1)S(1)}, bf16[64,1024]{1,0:T(8,128)(2,1)S(1)}, u32[]{:S(2)}, u32[]{:S(2)}) collective-permute-start(bf16[64,1024]{1,0:T(8,128)(2,1)S(1)} %get-tuple-element.23), channel_id=1, source_target_pairs={{16,0},{32,16},{48,32},{64,48},{80,64},{96,80},{112,96},{128,112},... | collective-permute-start | bytes 393224 | tf_op jit(solution)/shard_map/ppermute | solution.py:21
  242.4 2.5 gather_fusion.2
  244.9 5.0 %fusion.42 = bf16[64,16,1,128]{3,0,2,1:T(8,128)(2,1)S(1)} fusion(bf16[16,9,128,128]{3,2,1,0:T(8,128)(2,1)} %all-gather.3.cloned.1.call-done, bf16[16,9,64,128]{3,2,1,0:T(8,128)(2,1)} %bitcast.175, pred[16,9]{1,0:T(8,128)(4,1)S(1)} %copy.40), kind=kOutput, calls=%fused_computation.32 | convolution fusion | flops 303300608 | bytes 7340176 | tf_op jit(solution)/shard_map/hrkb,rkab->hra/dot_general | solution.py:71
  249.9 18.4 %all_to_all.75 = bf16[64,16,1,128]{3,0,2,1:T(8,128)(2,1)S(1)} all-to-all(bf16[64,16,1,128]{3,0,2,1:T(8,128)(2,1)S(1)} %fusion.42), channel_id=1, replica_groups=mesh['region_0'=4,'region_1'=8,'tm_0'=8,'tm_1'=2] {'tm_0','tm_1'}, dimensions={1} | all-to-all | bytes 524288 | tf_op jit(solution)/shard_map/all_to_all | solution.py:75
  270.1 14.5 %all_to_all.76 = bf16[16,2,4096]{2,1,0:T(2,128)(2,1)S(1)} all-to-all(bf16[16,2,4096]{2,1,0:T(2,128)(2,1)S(1)} %reshape.140), channel_id=1, replica_groups=mesh['region_0'=4,'region_1'=8,'tm_0'=8,'tm_1'=2] {'tm_0','tm_1'}, dimensions={0} | all-to-all | bytes 524288 | tf_op jit(solution)/shard_map/all_to_all | solution.py:76
  286.4 6.7 %psum.136 = f32[]{:T(128)} all-reduce(f32[]{:T(128)} %multiply_reduce_fusion), channel_id=1, replica_groups=mesh['region_0'=4,'region_1'=8,'tm_0'=8,'tm_1'=2] {'region_0'}, use_global_device_ids=true, to_apply=%region_16.18 | all-reduce | flops 1 | bytes 8 | tf_op jit(solution)/shard_map/psum | solution.py:34
  293.1 17.2 %psum.137 = f32[]{:T(128)} all-reduce(f32[]{:T(128)} %psum.136), channel_id=1, replica_groups=mesh['region_0'=4,'region_1'=8,'tm_0'=8,'tm_1'=2] {'region_1'}, use_global_device_ids=true, to_apply=%region_17.19 | all-reduce | flops 1 | bytes 8 | tf_op jit(solution)/shard_map/psum | solution.py:34
  310.3 11.6 %psum.138 = f32[]{:T(128)} all-reduce(f32[]{:T(128)} %psum.137), channel_id=1, replica_groups=mesh['region_0'=4,'region_1'=8,'tm_0'=8,'tm_1'=2] {'tm_0'}, use_global_device_ids=true, to_apply=%region_18.20 | all-reduce | flops 1 | bytes 8 | tf_op jit(solution)/shard_map/psum | solution.py:34
  321.9 11.5 %psum.139 = f32[]{:T(128)} all-reduce(f32[]{:T(128)} %psum.138), channel_id=1, replica_groups=mesh['region_0'=4,'region_1'=8,'tm_0'=8,'tm_1'=2] {'tm_1'}, use_global_device_ids=true, to_apply=%region_19.21 | all-reduce | flops 1 | bytes 8 | tf_op jit(solution)/shard_map/psum | solution.py:34
  334.1 1.5 multiply_subtract_fusion
  (65 shorter events, 17.8 us)
Async XLA Ops:
  7.2 53.3 %all-gather.3.cloned.1.call-start = ((), (), s32[]{:S(2)}) async-start(), calls=%async_computation.6 | async-start | bytes 5013504 | tf_op jit(solution)/shard_map/all_gather | solution.py:53
  7.9 94.4 %all-gather.5.cloned.1.call-start = ((), (), s32[]{:S(2)}) async-start(), calls=%async_computation.7 | async-start | bytes 2359296 | tf_op jit(solution)/shard_map/all_gather | solution.py:28
  19.3 11.2 %collective-permute-start = (bf16[64,1024]{1,0:T(8,128)(2,1)S(1)}, bf16[64,1024]{1,0:T(8,128)(2,1)S(1)}, u32[]{:S(2)}, u32[]{:S(2)}) collective-permute-start(bf16[64,1024]{1,0:T(8,128)(2,1)S(1)} %get-tuple-element.26), channel_id=1, source_target_pairs={{0,16},{16,32},{32,48},{48,64},{64,80},{80,96},{96,112},{112,128},... | collective-permute-start | bytes 393224 | tf_op jit(solution)/shard_map/ppermute | solution.py:20
  21.2 10.2 %collective-permute-start.1 = (bf16[64,1024]{1,0:T(8,128)(2,1)S(1)}, bf16[64,1024]{1,0:T(8,128)(2,1)S(1)}, u32[]{:S(2)}, u32[]{:S(2)}) collective-permute-start(bf16[64,1024]{1,0:T(8,128)(2,1)S(1)} %get-tuple-element.27), channel_id=1, source_target_pairs={{16,0},{32,16},{48,32},{64,48},{80,64},{96,80},{112,96},{128,112},... | collective-permute-start | bytes 393224 | tf_op jit(solution)/shard_map/ppermute | solution.py:21
  65.5 36.9 %all-to-all-start = ((bf16[64,16,1,128]{3,0,2,1:T(8,128)(2,1)}), bf16[64,16,1,128]{3,0,2,1:T(8,128)(2,1)S(1)}, u32[]{:S(2)}, u32[]{:S(2)}) async-start(bf16[64,16,1,128]{3,0,2,1:T(8,128)(2,1)} %fusion.36), calls=%async_computation | async-start | bytes 524288 | tf_op jit(solution)/shard_map/all_to_all | solution.py:75
  106.2 20.8 %copy-start.3 = (f32[64,2048]{1,0:T(8,128)S(1)}, f32[64,2048]{1,0:T(8,128)}, u32[]{:S(2)}) copy-start(f32[64,2048]{1,0:T(8,128)} %param.8) | copy-start | bytes 1572868
  106.2 20.8 %copy-start.5 = (f32[64,2048]{1,0:T(8,128)S(1)}, f32[64,2048]{1,0:T(8,128)}, u32[]{:S(2)}) copy-start(f32[64,2048]{1,0:T(8,128)} %param.7) | copy-start | bytes 1572868
  127.3 11.4 %collective-permute-start.2 = (bf16[64,1024]{1,0:T(8,128)(2,1)S(1)}, bf16[64,1024]{1,0:T(8,128)(2,1)S(1)}, u32[]{:S(2)}, u32[]{:S(2)}) collective-permute-start(bf16[64,1024]{1,0:T(8,128)(2,1)S(1)} %get-tuple-element.24), channel_id=1, source_target_pairs={{0,16},{16,32},{32,48},{48,64},{64,80},{80,96},{96,112},{112,128},... | collective-permute-start | bytes 393224 | tf_op jit(solution)/shard_map/ppermute | solution.py:20
  130.6 9.5 %collective-permute-start.3 = (bf16[64,1024]{1,0:T(8,128)(2,1)S(1)}, bf16[64,1024]{1,0:T(8,128)(2,1)S(1)}, u32[]{:S(2)}, u32[]{:S(2)}) collective-permute-start(bf16[64,1024]{1,0:T(8,128)(2,1)S(1)} %get-tuple-element.25), channel_id=1, source_target_pairs={{16,0},{32,16},{48,32},{64,48},{80,64},{96,80},{112,96},{128,112},... | collective-permute-start | bytes 393224 | tf_op jit(solution)/shard_map/ppermute | solution.py:21
  142.7 19.8 %copy-start = (bf16[1024,1024]{1,0:T(8,128)(2,1)S(1)}, bf16[1024,1024]{1,0:T(8,128)(2,1)}, u32[]{:S(2)}) copy-start(bf16[1024,1024]{1,0:T(8,128)(2,1)} %all-gather.5.cloned.1.call-done) | copy-start | bytes 6291460
  179.4 62.0 %copy-start.1 = (f32[64,16,1,1,128]{4,1,0,3,2:T(8,128)}, f32[64,16,1,1,128]{4,1,0,3,2:T(8,128)S(1)}, u32[]{:S(2)}) copy-start(f32[64,16,1,1,128]{4,1,0,3,2:T(8,128)S(1)} %copy.53) | copy-start | bytes 1572868
  231.4 9.9 %collective-permute-start.4 = (bf16[64,1024]{1,0:T(8,128)(2,1)S(1)}, bf16[64,1024]{1,0:T(8,128)(2,1)S(1)}, u32[]{:S(2)}, u32[]{:S(2)}) collective-permute-start(bf16[64,1024]{1,0:T(8,128)(2,1)S(1)} %get-tuple-element.22), channel_id=1, source_target_pairs={{0,16},{16,32},{32,48},{48,64},{64,80},{80,96},{96,112},{112,128},... | collective-permute-start | bytes 393224 | tf_op jit(solution)/shard_map/ppermute | solution.py:20
  233.3 8.9 %collective-permute-start.5 = (bf16[64,1024]{1,0:T(8,128)(2,1)S(1)}, bf16[64,1024]{1,0:T(8,128)(2,1)S(1)}, u32[]{:S(2)}, u32[]{:S(2)}) collective-permute-start(bf16[64,1024]{1,0:T(8,128)(2,1)S(1)} %get-tuple-element.23), channel_id=1, source_target_pairs={{16,0},{32,16},{48,32},{64,48},{80,64},{96,80},{112,96},{128,112},... | collective-permute-start | bytes 393224 | tf_op jit(solution)/shard_map/ppermute | solution.py:21
  270.1 15.3 %copy-start.2 = (f32[64,16,1,1,128]{4,1,0,3,2:T(8,128)S(1)}, f32[64,16,1,1,128]{4,1,0,3,2:T(8,128)}, u32[]{:S(2)}) copy-start(f32[64,16,1,1,128]{4,1,0,3,2:T(8,128)} %copy-done.1) | copy-start | bytes 1572868
  284.6 49.4 %copy-start.4 = (f32[64,2048]{1,0:T(8,128)S(1)}, f32[64,2048]{1,0:T(8,128)}, u32[]{:S(2)}) copy-start(f32[64,2048]{1,0:T(8,128)} %param.8) | copy-start | bytes 1572868
Sparse Core Ops, SparseCore 0:
  10.1 50.3 all-gather.2
  62.5 39.7 all-gather.4
where the time goes:
time: 343 us; the launch traced here: 342 us
  blocking collectives  186 us (54%)
  waiting for transfers between devices  67.4 us (20%)
  starting transfers between devices  32.7 us (10%)
  matrix products  19.2 us (6%)
  between operations  18.8 us (5%)
  local copies, waits for them, and re-layouts  9.38 us (3%)
  other arithmetic  8.5 us (2%)
    psum x8, blocking collectives, one_axis_at_a_time(): value = lax.psum(value, axis)  94.3 us
    all_to_all x3, blocking collectives, operate(): lax.all_to_all(blended, TM, split_axis=0, concat_axis=1, tiled=True)  48.7 us
    all_to_all x2, blocking collectives, operate(): lax.all_to_all(spatial, TM, split_axis=1, concat_axis=0, tiled=True)  33.1 us
    all_gather x1, waiting for transfers between devices, gather_axes(): value = lax.all_gather(value, axis, axis=dim, tiled=True)  31.9 us
    all_gather x1, waiting for transfers between devices, local(): region_blocks = lax.all_gather(blocks, TM, axis=0, tiled=True)  27.8 us
    ppermute x3, starting transfers between devices, with_halo(): after = lax.ppermute(initial, axis, down)  20.6 us
    dot_general x3, matrix products, operate(): jnp.einsum('hrkb,rkab->hra', tile_stack, region_blocks, preferred_element...  15.1 us
    all_gather x1, blocking collectives, gather_axes(): value = lax.all_gather(value, axis, axis=dim, tiled=True)  10.2 us
  transfers between devices with their start and end apart: 9, of which 8 were waited for; matrix products, arithmetic and copies ran while one was open for 2% of the time, Pallas kernels for 0%

commit v1 on v0

v1 whole, which is shorter than its diff:
```python
import jax
import jax.numpy as jnp
from jax import lax
from jax.experimental import pallas as pl
from jax.experimental.pallas import tpu as pltpu
from jax.sharding import Mesh
from jax.sharding import PartitionSpec as P

REGION = ("region_0", "region_1")
TM = ("tm_0", "tm_1")
REGION_TM = ("region_0", "region_1", "tm_0", "tm_1")
F32 = jnp.float32
BF16 = jnp.bfloat16
VMEM = pl.BlockSpec(memory_space=pltpu.MemorySpace.VMEM)
SMEM = pl.BlockSpec(memory_space=pltpu.MemorySpace.SMEM)


def dot(a, b):
    return jnp.dot(a, b, preferred_element_type=F32)


def temporal_kernel(c_ref, v_ref, w_ref, shift_ref):
    hours, wide = v_ref.shape
    n = wide // 2
    row = lax.broadcasted_iota(jnp.int32, (n, n), 0)
    col = lax.broadcasted_iota(jnp.int32, (n, n), 1)
    diagonal = jnp.zeros((n, n), F32)
    for k in range(hours // n):
        tile = c_ref[k * n : (k + 1) * n, k * n : (k + 1) * n].astype(F32)
        diagonal = diagonal + jnp.where(row == col, tile, 0.0)
    c0 = jnp.sum(diagonal, axis=(0, 1), keepdims=True) / hours
    shift_ref[...] = jnp.broadcast_to(c0, shift_ref.shape)
    v = v_ref[...]
    first = (dot(c_ref[...], v) - c0 * v.astype(F32)).astype(BF16)
    w_ref[:, :wide] = first
    second = (dot(c_ref[...], first) - c0 * first.astype(F32)).astype(BF16)
    w_ref[:, wide : 2 * wide] = second
    third = second[:, :n]
    w_ref[:, 2 * wide :] = (dot(c_ref[...], third) - c0 * third.astype(F32)).astype(BF16)


def spatial_kernel(
    slots_ref, g_ref, xd_ref, shift_ref, b_ref, low_ref, high_ref, gram_ref, b_buf, f_buf, z_buf, w_buf, sums, sem
):
    rows, hours, n = f_buf.shape[0], xd_ref.shape[1], xd_ref.shape[2] // 2
    half = rows // 2
    slots = slots_ref.shape[1]

    def load(i):
        return pltpu.make_async_copy(b_ref.at[i], b_buf.at[i], sem.at[i])

    for i in range(rows):
        load(i).start()
    c0 = shift_ref[0:1, 0:1]
    for i in range(rows):
        x = xd_ref[i, :, 0:n].astype(F32)
        y1 = g_ref[i, :, 0:n].astype(F32)
        y2 = g_ref[i, :, 2 * n : 3 * n].astype(F32)
        y3 = g_ref[i, :, 4 * n : 5 * n].astype(F32)
        f_buf[i, 0:hours, :] = (c0 * x + y1).astype(BF16)
        f_buf[i, hours : 2 * hours, :] = (c0 * y1 + y2).astype(BF16)
        f_buf[i, 2 * hours :, :] = (c0 * y2 + y3).astype(BF16)

    def product(source, i):
        tiles = [source[i]] + [source[slots_ref[i, k]] for k in range(slots)]
        return dot(jnp.concatenate(tiles, axis=1), b_buf[i])

    def split(value):
        top = value.astype(BF16)
        return top, (value - top.astype(F32)).astype(BF16)

    def put(k, i, value):
        @pl.when(i < half)
        def _():
            low_ref[k, i] = value

        @pl.when(i >= half)
        def _():
            high_ref[k, i - half] = value

    def get(k, i):
        return jnp.where(i < half, low_ref[k, jnp.minimum(i, half - 1)], high_ref[k, jnp.maximum(i - half, 0)])

    def stage_one(i, _):
        load(i).wait()
        out = product(f_buf, i)
        d = xd_ref[i, :, n : 2 * n].astype(F32)
        e1 = g_ref[i, :, n : 2 * n].astype(F32)
        e2 = g_ref[i, :, 3 * n : 4 * n].astype(F32)
        r0 = d - out[0:hours]
        u1 = e1 - out[hours : 2 * hours]
        u2 = e2 - out[2 * hours :]
        put(0, i, r0)
        for k, z in enumerate((c0 * r0 + u1, c0 * (c0 * r0 + 2.0 * u1) + u2)):
            top, rest = split(z)
            z_buf[i, 2 * k * hours : (2 * k + 1) * hours, :] = top
            z_buf[i, (2 * k + 1) * hours : (2 * k + 2) * hours, :] = rest
        return 0

    def stage_two(i, _):
        out = product(z_buf, i)
        put(1, i, out[0:hours] + out[hours : 2 * hours])
        top, rest = split(out[2 * hours : 3 * hours] + out[3 * hours :])
        w_buf[i, 0:hours, :] = top
        w_buf[i, hours:, :] = rest
        return 0

    def add(k, value):
        sums[k] += jnp.sum(value.reshape(hours // 8, 8, n), axis=0)

    def stage_three(i, _):
        out = product(w_buf, i)
        m2 = out[0:hours] + out[hours:]
        put(2, i, m2)
        r0, m1 = get(0, i), get(1, i)
        add(0, r0 * r0)
        add(1, r0 * m1)
        add(2, m1 * m1)
        add(3, r0 * m2)
        add(4, m1 * m2)
        return 0

    sums[...] = jnp.zeros_like(sums)
    lax.fori_loop(0, rows, stage_one, 0)
    lax.fori_loop(0, rows, stage_two, 0)
    lax.fori_loop(0, rows, stage_three, 0)
    gram = jnp.sum(sums[...], axis=1)
    for k in range(gram_ref.shape[0]):
        gram_ref[k] = gram


def finish_kernel(gram_ref, x_ref, low_ref, high_ref, solution_ref, residual_ref):
    total = jnp.sum(jnp.sum(gram_ref[...], axis=0), axis=1, keepdims=True)
    rr, rm1, m11, rm2, m12 = (total[k : k + 1, 0:1] for k in range(5))
    rq = rr + rm1
    qq = rr + 2.0 * rm1 + m11
    rs = rr + 2.0 * rm1 + rm2
    qs = rr + 3.0 * rm1 + rm2 + 2.0 * m11 + m12
    alpha = rr / rq
    norm = rr - 2.0 * alpha * rq + alpha * alpha * qq
    keep = 1.0 + norm / rr
    curvature = keep * keep * rq - alpha * keep * (rs + qq) + alpha * alpha * qs
    step = norm / curvature
    half, n = low_ref.shape[1], low_ref.shape[3]
    for part, ref in ((0, low_ref), (1, high_ref)):
        for i in range(half):
            lanes = slice((part * half + i) * n, (part * half + i + 1) * n)
            r0, m1, m2 = ref[0, i], ref[1, i], ref[2, i]
            q = r0 + m1
            p1 = keep * r0 - alpha * q
            image = keep * q - alpha * (q + m1 + m2)
            solution_ref[:, lanes] = x_ref[:, lanes] + alpha * r0 + step * p1
            residual_ref[:, lanes] = r0 - alpha * q - step * image


def local(right_side, initial, blocks, neighbour_blocks, temporal_cov):
    hours, sites = right_side.shape
    n = blocks.shape[2]
    width = blocks.shape[1]
    rows = neighbour_blocks.shape[0]
    half = rows // 2
    slots = neighbour_blocks.shape[1]
    tm_count = lax.axis_size(TM)
    regions = lax.axis_size(REGION)

    covariance = lax.all_gather(temporal_cov, TM, axis=0, tiled=True)

    x = initial.astype(BF16).reshape(hours, rows, 1, n)
    d = (right_side - initial).astype(BF16).reshape(hours, rows, 1, n)
    pack = jnp.concatenate([x, d], axis=2).transpose(1, 0, 2, 3).reshape(rows, hours, 2 * n)
    local_slots = jnp.mod(neighbour_blocks, rows)
    extra = jnp.pad(local_slots[:half].astype(BF16)[:, None, :], ((0, 0), (0, 15), (0, 2 * n - slots)))
    shifted = lax.ppermute(
        jnp.concatenate([pack[:half], extra], axis=1), REGION, [((r + 1) % regions, r) for r in range(regions)]
    )
    xd = jnp.concatenate([shifted[:, :hours], pack[half:]], axis=0)
    window_slots = jnp.concatenate([shifted[:, hours, :slots].astype(jnp.int32), local_slots[half:]], axis=0)

    pairs = [
        (((r + (t < half)) % regions) * tm_count + t, r * tm_count + t) for r in range(regions) for t in range(tm_count)
    ]
    flipped = jnp.swapaxes(blocks[0], 1, 2).reshape(1, width * n, n)
    window_blocks = lax.all_gather(lax.ppermute(flipped, REGION_TM, pairs), TM, axis=0, tiled=True)

    arrived = lax.all_to_all(xd, TM, split_axis=0, concat_axis=0, tiled=True)
    powers, shift = pl.pallas_call(
        temporal_kernel,
        out_shape=(
            jax.ShapeDtypeStruct((tm_count * hours, 5 * n), BF16),
            jax.ShapeDtypeStruct((8, n), F32),
        ),
        in_specs=[VMEM, VMEM],
        out_specs=(VMEM, VMEM),
        name="temporal",
    )(covariance, arrived.reshape(tm_count * hours, 2 * n))
    returned = lax.all_to_all(powers.reshape(tm_count, hours, 5 * n), TM, split_axis=0, concat_axis=0, tiled=True)

    low, high, gram = pl.pallas_call(
        spatial_kernel,
        out_shape=(
            jax.ShapeDtypeStruct((3, half, hours, n), F32),
            jax.ShapeDtypeStruct((3, half, hours, n), F32),
            jax.ShapeDtypeStruct((tm_count, 8, n), F32),
        ),
        in_specs=[SMEM, VMEM, VMEM, VMEM, pl.BlockSpec(memory_space=pl.ANY)],
        out_specs=(VMEM, VMEM, VMEM),
        scratch_shapes=[
            pltpu.VMEM((rows, width * n, n), BF16),
            pltpu.VMEM((rows, 3 * hours, n), BF16),
            pltpu.VMEM((rows, 4 * hours, n), BF16),
            pltpu.VMEM((rows, 2 * hours, n), BF16),
            pltpu.VMEM((8, 8, n), F32),
            pltpu.SemaphoreType.DMA((rows,)),
        ],
        name="spatial",
    )(window_slots, returned, xd, shift, window_blocks)

    back = lax.ppermute(low, REGION, [(r, (r + 1) % regions) for r in range(regions)])
    over_tm = lax.all_to_all(gram, TM, split_axis=0, concat_axis=0, tiled=True)
    spread = jnp.broadcast_to(jnp.sum(over_tm, axis=0)[None], (regions, 8, n))
    over_region = lax.all_to_all(spread, REGION, split_axis=0, concat_axis=0, tiled=True)
    return pl.pallas_call(
        finish_kernel,
        out_shape=(
            jax.ShapeDtypeStruct((hours, sites), F32),
            jax.ShapeDtypeStruct((hours, sites), F32),
        ),
        in_specs=[VMEM, VMEM, VMEM, VMEM],
        out_specs=(VMEM, VMEM),
        name="finish",
    )(over_region, initial, back, high)


def solution(mesh):
    split = Mesh(mesh.devices.reshape(4, 8, 8, 2), ("region_0", "region_1", "tm_0", "tm_1"))
    return jax.shard_map(
        local,
        mesh=split,
        in_specs=(
            P(TM, REGION),
            P(TM, REGION),
            P(REGION_TM, None, None, None),
            P(REGION, None),
            P(TM, None),
        ),
        out_specs=(P(TM, REGION), P(TM, REGION)),
        check_vma=False,
    )
```

time: 343 us -> 197 us (0.57)
  blocking collectives: 186 us -> 54.8 us
  Pallas kernels: 0 us -> 25.9 us
  matrix products: 19.2 us -> 0 us
  starting transfers between devices: 32.7 us -> 26.8 us
  other arithmetic: 8.5 us -> 3.39 us
  local copies, waits for them, and re-layouts: 9.38 us -> 4.71 us
  between operations: 18.8 us -> 14.2 us
    psum x8 -> x0, blocking collectives: 94.3 us -> none  [one_axis_at_a_time(): value = lax.psum(value, axis)]
    all_gather x2, waiting for transfers between devices: 59.7 us -> 11.1 us  [the longest x1 11.1 us: local(): lax.all_gather(lax.ppermute(flipped, REGION_TM, pairs), TM, axis=0, tiled...]
    all_to_all x1, waiting for transfers between devices: 0.01 us -> 44.2 us  [local(): lax.all_to_all(powers.reshape(tm_count, hours, 5 * n), TM, split_axis=0,...]
    all_to_all x5 -> x3, blocking collectives: 81.8 us -> 54.8 us  [the longest x1 24.3 us: local(): arrived = lax.all_to_all(xd, TM, split_axis=0, concat_axis=0, tiled=True)]
    pallas_call x0 -> x3, Pallas kernels: none -> 25.9 us  [the longest x1 17.3 us: local(): pl.pallas_call(spatial_kernel, out_shape=(jax.ShapeDtypeStruct((3, half,...]
    dot_general x6 -> x0, matrix products: 19.2 us -> none  [the longest x3 15.1 us: operate(): jnp.einsum('hrkb,rkab->hra', tile_stack, region_blocks, preferred_element...]
    all_gather x1 -> x0, blocking collectives: 10.2 us -> none  [gather_axes(): value = lax.all_gather(value, axis, axis=dim, tiled=True)]
    gather x3 -> x0, local copies, waits for them, and re-layouts: 5.98 us -> none  [local_tiles(): return jnp.take(cell_tiles, places, axis=1)]
  transfers between devices with their start and end apart: 9 -> 6, of which waited for: 8 -> 4; matrix products, arithmetic and copies ran while one was open for 2% -> 3% of each run, Pallas kernels for 0% -> 3%
where the time goes in v1:
time: 197 us
  waiting for transfers between devices  67 us (34%)
  blocking collectives  54.8 us (28%)
  starting transfers between devices  26.8 us (14%)
  Pallas kernels  25.9 us (13%)
  between operations  14.2 us (7%)
  local copies, waits for them, and re-layouts  4.71 us (2%)
  other arithmetic  3.39 us (2%)
    all_to_all x1, waiting for transfers between devices, local(): lax.all_to_all(powers.reshape(tm_count, hours, 5 * n), TM, split_axis=0,...  44.2 us
    all_to_all x1, blocking collectives, local(): arrived = lax.all_to_all(xd, TM, split_axis=0, concat_axis=0, tiled=True)  24.3 us
    all_to_all x1, blocking collectives, local(): lax.all_to_all(spread, REGION, split_axis=0, concat_axis=0, tiled=True)  18.3 us
    pallas_call x1, Pallas kernels, local(): pl.pallas_call(spatial_kernel, out_shape=(jax.ShapeDtypeStruct((3, half,...  17.3 us
    ppermute x1, starting transfers between devices, local(): lax.ppermute(flipped, REGION_TM, pairs)  13.7 us
    all_to_all x1, blocking collectives, local(): over_tm = lax.all_to_all(gram, TM, split_axis=0, concat_axis=0, tiled=True)  12.2 us
    all_gather x1, waiting for transfers between devices, local(): lax.all_gather(lax.ppermute(flipped, REGION_TM, pairs), TM, axis=0, tiled...  11.1 us
    ppermute x1, starting transfers between devices, local(): lax.ppermute(jnp.concatenate([pack[:half], extra], axis=1), REGION, [((r...  7.49 us
  transfers between devices with their start and end apart: 6, of which 4 were waited for; matrix products, arithmetic and copies ran while one was open for 3% of the time, Pallas kernels for 3%

profile of v1, /device:TPU:1, one launch (start us, length us, event | category | flops | bytes accessed | tf_op | source)
XLA Modules:
  0.0 196.8 jit_solution(16482684696334633315)
XLA Ops:
  7.2 0.0 all-gather.3.cloned.1.call-start
  7.2 0.7 all-gather.3.cloned.1.call-update
  7.9 0.0 all-gather.5.cloned.1.call-start
  7.9 1.2 copy.20
  9.1 13.7 %collective-permute-start.1 = (bf16[1,1152,128]{2,1,0:T(8,128)(2,1)S(1)}, bf16[1,1152,128]{2,1,0:T(8,128)(2,1)S(1)}, u32[]{:S(2)}, u32[]{:S(2)}) collective-permute-start(bf16[1,1152,128]{2,1,0:T(8,128)(2,1)S(1)} %bitcast.26), channel_id=1, source_target_pairs={{16,0},{17,1},{18,2},{19,3},{20,4},{21,5},{22,6},{23,7},{8,8},{9,9... | collective-permute-start | bytes 884744 | tf_op jit(solution)/shard_map/ppermute | solution.py:183
  22.8 5.7 %collective-permute-done.1 = bf16[1,1152,128]{2,1,0:T(8,128)(2,1)S(1)} collective-permute-done((bf16[1,1152,128]{2,1,0:T(8,128)(2,1)S(1)}, bf16[1,1152,128]{2,1,0:T(8,128)(2,1)S(1)}, u32[]{:S(2)}, u32[]{:S(2)}) %collective-permute-start.1) | collective-permute-done | bytes 294944 | tf_op jit(solution)/shard_map/ppermute | solution.py:183
  28.5 0.7 copy-done.3
  29.2 0.0 all-gather.5.cloned.1.call-update
  29.2 1.5 convert_bitcast_fusion
  30.7 0.5 copy.14
  31.3 0.0 copy-start.4
  31.3 0.5 copy.15
  31.8 1.2 maximum_bitcast_fusion
  33.0 0.4 fusion.5
  33.4 0.2 slice.26
  33.6 0.1 copy.16
  33.7 7.5 %collective-permute-start = (bf16[8,80,256]{2,1,0:T(8,128)(2,1)S(1)}, bf16[8,80,256]{2,1,0:T(8,128)(2,1)S(1)}, u32[]{:S(2)}, u32[]{:S(2)}) collective-permute-start(bf16[8,80,256]{2,1,0:T(8,128)(2,1)S(1)} %fusion.1), channel_id=1, source_target_pairs={{16,0},{32,16},{48,32},{64,48},{80,64},{96,80},{112,96},{128,112},... | collective-permute-start | bytes 983048 | tf_op jit(solution)/shard_map/ppermute | solution.py:173
  41.2 0.2 slice.32
  41.4 5.4 %collective-permute-done = bf16[8,80,256]{2,1,0:T(8,128)(2,1)S(1)} collective-permute-done((bf16[8,80,256]{2,1,0:T(8,128)(2,1)S(1)}, bf16[8,80,256]{2,1,0:T(8,128)(2,1)S(1)}, u32[]{:S(2)}, u32[]{:S(2)}) %collective-permute-start) | collective-permute-done | bytes 327712 | tf_op jit(solution)/shard_map/ppermute | solution.py:173
  46.9 0.0 copy-start.1
  46.9 24.3 %all_to_all.20 = bf16[16,64,256]{2,1,0:T(8,128)(2,1)} all-to-all(bf16[16,64,256]{2,1,0:T(8,128)(2,1)S(1)} %pad_maximum_fusion.xd_ref), channel_id=1, replica_groups=mesh['region_0'=4,'region_1'=8,'tm_0'=8,'tm_1'=2] {'tm_0','tm_1'}, dimensions={0} | all-to-all | bytes 1048576 | tf_op jit(solution)/shard_map/all_to_all | solution.py:185
  71.2 5.5 %temporal.1 = (bf16[1024,640]{1,0:T(8,128)(2,1)}, f32[8,128]{1,0:T(8,128)}) custom-call(bf16[1024,1024]{1,0:T(8,128)(2,1)} %all-gather.3.cloned.1.call-done.c_ref, bf16[1024,256]{1,0:T(8,128)(2,1)} %bitcast.21), custom_call_target="tpu_custom_call" | custom-call | tf_op jit(solution)/shard_map/temporal/pallas_call | solution.py:186
  76.8 3.6 %all-to-all-start.1 = ((bf16[16,64,640]{2,1,0:T(8,128)(2,1)}), bf16[16,64,640]{2,1,0:T(8,128)(2,1)S(1)}, u32[]{:S(2)}, u32[]{:S(2)}) async-start(bf16[16,64,640]{2,1,0:T(8,128)(2,1)} %bitcast.22), calls=%async_computation.1 | async-start | bytes 2621440 | tf_op jit(solution)/shard_map/all_to_all | solution.py:196
  80.4 0.6 pad_add_fusion.slots_ref
  81.0 44.2 %all-to-all-done.1.g_ref = bf16[16,64,640]{2,1,0:T(8,128)(2,1)S(1)} async-done(((bf16[16,64,640]{2,1,0:T(8,128)(2,1)}), bf16[16,64,640]{2,1,0:T(8,128)(2,1)S(1)}, u32[]{:S(2)}, u32[]{:S(2)}) %all-to-all-start.1) | async-done | bytes 1310752 | tf_op jit(solution)/shard_map/all_to_all | solution.py:196
  125.2 11.1 %all-gather.5.cloned.1.call-done.b_ref = bf16[16,1152,128]{2,1,0:T(8,128)(2,1)} async-done(((bf16[1,1152,128]{2,1,0:T(8,128)(2,1)}), bf16[16,1152,128]{2,1,0:T(8,128)(2,1)}) %all-gather.5.cloned.1.call-update) | async-done | bytes 4718608 | tf_op jit(solution)/shard_map/all_gather | solution.py:183
  136.3 17.3 %spatial.1 = (f32[3,8,64,128]{3,2,1,0:T(8,128)}, f32[3,8,64,128]{3,2,1,0:T(8,128)}, f32[16,8,128]{2,1,0:T(8,128)}) custom-call(s32[16,8]{1,0:T(8,128)} %pad_add_fusion.slots_ref, bf16[16,64,640]{2,1,0:T(8,128)(2,1)} %copy-done, bf16[16,64,256]{2,1,0:T(8,128)(2,1)} %copy-done.1, f32[8,128]{1,0:T(8,128)} %get-tuple-element.8.shift_ref, ...), custom_call_target="tpu_custom_call" | custom-call | tf_op jit(solution)/shard_map/spatial/pallas_call | solution.py:198
  153.6 1.9 collective-permute-start.2
  155.5 12.2 %all_to_all.21 = f32[16,8,128]{2,1,0:T(8,128)S(1)} all-to-all(f32[16,8,128]{2,1,0:T(8,128)} %get-tuple-element.9), channel_id=1, replica_groups=mesh['region_0'=4,'region_1'=8,'tm_0'=8,'tm_1'=2] {'tm_0','tm_1'}, dimensions={0} | all-to-all | bytes 131072 | tf_op jit(solution)/shard_map/all_to_all | solution.py:219
  167.8 18.3 %all_to_all.22.gram_ref = f32[32,8,128]{2,1,0:T(8,128)} all-to-all(f32[32,8,128]{2,1,0:T(8,128)S(1)} %broadcast_in_dim.10), channel_id=1, replica_groups=mesh['region_0'=4,'region_1'=8,'tm_0'=8,'tm_1'=2] {'region_0','region_1'}, dimensions={0} | all-to-all | bytes 262144 | tf_op jit(solution)/shard_map/all_to_all | solution.py:221
  186.0 0.9 copy-done.2
  186.9 3.0 %finish.1 = (f32[64,2048]{1,0:T(8,128)}, f32[64,2048]{1,0:T(8,128)}) custom-call(f32[32,8,128]{2,1,0:T(8,128)} %all_to_all.22.gram_ref, f32[64,2048]{1,0:T(8,128)} %x_ref.1, f32[3,8,64,128]{3,2,1,0:T(8,128)} %copy-done.2, f32[3,8,64,128]{3,2,1,0:T(8,128)} %get-tuple-element.11.high_ref), custom_call_target="tpu_custom_call" | custom-call | tf_op jit(solution)/shard_map/finish/pallas_call | solution.py:222
  (19 shorter events, 0.2 us)
Async XLA Ops:
  7.2 64.1 %all-gather.3.cloned.1.call-start = ((), (), s32[]{:S(2)}) async-start(), calls=%async_computation.4 | async-start | bytes 2228224 | tf_op jit(solution)/shard_map/all_gather | solution.py:166
  7.9 128.4 %all-gather.5.cloned.1.call-start = ((), (), s32[]{:S(2)}) async-start(), calls=%async_computation.5 | async-start | bytes 5013504 | tf_op jit(solution)/shard_map/all_gather | solution.py:183
  9.1 19.4 %collective-permute-start.1 = (bf16[1,1152,128]{2,1,0:T(8,128)(2,1)S(1)}, bf16[1,1152,128]{2,1,0:T(8,128)(2,1)S(1)}, u32[]{:S(2)}, u32[]{:S(2)}) collective-permute-start(bf16[1,1152,128]{2,1,0:T(8,128)(2,1)S(1)} %bitcast.26), channel_id=1, source_target_pairs={{16,0},{17,1},{18,2},{19,3},{20,4},{21,5},{22,6},{23,7},{8,8},{9,9... | collective-permute-start | bytes 884744 | tf_op jit(solution)/shard_map/ppermute | solution.py:183
  28.5 0.7 copy-start.3
  31.3 2.3 %copy-start.4 = (s32[16,8]{0,1:T(8,128)S(1)}, s32[16,8]{0,1:T(8,128)}, u32[]{:S(2)}) copy-start(s32[16,8]{0,1:T(8,128)} %param.8) | copy-start | bytes 1540
  33.7 13.1 %collective-permute-start = (bf16[8,80,256]{2,1,0:T(8,128)(2,1)S(1)}, bf16[8,80,256]{2,1,0:T(8,128)(2,1)S(1)}, u32[]{:S(2)}, u32[]{:S(2)}) collective-permute-start(bf16[8,80,256]{2,1,0:T(8,128)(2,1)S(1)} %fusion.1), channel_id=1, source_target_pairs={{16,0},{32,16},{48,32},{64,48},{80,64},{96,80},{112,96},{128,112},... | collective-permute-start | bytes 983048 | tf_op jit(solution)/shard_map/ppermute | solution.py:173
  46.9 29.9 %copy-start.1 = (bf16[16,64,256]{2,1,0:T(8,128)(2,1)}, bf16[16,64,256]{2,1,0:T(8,128)(2,1)S(1)}, u32[]{:S(2)}) copy-start(bf16[16,64,256]{2,1,0:T(8,128)(2,1)S(1)} %pad_maximum_fusion.xd_ref) | copy-start | bytes 1572868
  76.8 48.4 %all-to-all-start.1 = ((bf16[16,64,640]{2,1,0:T(8,128)(2,1)}), bf16[16,64,640]{2,1,0:T(8,128)(2,1)S(1)}, u32[]{:S(2)}, u32[]{:S(2)}) async-start(bf16[16,64,640]{2,1,0:T(8,128)(2,1)} %bitcast.22), calls=%async_computation.1 | async-start | bytes 2621440 | tf_op jit(solution)/shard_map/all_to_all | solution.py:196
  125.2 11.1 %copy-start = (bf16[16,64,640]{2,1,0:T(8,128)(2,1)}, bf16[16,64,640]{2,1,0:T(8,128)(2,1)S(1)}, u32[]{:S(2)}) copy-start(bf16[16,64,640]{2,1,0:T(8,128)(2,1)S(1)} %all-to-all-done.1.g_ref) | copy-start | bytes 3932164
  153.6 32.4 %collective-permute-start.2 = (f32[3,8,64,128]{3,2,1,0:T(8,128)}, f32[3,8,64,128]{3,2,1,0:T(8,128)S(1)}, u32[]{:S(2)}, u32[]{:S(2)}) collective-permute-start(f32[3,8,64,128]{3,2,1,0:T(8,128)} %get-tuple-element.10), channel_id=1, source_target_pairs={{0,16},{16,32},{32,48},{48,64},{64,80},{80,96},{96,112},{112,128},... | collective-permute-start | bytes 2359304 | tf_op jit(solution)/shard_map/ppermute | solution.py:218
  186.0 0.9 copy-start.2
Sparse Core Ops, SparseCore 0:
  10.1 47.6 all-gather.2
  60.5 75.7 all-gather.4

commit v2 on v1

v2 whole, which is shorter than its diff:
```python
import jax
import jax.numpy as jnp
from jax import lax
from jax.experimental import pallas as pl
from jax.experimental.pallas import tpu as pltpu
from jax.sharding import Mesh
from jax.sharding import PartitionSpec as P


REGION = ("region_0", "region_1")
TM = ("tm_0", "tm_1")
REGION_TM = ("region_0", "region_1", "tm_0", "tm_1")
F32 = jnp.float32
BF16 = jnp.bfloat16
UNROLL = 2
VMEM = pl.BlockSpec(memory_space=pltpu.MemorySpace.VMEM)
SMEM = pl.BlockSpec(memory_space=pltpu.MemorySpace.SMEM)


def dot(a, b):
    return jnp.dot(a, b, preferred_element_type=F32)


def pack_kernel(right_ref, initial_ref, blocks_ref, slots_ref, send_ref, keep_ref, own_ref):
    hours = right_ref.shape[0]
    width, n = blocks_ref.shape[0], blocks_ref.shape[1]
    half = keep_ref.shape[0]
    for i in range(2 * half):
        lanes = slice(i * n, (i + 1) * n)
        x = initial_ref[:, lanes]
        pair = jnp.concatenate([x.astype(BF16), (right_ref[:, lanes] - x).astype(BF16)], axis=0)
        if i < half:
            send_ref[2 * hours * i : 2 * hours * (i + 1), :] = pair
        else:
            keep_ref[i - half] = pair
    base = 2 * hours * half
    extra = slots_ref.shape[0]
    send_ref[base : base + extra, :] = slots_ref[...]
    for k in range(width):
        flipped = blocks_ref[k].T
        own_ref[k * n : (k + 1) * n, :] = flipped
        send_ref[base + extra + k * n : base + extra + (k + 1) * n, :] = flipped


def temporal_kernel(core_ref, own_ref, other_ref, v_ref, w_ref, shift_ref):
    groups, part, hours = own_ref.shape
    n = v_ref.shape[2]
    core = core_ref[0]
    row = lax.broadcasted_iota(jnp.int32, (part, n), 0)
    lane = lax.broadcasted_iota(jnp.int32, (part, n), 1)
    diagonal = jnp.zeros((part, n), F32)
    for t in range(groups):
        first_row = 2 * part * t
        lanes = slice(first_row // n * n, first_row // n * n + n)
        for ref, which in ((own_ref, core), (other_ref, 1 - core)):
            at = row + (first_row % n + part * which)
            diagonal = diagonal + jnp.where(lane == at, ref[t, :, lanes].astype(F32), 0.0)
    c0 = jnp.sum(diagonal, axis=(0, 1), keepdims=True) / hours
    shift_ref[...] = jnp.broadcast_to(c0, shift_ref.shape)

    mine = own_ref[...].reshape(groups * part, hours)
    theirs = other_ref[...].reshape(groups * part, hours)

    def power(v, base):
        wide = v.shape[1]
        by_core = jnp.stack([dot(mine, v).reshape(groups, part, wide), dot(theirs, v).reshape(groups, part, wide)], axis=1)
        swapped = jnp.stack([by_core[:, 1], by_core[:, 0]], axis=1)
        full = jnp.where(core == 0, by_core, swapped).reshape(hours, wide)
        out = (full - c0 * v.astype(F32)).astype(BF16)
        w_ref[:, base : base + wide] = out
        return out

    v = v_ref[...]
    pairs = [v[:, k * 2 * part : (k + 1) * 2 * part].reshape(hours, n) for k in range(2)]
    first = power(jnp.concatenate(pairs, axis=1), 0)
    second = power(first, 2 * n)
    power(second[:, :n], 4 * n)


def spatial_kernel(
    slots_ref, g_ref, xd_ref, shift_ref, b_ref, low_ref, high_ref, gram_ref, centre_ref,
    b_buf, f_buf, z_buf, w_buf, r_buf, m_buf, t_buf, s_buf, sums, sem,
):
    rows, hours, n = r_buf.shape
    half = rows // 2
    slots = slots_ref.shape[1]

    def load(i):
        return pltpu.make_async_copy(b_ref.at[i], b_buf.at[i], sem.at[i])

    for i in range(rows):
        load(i).start()
    c0 = shift_ref[0:1, 0:1]
    for i in range(rows):
        x = xd_ref[i, 0:hours].astype(F32)
        y1 = g_ref[i, :, 0:n].astype(F32)
        y2 = g_ref[i, :, 2 * n : 3 * n].astype(F32)
        y3 = g_ref[i, :, 4 * n : 5 * n].astype(F32)
        f_buf[i, 0:hours, :] = (c0 * x + y1).astype(BF16)
        f_buf[i, hours : 2 * hours, :] = (c0 * y1 + y2).astype(BF16)
        f_buf[i, 2 * hours :, :] = (c0 * y2 + y3).astype(BF16)

    def product(source, i):
        tiles = [source[i]] + [source[slots_ref[i, k]] for k in range(slots)]
        return dot(jnp.concatenate(tiles, axis=1), b_buf[i])

    diagonal = lax.broadcasted_iota(jnp.int32, (n, n), 0) == lax.broadcasted_iota(jnp.int32, (n, n), 1)

    def stage_one(i, _):
        load(i).wait()
        block = b_buf[i, 0:n].astype(F32)
        s_buf[i] = jnp.broadcast_to(jnp.sum(jnp.where(diagonal, block, 0.0), axis=(0, 1), keepdims=True) / n, (8, n))
        out = product(f_buf, i)
        d = xd_ref[i, hours : 2 * hours].astype(F32)
        e1 = g_ref[i, :, n : 2 * n].astype(F32)
        e2 = g_ref[i, :, 3 * n : 4 * n].astype(F32)
        r0 = d - out[0:hours]
        u1 = e1 - out[hours : 2 * hours]
        u2 = e2 - out[2 * hours :]
        r_buf[i] = r0
        z1 = c0 * r0 + u1
        rest = c0 * u1 + u2
        z_buf[i, 0:hours, :] = z1.astype(BF16)
        z_buf[i, hours:, :] = rest.astype(BF16)
        m_buf[i] = z1
        t_buf[i] = rest
        return 0

    def stage_two(i, _):
        out = product(z_buf, i)
        s = s_buf[i, 0:1, :]
        first = out[0:hours] - s * z_buf[i, 0:hours].astype(F32)
        second = out[hours:] - s * z_buf[i, hours:].astype(F32)
        z1 = m_buf[i]
        w2 = s * (c0 * z1 + t_buf[i]) + c0 * first + second
        m_buf[i] = s * z1 + first
        t_buf[i] = w2
        w_buf[i] = w2.astype(BF16)
        return 0

    def add(k, value):
        sums[k] += jnp.sum(value.reshape(hours // 8, 8, n), axis=0)

    def stage_three(mu, low, i):
        s = s_buf[i, 0:1, :]
        m2 = product(w_buf, i) - s * w_buf[i].astype(F32) + s * t_buf[i]
        r0, m1 = r_buf[i], m_buf[i]
        add(0, r0 * r0)
        add(1, r0 * m1)
        add(2, m1 * m1)
        add(3, r0 * m2)
        add(4, m1 * m2)
        centred = (r0, m1 - mu * r0, m2 - mu * (2.0 * m1 - mu * r0))
        for k, value in enumerate(centred):
            if low:
                start = pl.multiple_of((k * half + i) * hours, hours)
                low_ref[pl.ds(start, hours), :] = value.astype(BF16)
            else:
                high_ref[k, i - half] = value

    sums[...] = jnp.zeros_like(sums)
    lax.fori_loop(0, rows, stage_one, 0, unroll=UNROLL)
    lax.fori_loop(0, rows, stage_two, 0, unroll=UNROLL)
    mean = jnp.sum(s_buf[:, 0:1, :], axis=0) / rows
    rounded = (c0 * mean).astype(BF16)
    mu = rounded.astype(F32)
    centre_ref[...] = jnp.broadcast_to(mu, centre_ref.shape)
    low_ref[3 * half * hours :, :] = jnp.broadcast_to(mu, (16, n)).astype(BF16)
    lax.fori_loop(0, half, lambda i, _: (stage_three(mu, True, i), 0)[1], 0, unroll=UNROLL)
    lax.fori_loop(half, rows, lambda i, _: (stage_three(mu, False, i), 0)[1], 0, unroll=UNROLL)
    gram = jnp.sum(sums[...], axis=1)
    for k in range(gram_ref.shape[0]):
        gram_ref[k] = gram


def finish_kernel(gram_ref, x_ref, low_ref, high_ref, centre_ref, solution_ref, residual_ref):
    total = jnp.sum(jnp.sum(gram_ref[...], axis=0), axis=1, keepdims=True)
    rr, rm1, m11, rm2, m12 = (total[k : k + 1, 0:1] for k in range(5))
    rq = rr + rm1
    qq = rr + 2.0 * rm1 + m11
    rs = rr + 2.0 * rm1 + rm2
    qs = rr + 3.0 * rm1 + rm2 + 2.0 * m11 + m12
    alpha = rr / rq
    norm = rr - 2.0 * alpha * rq + alpha * alpha * qq
    keep = 1.0 + norm / rr
    curvature = keep * keep * rq - alpha * keep * (rs + qq) + alpha * alpha * qs
    step = norm / curvature
    x_0 = alpha + step * (keep - alpha)
    x_1 = -step * alpha
    g_0 = 1.0 - x_0
    g_1 = -alpha - step * (keep - 2.0 * alpha)
    g_2 = step * alpha
    _, half, hours, n = high_ref.shape

    def write(mu, first, load):
        a_0, a_1 = x_0 + mu * x_1, x_1
        b_0, b_1, b_2 = g_0 + mu * (g_1 + mu * g_2), g_1 + 2.0 * mu * g_2, g_2
        for i in range(half):
            lanes = slice((first + i) * n, (first + i + 1) * n)
            r0, e1, e2 = load(0, i), load(1, i), load(2, i)
            solution_ref[:, lanes] = x_ref[:, lanes] + (a_0 * r0 + a_1 * e1)
            residual_ref[:, lanes] = b_0 * r0 + b_1 * e1 + b_2 * e2

    write(centre_ref[0:1, 0:1], half, lambda k, i: high_ref[k, i])
    base = 3 * half * hours
    write(
        low_ref[base : base + 16, :].astype(F32)[0:1, 0:1],
        0,
        lambda k, i: low_ref[(k * half + i) * hours : (k * half + i + 1) * hours, :].astype(F32),
    )


def steps(right_side, initial, blocks, neighbour_blocks, temporal_cov):
    hours, sites = right_side.shape
    n = blocks.shape[2]
    width = blocks.shape[1]
    rows = neighbour_blocks.shape[0]
    half = rows // 2
    slots = neighbour_blocks.shape[1]
    tm_count = lax.axis_size(TM)
    regions = lax.axis_size(REGION)
    all_hours = temporal_cov.shape[1]
    part = hours // 2

    local_slots = lax.rem(neighbour_blocks, rows)
    extra = jnp.pad(local_slots[:half].astype(BF16), ((0, 16 - half), (0, n - slots)))
    base = 2 * hours * half
    halves = jnp.broadcast_to(temporal_cov.reshape(1, 2, part, all_hours), (tm_count // 2, 2, part, all_hours))
    mine = lax.all_to_all(
        halves.reshape(tm_count, part, all_hours), TM, split_axis=0, concat_axis=0, tiled=True
    )
    packed, keep, own_blocks = pl.pallas_call(
        pack_kernel,
        out_shape=(
            jax.ShapeDtypeStruct((base + 16 + width * n, n), BF16),
            jax.ShapeDtypeStruct((half, 2 * hours, n), BF16),
            jax.ShapeDtypeStruct((width * n, n), BF16),
        ),
        in_specs=[VMEM] * 4,
        out_specs=(VMEM,) * 3,
        name="pack",
    )(right_side, initial, blocks[0], extra)
    shifted = lax.ppermute(packed, REGION, [((r + 1) % regions, r) for r in range(regions)])
    window_row = jnp.where(lax.axis_index(TM) < half, shifted[base + 16 :], own_blocks)
    window_blocks = lax.all_gather(window_row[None], TM, axis=0, tiled=True)
    xd = jnp.concatenate([shifted[:base].reshape(half, 2 * hours, n), keep], axis=0)
    window_slots = jnp.concatenate(
        [shifted[base : base + half, :slots].astype(jnp.int32), local_slots[half:]], axis=0
    )

    theirs = lax.ppermute(mine, TM[1], [(0, 1), (1, 0)])
    core = lax.axis_index(TM[1]).astype(jnp.int32).reshape(1)
    arrived = lax.all_to_all(xd, TM, split_axis=0, concat_axis=0, tiled=True)
    powers, shift = pl.pallas_call(
        temporal_kernel,
        out_shape=(
            jax.ShapeDtypeStruct((all_hours, 5 * n), BF16),
            jax.ShapeDtypeStruct((8, n), F32),
        ),
        in_specs=[SMEM, VMEM, VMEM, VMEM],
        out_specs=(VMEM, VMEM),
        name="temporal",
    )(core, mine, theirs, arrived)
    returned = lax.all_to_all(powers.reshape(tm_count, hours, 5 * n), TM, split_axis=0, concat_axis=0, tiled=True)

    low, high, gram, centre = pl.pallas_call(
        spatial_kernel,
        out_shape=(
            jax.ShapeDtypeStruct((3 * half * hours + 16, n), BF16),
            jax.ShapeDtypeStruct((3, half, hours, n), F32),
            jax.ShapeDtypeStruct((tm_count, 8, n), F32),
            jax.ShapeDtypeStruct((8, n), F32),
        ),
        in_specs=[SMEM, VMEM, VMEM, VMEM, pl.BlockSpec(memory_space=pl.ANY)],
        out_specs=(VMEM,) * 4,
        scratch_shapes=[
            pltpu.VMEM((rows, width * n, n), BF16),
            pltpu.VMEM((rows, 3 * hours, n), BF16),
            pltpu.VMEM((rows, 2 * hours, n), BF16),
            pltpu.VMEM((rows, hours, n), BF16),
            pltpu.VMEM((rows, hours, n), F32),
            pltpu.VMEM((rows, hours, n), F32),
            pltpu.VMEM((rows, hours, n), F32),
            pltpu.VMEM((rows, 8, n), F32),
            pltpu.VMEM((8, 8, n), F32),
            pltpu.SemaphoreType.DMA((rows,)),
        ],
        name="spatial",
    )(window_slots, returned, xd, shift, window_blocks)

    back = lax.ppermute(low, REGION, [(r, (r + 1) % regions) for r in range(regions)])
    over_tm = lax.all_to_all(gram, TM, split_axis=0, concat_axis=0, tiled=True)
    spread = jnp.broadcast_to(jnp.sum(over_tm, axis=0)[None], (regions, 8, n))
    over_region = lax.all_to_all(spread, REGION, split_axis=0, concat_axis=0, tiled=True)
    return pl.pallas_call(
        finish_kernel,
        out_shape=(
            jax.ShapeDtypeStruct((hours, sites), F32),
            jax.ShapeDtypeStruct((hours, sites), F32),
        ),
        in_specs=[VMEM] * 5,
        out_specs=(VMEM, VMEM),
        name="finish",
    )(over_region, initial, back, high, centre)


def solution(mesh):
    split = Mesh(mesh.devices.reshape(4, 8, 8, 2), ("region_0", "region_1", "tm_0", "tm_1"))
    return jax.shard_map(
        steps,
        mesh=split,
        in_specs=(
            P(TM, REGION),
            P(TM, REGION),
            P(REGION_TM, None, None, None),
            P(REGION, None),
            P(TM, None),
        ),
        out_specs=(P(TM, REGION), P(TM, REGION)),
        check_vma=False,
    )
```

time: 197 us -> 209 us (1.061)
  waiting for transfers between devices: 67 us -> 81.2 us
  starting transfers between devices: 26.8 us -> 31.9 us
  blocking collectives: 54.8 us -> 50.9 us
  Pallas kernels: 25.9 us -> 22.6 us
    all_to_all x1 -> x2, waiting for transfers between devices: 44.2 us -> 69.5 us  [the longest x1 36.8 us: steps(): lax.all_to_all(halves.reshape(tm_count, part, all_hours), TM, split_axis=...]
    all_gather x2 -> x1, waiting for transfers between devices: 11.1 us -> 0.01 us  [steps(): window_blocks = lax.all_gather(window_row[None], TM, axis=0, tiled=True)]
    all_to_all x1 -> x2, starting transfers between devices: 3.61 us -> 14.4 us  [the longest x1 9.6 us: steps(): lax.all_to_all(halves.reshape(tm_count, part, all_hours), TM, split_axis=...]
    ppermute x3, starting transfers between devices: 23.1 us -> 17.5 us  [the longest x1 13.7 us: steps(): lax.ppermute(packed, REGION, [((r + 1) % regions, r) for r in range(regio...]
    all_to_all x3, blocking collectives: 54.8 us -> 50.9 us  [the longest x1 21.6 us: steps(): arrived = lax.all_to_all(xd, TM, split_axis=0, concat_axis=0, tiled=True)]
    pallas_call x3 -> x4, Pallas kernels: 25.9 us -> 22.6 us  [the longest x1 12.6 us: steps(): pl.pallas_call(spatial_kernel, out_shape=(jax.ShapeDtypeStruct((3 * half...]
  transfers between devices with their start and end apart: 6 -> 6, of which waited for: 4 -> 3; matrix products, arithmetic and copies ran while one was open for 3% -> 1% of each run, Pallas kernels for 3% -> 2%
where the time goes in v2:
time: 209 us; the launch traced here: 208 us
  waiting for transfers between devices  81.2 us (39%)
  blocking collectives  50.9 us (24%)
  starting transfers between devices  31.9 us (15%)
  Pallas kernels  22.6 us (11%)
  between operations  14.1 us (7%)
  local copies, waits for them, and re-layouts  5.38 us (3%)
  other arithmetic  2.42 us (1%)
    all_to_all x1, waiting for transfers between devices, steps(): lax.all_to_all(halves.reshape(tm_count, part, all_hours), TM, split_axis=...  36.8 us
    all_to_all x1, waiting for transfers between devices, steps(): lax.all_to_all(powers.reshape(tm_count, hours, 5 * n), TM, split_axis=0,...  32.7 us
    all_to_all x1, blocking collectives, steps(): arrived = lax.all_to_all(xd, TM, split_axis=0, concat_axis=0, tiled=True)  21.6 us
    all_to_all x1, blocking collectives, steps(): lax.all_to_all(spread, REGION, split_axis=0, concat_axis=0, tiled=True)  17.7 us
    ppermute x1, starting transfers between devices, steps(): lax.ppermute(packed, REGION, [((r + 1) % regions, r) for r in range(regio...  13.7 us
    pallas_call x1, Pallas kernels, steps(): pl.pallas_call(spatial_kernel, out_shape=(jax.ShapeDtypeStruct((3 * half...  12.6 us
    ppermute x1, waiting for transfers between devices, steps(): lax.ppermute(packed, REGION, [((r + 1) % regions, r) for r in range(regio...  11.7 us
    all_to_all x1, blocking collectives, steps(): over_tm = lax.all_to_all(gram, TM, split_axis=0, concat_axis=0, tiled=True)  11.6 us
  transfers between devices with their start and end apart: 6, of which 3 were waited for; matrix products, arithmetic and copies ran while one was open for 1% of the time, Pallas kernels for 2%

profile of v2, /device:TPU:1, one launch (start us, length us, event | category | flops | bytes accessed | tf_op | source)
XLA Modules:
  0.0 208.4 jit_solution(3590119373901789347)
XLA Ops:
  7.2 0.0 copy-start.5
  7.2 0.0 all-gather.3.cloned.1.call-start
  7.2 0.8 copy.7
  8.0 0.6 pad.4.slots_ref
  8.6 2.4 %pack.1 = (bf16[2192,128]{1,0:T(8,128)(2,1)}, bf16[8,128,128]{2,1,0:T(8,128)(2,1)}, bf16[1152,128]{1,0:T(8,128)(2,1)}) custom-call(f32[64,2048]{1,0:T(8,128)} %right_ref.1, f32[64,2048]{1,0:T(8,128)} %x_ref.1, bf16[9,128,128]{2,1,0:T(8,128)(2,1)} %bitcast.10, bf16[16,128]{1,0:T(8,128)(2,1)} %pad.4.slots_ref), custom_call_target="tpu_custom_call" | custom-call | tf_op jit(solution)/shard_map/pack/pallas_call | solution.py:232
  11.0 13.7 %collective-permute-start = (bf16[2192,128]{1,0:T(8,128)(2,1)}, bf16[2192,128]{1,0:T(8,128)(2,1)S(1)}, u32[]{:S(2)}, u32[]{:S(2)}) collective-permute-start(bf16[2192,128]{1,0:T(8,128)(2,1)} %get-tuple-element.11), channel_id=1, source_target_pairs={{16,0},{32,16},{48,32},{64,48},{80,64},{96,80},{112,96},{128,112},... | collective-permute-start | bytes 1683464 | tf_op jit(solution)/shard_map/ppermute | solution.py:243
  24.7 11.7 %collective-permute-done = bf16[2192,128]{1,0:T(8,128)(2,1)S(1)} collective-permute-done((bf16[2192,128]{1,0:T(8,128)(2,1)}, bf16[2192,128]{1,0:T(8,128)(2,1)S(1)}, u32[]{:S(2)}, u32[]{:S(2)}) %collective-permute-start) | collective-permute-done | bytes 561184 | tf_op jit(solution)/shard_map/ppermute | solution.py:243
  36.4 0.7 slice_select_fusion
  37.1 0.0 all-gather.3.cloned.1.call-update
  37.1 0.0 copy-done.5
  37.2 1.1 broadcast_in_dim.17
  38.3 9.6 %all-to-all-start = ((bf16[16,32,1024]{2,1,0:T(8,128)(2,1)}), bf16[16,32,1024]{2,1,0:T(8,128)(2,1)S(1)}, u32[]{:S(2)}, u32[]{:S(2)}) async-start(bf16[16,32,1024]{2,1,0:T(8,128)(2,1)} %bitcast.3), calls=%async_computation | async-start | bytes 2097152 | tf_op jit(solution)/shard_map/all_to_all | solution.py:229
  47.9 36.8 %all-to-all-done.own_ref = bf16[16,32,1024]{2,1,0:T(8,128)(2,1)S(1)} async-done(((bf16[16,32,1024]{2,1,0:T(8,128)(2,1)}), bf16[16,32,1024]{2,1,0:T(8,128)(2,1)S(1)}, u32[]{:S(2)}, u32[]{:S(2)}) %all-to-all-start) | async-done | bytes 1048608 | tf_op jit(solution)/shard_map/all_to_all | solution.py:229
  84.7 1.9 collective-permute-start.1
  86.6 1.0 pad_maximum_fusion.xd_ref
  87.7 0.0 copy-start.1
  87.7 21.6 %all_to_all.25.v_ref = bf16[16,128,128]{2,1,0:T(8,128)(2,1)} all-to-all(bf16[16,128,128]{2,1,0:T(8,128)(2,1)S(1)} %pad_maximum_fusion.xd_ref), channel_id=1, replica_groups=mesh['region_0'=4,'region_1'=8,'tm_0'=8,'tm_1'=2] {'tm_0','tm_1'}, dimensions={0} | all-to-all | bytes 1048576 | tf_op jit(solution)/shard_map/all_to_all | solution.py:253
  109.3 0.0 collective-permute-done.1.other_ref
  109.3 0.0 copy-done.2
  109.3 1.0 copy-done.3
  110.3 4.7 %temporal.1 = (bf16[1024,640]{1,0:T(8,128)(2,1)}, f32[8,128]{1,0:T(8,128)}) custom-call(s32[1]{0:T(128)} %bitcast.1.core_ref, bf16[16,32,1024]{2,1,0:T(8,128)(2,1)} %copy-done.2, bf16[16,32,1024]{2,1,0:T(8,128)(2,1)} %copy-done.3, bf16[16,128,128]{2,1,0:T(8,128)(2,1)} %all_to_all.25.v_ref), custom_call_target="tpu_custom_call" | custom-call | tf_op jit(solution)/shard_map/temporal/pallas_call | solution.py:254
  115.0 4.8 %all-to-all-start.2 = ((bf16[16,64,640]{2,1,0:T(8,128)(2,1)}), bf16[16,64,640]{2,1,0:T(8,128)(2,1)S(1)}, u32[]{:S(2)}, u32[]{:S(2)}) async-start(bf16[16,64,640]{2,1,0:T(8,128)(2,1)} %bitcast.8), calls=%async_computation.2 | async-start | bytes 2621440 | tf_op jit(solution)/shard_map/all_to_all | solution.py:264
  119.8 0.6 pad_add_fusion.slots_ref
  120.4 32.7 %all-to-all-done.2.g_ref = bf16[16,64,640]{2,1,0:T(8,128)(2,1)S(1)} async-done(((bf16[16,64,640]{2,1,0:T(8,128)(2,1)}), bf16[16,64,640]{2,1,0:T(8,128)(2,1)S(1)}, u32[]{:S(2)}, u32[]{:S(2)}) %all-to-all-start.2) | async-done | bytes 1310752 | tf_op jit(solution)/shard_map/all_to_all | solution.py:264
  153.1 1.1 copy-done
  154.2 12.6 %spatial.1 = (bf16[1552,128]{1,0:T(8,128)(2,1)}, f32[3,8,64,128]{3,2,1,0:T(8,128)}, f32[16,8,128]{2,1,0:T(8,128)}, f32[8,128]{1,0:T(8,128)}) custom-call(s32[16,8]{1,0:T(8,128)} %pad_add_fusion.slots_ref, bf16[16,64,640]{2,1,0:T(8,128)(2,1)} %copy-done, bf16[16,128,128]{2,1,0:T(8,128)(2,1)} %copy-done.1, f32[8,128]{1,0:T(8,128)} %get-tuple-element.14.shift_ref, ...), custom_call_target="tpu_custom_call" | custom-call | tf_op jit(solution)/shard_map/spatial/pallas_call | solution.py:266
  166.8 1.9 collective-permute-start.2
  168.8 11.6 %all_to_all.26 = f32[16,8,128]{2,1,0:T(8,128)S(1)} all-to-all(f32[16,8,128]{2,1,0:T(8,128)} %get-tuple-element.16), channel_id=1, replica_groups=mesh['region_0'=4,'region_1'=8,'tm_0'=8,'tm_1'=2] {'tm_0','tm_1'}, dimensions={0} | all-to-all | bytes 131072 | tf_op jit(solution)/shard_map/all_to_all | solution.py:292
  180.3 17.7 %all_to_all.27.gram_ref = f32[32,8,128]{2,1,0:T(8,128)} all-to-all(f32[32,8,128]{2,1,0:T(8,128)S(1)} %broadcast_in_dim.19), channel_id=1, replica_groups=mesh['region_0'=4,'region_1'=8,'tm_0'=8,'tm_1'=2] {'region_0','region_1'}, dimensions={0} | all-to-all | bytes 262144 | tf_op jit(solution)/shard_map/all_to_all | solution.py:294
  198.0 0.0 collective-permute-done.2.low_ref
  198.0 0.8 copy-done.4
  198.8 2.8 %finish.1 = (f32[64,2048]{1,0:T(8,128)}, f32[64,2048]{1,0:T(8,128)}) custom-call(f32[32,8,128]{2,1,0:T(8,128)} %all_to_all.27.gram_ref, f32[64,2048]{1,0:T(8,128)} %x_ref.1, bf16[1552,128]{1,0:T(8,128)(2,1)} %copy-done.4, f32[3,8,64,128]{3,2,1,0:T(8,128)} %get-tuple-element.18.high_ref, f32[8,128]{1,0:T(8,128)} %get-tuple-element.19.centre_ref), custom_call_target="tpu_custom_call" | custom-call | tf_op jit(solution)/shard_map/finish/pallas_call | solution.py:295
  (12 shorter events, 0.1 us)
Async XLA Ops:
  7.2 30.0 %copy-start.5 = (bf16[64,1024]{1,0:T(8,128)(2,1)S(1)}, bf16[64,1024]{1,0:T(8,128)(2,1)}, u32[]{:S(2)}) copy-start(bf16[64,1024]{1,0:T(8,128)(2,1)} %param.9) | copy-start | bytes 393220
  7.2 145.9 %all-gather.3.cloned.1.call-start = ((), (), s32[]{:S(2)}) async-start(), calls=%async_computation.5 | async-start | bytes 5013504 | tf_op jit(solution)/shard_map/all_gather | solution.py:245
  11.0 25.4 %collective-permute-start = (bf16[2192,128]{1,0:T(8,128)(2,1)}, bf16[2192,128]{1,0:T(8,128)(2,1)S(1)}, u32[]{:S(2)}, u32[]{:S(2)}) collective-permute-start(bf16[2192,128]{1,0:T(8,128)(2,1)} %get-tuple-element.11), channel_id=1, source_target_pairs={{16,0},{32,16},{48,32},{64,48},{80,64},{96,80},{112,96},{128,112},... | collective-permute-start | bytes 1683464 | tf_op jit(solution)/shard_map/ppermute | solution.py:243
  38.3 46.4 %all-to-all-start = ((bf16[16,32,1024]{2,1,0:T(8,128)(2,1)}), bf16[16,32,1024]{2,1,0:T(8,128)(2,1)S(1)}, u32[]{:S(2)}, u32[]{:S(2)}) async-start(bf16[16,32,1024]{2,1,0:T(8,128)(2,1)} %bitcast.3), calls=%async_computation | async-start | bytes 2097152 | tf_op jit(solution)/shard_map/all_to_all | solution.py:229
  84.7 24.6 %copy-start.2 = (bf16[16,32,1024]{2,1,0:T(8,128)(2,1)}, bf16[16,32,1024]{2,1,0:T(8,128)(2,1)S(1)}, u32[]{:S(2)}) copy-start(bf16[16,32,1024]{2,1,0:T(8,128)(2,1)S(1)} %all-to-all-done.own_ref) | copy-start | bytes 3145732
  84.7 24.6 %collective-permute-start.1 = (bf16[16,32,1024]{2,1,0:T(8,128)(2,1)S(1)}, bf16[16,32,1024]{2,1,0:T(8,128)(2,1)S(1)}, u32[]{:S(2)}, u32[]{:S(2)}) collective-permute-start(bf16[16,32,1024]{2,1,0:T(8,128)(2,1)S(1)} %all-to-all-done.own_ref), channel_id=1, source_target_pairs={{0,1},{1,0},{2,3},{3,2},{4,5},{5,4},{6,7},{7,6},{8,9},{9,8},{10,11... | collective-permute-start | bytes 3145736 | tf_op jit(solution)/shard_map/ppermute | solution.py:251
  87.7 27.4 %copy-start.1 = (bf16[16,128,128]{2,1,0:T(8,128)(2,1)}, bf16[16,128,128]{2,1,0:T(8,128)(2,1)S(1)}, u32[]{:S(2)}) copy-start(bf16[16,128,128]{2,1,0:T(8,128)(2,1)S(1)} %pad_maximum_fusion.xd_ref) | copy-start | bytes 1572868
  109.3 1.0 copy-start.3
  115.0 38.1 %all-to-all-start.2 = ((bf16[16,64,640]{2,1,0:T(8,128)(2,1)}), bf16[16,64,640]{2,1,0:T(8,128)(2,1)S(1)}, u32[]{:S(2)}, u32[]{:S(2)}) async-start(bf16[16,64,640]{2,1,0:T(8,128)(2,1)} %bitcast.8), calls=%async_computation.2 | async-start | bytes 2621440 | tf_op jit(solution)/shard_map/all_to_all | solution.py:264
  153.1 1.1 copy-start
  166.8 31.2 %collective-permute-start.2 = (bf16[1552,128]{1,0:T(8,128)(2,1)}, bf16[1552,128]{1,0:T(8,128)(2,1)S(1)}, u32[]{:S(2)}, u32[]{:S(2)}) collective-permute-start(bf16[1552,128]{1,0:T(8,128)(2,1)} %get-tuple-element.17), channel_id=1, source_target_pairs={{0,16},{16,32},{32,48},{48,64},{64,80},{80,96},{96,112},{112,128},... | collective-permute-start | bytes 1191944 | tf_op jit(solution)/shard_map/ppermute | solution.py:291
  198.0 0.8 copy-start.4
Sparse Core Ops, SparseCore 0:
  37.3 70.1 all-gather.2

commit v3 on v2

--- a/solution.py
+++ b/solution.py
@@ -33,13 +33,9 @@
             send_ref[2 * hours * i : 2 * hours * (i + 1), :] = pair
         else:
             keep_ref[i - half] = pair
-    base = 2 * hours * half
-    extra = slots_ref.shape[0]
-    send_ref[base : base + extra, :] = slots_ref[...]
+    send_ref[2 * hours * half :, :] = slots_ref[...]
     for k in range(width):
-        flipped = blocks_ref[k].T
-        own_ref[k * n : (k + 1) * n, :] = flipped
-        send_ref[base + extra + k * n : base + extra + (k + 1) * n, :] = flipped
+        own_ref[k * n : (k + 1) * n, :] = blocks_ref[k].T
 
 
 def temporal_kernel(core_ref, own_ref, other_ref, v_ref, w_ref, shift_ref):
@@ -77,19 +73,30 @@
     power(second[:, :n], 4 * n)
 
 
-def spatial_kernel(
-    slots_ref, g_ref, xd_ref, shift_ref, b_ref, low_ref, high_ref, gram_ref, centre_ref,
-    b_buf, f_buf, z_buf, w_buf, r_buf, m_buf, t_buf, s_buf, sums, sem,
-):
+def spatial_kernel(tm_ref, slots_ref, g_ref, xd_ref, shift_ref, *refs):
+    parts, refs = refs[:10], refs[10:]
+    low_ref, high_ref, gram_ref, centre_ref, b_buf, f_buf, z_buf, w_buf, r_buf, m_buf, t_buf, s_buf, sums, sem = refs
     rows, hours, n = r_buf.shape
     half = rows // 2
     slots = slots_ref.shape[1]
-
-    def load(i):
-        return pltpu.make_async_copy(b_ref.at[i], b_buf.at[i], sem.at[i])
-
-    for i in range(rows):
-        load(i).start()
+    deep = b_buf.shape[1]
+
+    sources = [ref.at[...] for ref in parts[:8]]
+    for ref in parts[8:]:
+        sources += [ref.at[k * deep : (k + 1) * deep] for k in range(ref.shape[0] // deep)]
+    for k in range(rows):
+        pltpu.make_async_copy(sources[k], b_buf.at[k], sem.at[k]).start()
+    position = tm_ref[0]
+
+    def place(i):
+        away = lax.rem(position // 2 - i // 2 + half, half)
+        order = jnp.where(
+            away == half // 2,
+            half - 1,
+            jnp.where(away < half // 2, jnp.maximum(2 * away - 1, 0), 2 * (half - away)),
+        )
+        return order + half * (lax.rem(i, 2) != lax.rem(position, 2)).astype(jnp.int32)
+
     c0 = shift_ref[0:1, 0:1]
     for i in range(rows):
         x = xd_ref[i, 0:hours].astype(F32)
@@ -102,13 +109,14 @@
 
     def product(source, i):
         tiles = [source[i]] + [source[slots_ref[i, k]] for k in range(slots)]
-        return dot(jnp.concatenate(tiles, axis=1), b_buf[i])
+        return dot(jnp.concatenate(tiles, axis=1), b_buf[place(i)])
 
     diagonal = lax.broadcasted_iota(jnp.int32, (n, n), 0) == lax.broadcasted_iota(jnp.int32, (n, n), 1)
 
     def stage_one(i, _):
-        load(i).wait()
-        block = b_buf[i, 0:n].astype(F32)
+        at = place(i)
+        pltpu.make_async_copy(sources[0], b_buf.at[at], sem.at[at]).wait()
+        block = b_buf[at, 0:n].astype(F32)
         s_buf[i] = jnp.broadcast_to(jnp.sum(jnp.where(diagonal, block, 0.0), axis=(0, 1), keepdims=True) / n, (8, n))
         out = product(f_buf, i)
         d = xd_ref[i, hours : 2 * hours].astype(F32)
@@ -210,6 +218,21 @@
     )
 
 
+def ring(row):
+    count = lax.axis_size(TM[0])
+    up = [(i, (i + 1) % count) for i in range(count)]
+    down = [(j, i) for i, j in up]
+    found = [row]
+    forward = backward = row
+    for k in range(1, count // 2 + 1):
+        forward = lax.ppermute(forward, TM[0], up)
+        found.append(forward)
+        if k < count // 2:
+            backward = lax.ppermute(backward, TM[0], down)
+            found.append(backward)
+    return found[:5], found[5:]
+
+
 def steps(right_side, initial, blocks, neighbour_blocks, temporal_cov):
     hours, sites = right_side.shape
     n = blocks.shape[2]
@@ -232,7 +255,7 @@
     packed, keep, own_blocks = pl.pallas_call(
         pack_kernel,
         out_shape=(
-            jax.ShapeDtypeStruct((base + 16 + width * n, n), BF16),
+            jax.ShapeDtypeStruct((base + 16, n), BF16),
             jax.ShapeDtypeStruct((half, 2 * hours, n), BF16),
             jax.ShapeDtypeStruct((width * n, n), BF16),
         ),
@@ -241,15 +264,19 @@
         name="pack",
     )(right_side, initial, blocks[0], extra)
     shifted = lax.ppermute(packed, REGION, [((r + 1) % regions, r) for r in range(regions)])
-    window_row = jnp.where(lax.axis_index(TM) < half, shifted[base + 16 :], own_blocks)
-    window_blocks = lax.all_gather(window_row[None], TM, axis=0, tiled=True)
+    pairs = [
+        (((r + (t < half)) % regions) * tm_count + t, r * tm_count + t) for r in range(regions) for t in range(tm_count)
+    ]
+    row = lax.ppermute(own_blocks, REGION_TM, pairs)
+    near, far = ring(row)
+    other_near = lax.ppermute(jnp.concatenate(near, axis=0), TM[1], [(0, 1), (1, 0)])
+    other_far = lax.ppermute(jnp.concatenate(far, axis=0), TM[1], [(0, 1), (1, 0)])
     xd = jnp.concatenate([shifted[:base].reshape(half, 2 * hours, n), keep], axis=0)
-    window_slots = jnp.concatenate(
-        [shifted[base : base + half, :slots].astype(jnp.int32), local_slots[half:]], axis=0
-    )
+    window_slots = jnp.concatenate([shifted[base : base + half, :slots].astype(jnp.int32), local_slots[half:]], axis=0)
 
     theirs = lax.ppermute(mine, TM[1], [(0, 1), (1, 0)])
     core = lax.axis_index(TM[1]).astype(jnp.int32).reshape(1)
+    position = lax.axis_index(TM).astype(jnp.int32).reshape(1)
     arrived = lax.all_to_all(xd, TM, split_axis=0, concat_axis=0, tiled=True)
     powers, shift = pl.pallas_call(
         temporal_kernel,
@@ -261,7 +288,9 @@
         out_specs=(VMEM, VMEM),
         name="temporal",
     )(core, mine, theirs, arrived)
-    returned = lax.all_to_all(powers.reshape(tm_count, hours, 5 * n), TM, split_axis=0, concat_axis=0, tiled=True)
+    returned = lax.all_to_all(
+        powers.reshape(tm_count, hours, 5 * n), TM, split_axis=0, concat_axis=0, tiled=True
+    )
 
     low, high, gram, centre = pl.pallas_call(
         spatial_kernel,
@@ -271,7 +300,7 @@
             jax.ShapeDtypeStruct((tm_count, 8, n), F32),
             jax.ShapeDtypeStruct((8, n), F32),
         ),
-        in_specs=[SMEM, VMEM, VMEM, VMEM, pl.BlockSpec(memory_space=pl.ANY)],
+        in_specs=[SMEM, SMEM, VMEM, VMEM, VMEM] + [pl.BlockSpec(memory_space=pl.ANY)] * 10,
         out_specs=(VMEM,) * 4,
         scratch_shapes=[
             pltpu.VMEM((rows, width * n, n), BF16),
@@ -286,7 +315,7 @@
             pltpu.SemaphoreType.DMA((rows,)),
         ],
         name="spatial",
-    )(window_slots, returned, xd, shift, window_blocks)
+    )(position, window_slots, returned, xd, shift, *near, *far, other_near, other_far)
 
     back = lax.ppermute(low, REGION, [(r, (r + 1) % regions) for r in range(regions)])
     over_tm = lax.all_to_all(gram, TM, split_axis=0, concat_axis=0, tiled=True)

time: 209 us -> 205 us (0.981)
  starting transfers between devices: 31.9 us -> 74.3 us
  waiting for transfers between devices: 81.2 us -> 57 us
  blocking collectives: 50.9 us -> 33.1 us
  between operations: 14.1 us -> 0.89 us
  local copies, waits for them, and re-layouts: 5.38 us -> 10.7 us
    ppermute x0 -> x10, waiting for transfers between devices: none -> 44.2 us  [the longest x3 28.1 us: ring(): backward = lax.ppermute(backward, TM[0], down)]
    ppermute x0 -> x10, starting transfers between devices: none -> 38.2 us  [the longest x3 11.4 us: ring(): backward = lax.ppermute(backward, TM[0], down)]
    all_to_all x1, waiting for transfers between devices: 32.7 us -> 0.01 us  [steps(): lax.all_to_all(powers.reshape(tm_count, hours, 5 * n), TM, split_axis=0,...]
    all_to_all x1, waiting for transfers between devices: 36.8 us -> 6.85 us  [steps(): lax.all_to_all(halves.reshape(tm_count, part, all_hours), TM, split_axis=...]
    all_to_all x1 -> x0, blocking collectives: 21.6 us -> none  [steps(): arrived = lax.all_to_all(xd, TM, split_axis=0, concat_axis=0, tiled=True)]
    ppermute x1, waiting for transfers between devices: 11.7 us -> 5.94 us  [steps(): lax.ppermute(packed, REGION, [((r + 1) % regions, r) for r in range(regio...]
    all_to_all x1, blocking collectives: 11.6 us -> 15.4 us  [steps(): over_tm = lax.all_to_all(gram, TM, split_axis=0, concat_axis=0, tiled=True)]
    all_to_all x0 -> x1, starting transfers between devices: none -> 3.86 us  [steps(): arrived = lax.all_to_all(xd, TM, split_axis=0, concat_axis=0, tiled=True)]
  transfers between devices with their start and end apart: 6 -> 16, of which waited for: 3 -> 7; matrix products, arithmetic and copies ran while one was open for 1% -> 5% of each run, Pallas kernels for 2% -> 3%
where the time goes in v3:
time: 205 us; the launch traced here: 204 us
  starting transfers between devices  74.3 us (36%)
  waiting for transfers between devices  57 us (28%)
  blocking collectives  33.1 us (16%)
  Pallas kernels  23.5 us (11%)
  local copies, waits for them, and re-layouts  10.7 us (5%)
  other arithmetic  4.07 us (2%)
    ppermute x3, waiting for transfers between devices, ring(): backward = lax.ppermute(backward, TM[0], down)  28.1 us
    all_to_all x1, blocking collectives, steps(): lax.all_to_all(spread, REGION, split_axis=0, concat_axis=0, tiled=True)  17.7 us
    all_to_all x1, blocking collectives, steps(): over_tm = lax.all_to_all(gram, TM, split_axis=0, concat_axis=0, tiled=True)  15.4 us
    pallas_call x1, Pallas kernels, steps(): pl.pallas_call(spatial_kernel, out_shape=(jax.ShapeDtypeStruct((3 * half...  13.7 us
    ppermute x3, starting transfers between devices, ring(): backward = lax.ppermute(backward, TM[0], down)  11.4 us
    ppermute x1, starting transfers between devices, steps(): lax.ppermute(packed, REGION, [((r + 1) % regions, r) for r in range(regio...  11.3 us
    ppermute x1, starting transfers between devices, steps(): row = lax.ppermute(own_blocks, REGION_TM, pairs)  11.1 us
    all_to_all x1, starting transfers between devices, steps(): lax.all_to_all(halves.reshape(tm_count, part, all_hours), TM, split_axis=...  10.3 us
  transfers between devices with their start and end apart: 16, of which 7 were waited for; matrix products, arithmetic and copies ran while one was open for 5% of the time, Pallas kernels for 3%

profile of v3, /device:TPU:1, one launch (start us, length us, event | category | flops | bytes accessed | tf_op | source)
XLA Modules:
  0.0 203.5 jit_solution(5832077904214423157)
XLA Ops:
  0.6 2.0 broadcast_in_dim.14
  2.7 10.3 %all-to-all-start = ((bf16[16,32,1024]{2,1,0:T(8,128)(2,1)}), bf16[16,32,1024]{2,1,0:T(8,128)(2,1)S(1)}, u32[]{:S(2)}, u32[]{:S(2)}) async-start(bf16[16,32,1024]{2,1,0:T(8,128)(2,1)} %bitcast.4), calls=%async_computation | async-start | bytes 2097152 | tf_op jit(solution)/shard_map/all_to_all | solution.py:252
  13.6 2.3 %pack.1 = (bf16[1040,128]{1,0:T(8,128)(2,1)}, bf16[8,128,128]{2,1,0:T(8,128)(2,1)}, bf16[1152,128]{1,0:T(8,128)(2,1)}) custom-call(f32[64,2048]{1,0:T(8,128)} %right_ref.1, f32[64,2048]{1,0:T(8,128)} %x_ref.1, bf16[9,128,128]{2,1,0:T(8,128)(2,1)} %bitcast.9, bf16[16,128]{1,0:T(8,128)(2,1)} %pad.4.slots_ref), custom_call_target="tpu_custom_call" | custom-call | tf_op jit(solution)/shard_map/pack/pallas_call | solution.py:255
  15.9 11.3 %collective-permute-start = (bf16[1040,128]{1,0:T(8,128)(2,1)}, bf16[1040,128]{1,0:T(8,128)(2,1)}, u32[]{:S(2)}, u32[]{:S(2)}) collective-permute-start(bf16[1040,128]{1,0:T(8,128)(2,1)} %get-tuple-element.11), channel_id=1, source_target_pairs={{16,0},{32,16},{48,32},{64,48},{80,64},{96,80},{112,96},{128,112},... | collective-permute-start | bytes 798728 | tf_op jit(solution)/shard_map/ppermute | solution.py:266
  27.2 5.9 %collective-permute-done = bf16[1040,128]{1,0:T(8,128)(2,1)} collective-permute-done((bf16[1040,128]{1,0:T(8,128)(2,1)}, bf16[1040,128]{1,0:T(8,128)(2,1)}, u32[]{:S(2)}, u32[]{:S(2)}) %collective-permute-start) | collective-permute-done | bytes 266272 | tf_op jit(solution)/shard_map/ppermute | solution.py:266
  34.1 6.8 %all-to-all-done.own_ref = bf16[16,32,1024]{2,1,0:T(8,128)(2,1)S(1)} async-done(((bf16[16,32,1024]{2,1,0:T(8,128)(2,1)}), bf16[16,32,1024]{2,1,0:T(8,128)(2,1)S(1)}, u32[]{:S(2)}, u32[]{:S(2)}) %all-to-all-start) | async-done | bytes 1048608 | tf_op jit(solution)/shard_map/all_to_all | solution.py:252
  41.0 1.9 collective-permute-start.1
  42.9 1.8 pad_maximum_fusion.1.xd_ref
  44.7 3.9 %all-to-all-start.1 = ((bf16[16,128,128]{2,1,0:T(8,128)(2,1)}), bf16[16,128,128]{2,1,0:T(8,128)(2,1)S(1)}, u32[]{:S(2)}, u32[]{:S(2)}) async-start(bf16[16,128,128]{2,1,0:T(8,128)(2,1)} %pad_maximum_fusion.1.xd_ref), calls=%async_computation.1 | async-start | bytes 1048576 | tf_op jit(solution)/shard_map/all_to_all | solution.py:280
  48.6 11.1 %collective-permute-start.2 = (bf16[1152,128]{1,0:T(8,128)(2,1)S(1)}, bf16[1152,128]{1,0:T(8,128)(2,1)S(1)}, u32[]{:S(2)}, u32[]{:S(2)}) collective-permute-start(bf16[1152,128]{1,0:T(8,128)(2,1)S(1)} %copy-done.14), channel_id=1, source_target_pairs={{16,0},{17,1},{18,2},{19,3},{20,4},{21,5},{22,6},{23,7},{8,8},{9,9... | collective-permute-start | bytes 884744 | tf_op jit(solution)/shard_map/ppermute | solution.py:270
  59.7 6.1 %collective-permute-done.2.refs_0_ = bf16[1152,128]{1,0:T(8,128)(2,1)S(1)} collective-permute-done((bf16[1152,128]{1,0:T(8,128)(2,1)S(1)}, bf16[1152,128]{1,0:T(8,128)(2,1)S(1)}, u32[]{:S(2)}, u32[]{:S(2)}) %collective-permute-start.2) | collective-permute-done | bytes 294944 | tf_op jit(solution)/shard_map/ppermute | solution.py:270
  65.8 3.1 %collective-permute-start.3 = (bf16[1152,128]{1,0:T(8,128)(2,1)S(1)}, bf16[1152,128]{1,0:T(8,128)(2,1)S(1)}, u32[]{:S(2)}, u32[]{:S(2)}) collective-permute-start(bf16[1152,128]{1,0:T(8,128)(2,1)S(1)} %collective-permute-done.2.refs_0_), channel_id=1, source_target_pairs={{0,2},{2,4},{4,6},{6,8},{8,10},{10,12},{12,14},{14,0},{1,3},{3,5},... | collective-permute-start | bytes 884744 | tf_op jit(solution)/shard_map/ppermute | solution.py:228
  68.9 3.4 %collective-permute-start.4 = (bf16[1152,128]{1,0:T(8,128)(2,1)S(1)}, bf16[1152,128]{1,0:T(8,128)(2,1)S(1)}, u32[]{:S(2)}, u32[]{:S(2)}) collective-permute-start(bf16[1152,128]{1,0:T(8,128)(2,1)S(1)} %collective-permute-done.2.refs_0_), channel_id=1, source_target_pairs={{2,0},{4,2},{6,4},{8,6},{10,8},{12,10},{14,12},{0,14},{3,1},{5,3},... | collective-permute-start | bytes 884744 | tf_op jit(solution)/shard_map/ppermute | solution.py:231
  72.3 4.1 %collective-permute-done.3.refs_1_ = bf16[1152,128]{1,0:T(8,128)(2,1)S(1)} collective-permute-done((bf16[1152,128]{1,0:T(8,128)(2,1)S(1)}, bf16[1152,128]{1,0:T(8,128)(2,1)S(1)}, u32[]{:S(2)}, u32[]{:S(2)}) %collective-permute-start.3) | collective-permute-done | bytes 294944 | tf_op jit(solution)/shard_map/ppermute | solution.py:228
  76.4 1.9 collective-permute-start.5
  79.1 4.7 %temporal.1 = (bf16[1024,640]{1,0:T(8,128)(2,1)}, f32[8,128]{1,0:T(8,128)}) custom-call(s32[1]{0:T(128)} %bitcast.2.core_ref, bf16[16,32,1024]{2,1,0:T(8,128)(2,1)} %copy-done.1, bf16[16,32,1024]{2,1,0:T(8,128)(2,1)} %collective-permute-done.1.other_ref, bf16[16,128,128]{2,1,0:T(8,128)(2,1)} %copy-done.2), custom_call_target="tpu_custom_call" | custom-call | tf_op jit(solution)/shard_map/temporal/pallas_call | solution.py:281
  83.8 6.8 %all-to-all-start.2 = ((bf16[16,64,640]{2,1,0:T(8,128)(2,1)}), bf16[16,64,640]{2,1,0:T(8,128)(2,1)S(1)}, u32[]{:S(2)}, u32[]{:S(2)}) async-start(bf16[16,64,640]{2,1,0:T(8,128)(2,1)} %bitcast.7), calls=%async_computation.2 | async-start | bytes 2621440 | tf_op jit(solution)/shard_map/all_to_all | solution.py:291
  91.4 4.5 %collective-permute-start.6 = (bf16[1152,128]{1,0:T(8,128)(2,1)S(1)}, bf16[1152,128]{1,0:T(8,128)(2,1)S(1)}, u32[]{:S(2)}, u32[]{:S(2)}) collective-permute-start(bf16[1152,128]{1,0:T(8,128)(2,1)S(1)} %collective-permute-done.4.refs_2_), channel_id=1, source_target_pairs={{2,0},{4,2},{6,4},{8,6},{10,8},{12,10},{14,12},{0,14},{3,1},{5,3},... | collective-permute-start | bytes 884744 | tf_op jit(solution)/shard_map/ppermute | solution.py:231
  96.6 1.9 collective-permute-start.7
  99.2 28.1 %collective-permute-done.6.refs_4_ = bf16[1152,128]{1,0:T(8,128)(2,1)S(1)} collective-permute-done((bf16[1152,128]{1,0:T(8,128)(2,1)S(1)}, bf16[1152,128]{1,0:T(8,128)(2,1)S(1)}, u32[]{:S(2)}, u32[]{:S(2)}) %collective-permute-start.6) | collective-permute-done | bytes 294944 | tf_op jit(solution)/shard_map/ppermute | solution.py:231
  127.3 3.6 %collective-permute-start.8 = (bf16[1152,128]{1,0:T(8,128)(2,1)S(1)}, bf16[1152,128]{1,0:T(8,128)(2,1)S(1)}, u32[]{:S(2)}, u32[]{:S(2)}) collective-permute-start(bf16[1152,128]{1,0:T(8,128)(2,1)S(1)} %collective-permute-done.6.refs_4_), channel_id=1, source_target_pairs={{2,0},{4,2},{6,4},{8,6},{10,8},{12,10},{14,12},{0,14},{3,1},{5,3},... | collective-permute-start | bytes 884744 | tf_op jit(solution)/shard_map/ppermute | solution.py:231
  131.6 1.9 collective-permute-start.9
  134.3 3.2 %collective-permute-start.10 = (bf16[5760,128]{1,0:T(8,128)(2,1)}, bf16[5760,128]{1,0:T(8,128)(2,1)S(1)}, u32[]{:S(2)}, u32[]{:S(2)}) collective-permute-start(bf16[5760,128]{1,0:T(8,128)(2,1)} %constant_dynamic-update-slice_fusion), channel_id=1, source_target_pairs={{0,1},{1,0},{2,3},{3,2},{4,5},{5,4},{6,7},{7,6},{8,9},{9,8},{10,11... | collective-permute-start | bytes 4423688 | tf_op jit(solution)/shard_map/ppermute | solution.py:272
  137.6 4.8 %collective-permute-done.9.refs_7_ = bf16[1152,128]{1,0:T(8,128)(2,1)S(1)} collective-permute-done((bf16[1152,128]{1,0:T(8,128)(2,1)S(1)}, bf16[1152,128]{1,0:T(8,128)(2,1)S(1)}, u32[]{:S(2)}, u32[]{:S(2)}) %collective-permute-start.9) | collective-permute-done | bytes 294944 | tf_op jit(solution)/shard_map/ppermute | solution.py:228
  144.1 3.6 %collective-permute-start.11 = (bf16[3456,128]{1,0:T(8,128)(2,1)}, bf16[3456,128]{1,0:T(8,128)(2,1)}, u32[]{:S(2)}, u32[]{:S(2)}) collective-permute-start(bf16[3456,128]{1,0:T(8,128)(2,1)} %pad_maximum_fusion), channel_id=1, source_target_pairs={{0,1},{1,0},{2,3},{3,2},{4,5},{5,4},{6,7},{7,6},{8,9},{9,8},{10,11... | collective-permute-start | bytes 2654216 | tf_op jit(solution)/shard_map/ppermute | solution.py:273
  149.0 1.1 collective-permute-done.11.refs_9_
  150.2 1.0 copy-done
  151.2 13.7 %spatial.1 = (bf16[1552,128]{1,0:T(8,128)(2,1)}, f32[3,8,64,128]{3,2,1,0:T(8,128)}, f32[16,8,128]{2,1,0:T(8,128)}, f32[8,128]{1,0:T(8,128)}) custom-call(s32[1]{0:T(128)} %bitcast.tm_ref, s32[16,8]{1,0:T(8,128)} %pad_add_fusion.slots_ref, bf16[16,64,640]{2,1,0:T(8,128)(2,1)} %copy-done, bf16[16,128,128]{2,1,0:T(8,128)(2,1)} %pad_maximum_fusion.1.xd_ref, ...), custom_call_target="tpu_custom_call" | custom-call | tf_op jit(solution)/shard_map/spatial/pallas_call | solution.py:295
  164.9 1.9 collective-permute-start.12
  166.8 15.4 %all_to_all.25 = f32[16,8,128]{2,1,0:T(8,128)S(1)} all-to-all(f32[16,8,128]{2,1,0:T(8,128)} %get-tuple-element.16), channel_id=1, replica_groups=mesh['region_0'=4,'region_1'=8,'tm_0'=8,'tm_1'=2] {'tm_0','tm_1'}, dimensions={0} | all-to-all | bytes 131072 | tf_op jit(solution)/shard_map/all_to_all | solution.py:321
  182.3 17.7 %all_to_all.26.gram_ref = f32[32,8,128]{2,1,0:T(8,128)} all-to-all(f32[32,8,128]{2,1,0:T(8,128)S(1)} %broadcast_in_dim.15), channel_id=1, replica_groups=mesh['region_0'=4,'region_1'=8,'tm_0'=8,'tm_1'=2] {'region_0','region_1'}, dimensions={0} | all-to-all | bytes 262144 | tf_op jit(solution)/shard_map/all_to_all | solution.py:323
  200.7 2.8 %finish.1 = (f32[64,2048]{1,0:T(8,128)}, f32[64,2048]{1,0:T(8,128)}) custom-call(f32[32,8,128]{2,1,0:T(8,128)} %all_to_all.26.gram_ref, f32[64,2048]{1,0:T(8,128)} %x_ref.1, bf16[1552,128]{1,0:T(8,128)(2,1)} %copy-done.12, f32[3,8,64,128]{3,2,1,0:T(8,128)} %get-tuple-element.18.high_ref, f32[8,128]{1,0:T(8,128)} %get-tuple-element.19.centre_ref), custom_call_target="tpu_custom_call" | custom-call | tf_op jit(solution)/shard_map/finish/pallas_call | solution.py:324
  (53 shorter events, 10.0 us)
Async XLA Ops:
  0.6 12.3 %copy-start.13 = (s32[16,8]{0,1:T(8,128)S(1)}, s32[16,8]{0,1:T(8,128)}, u32[]{:S(2)}) copy-start(s32[16,8]{0,1:T(8,128)} %param.8) | copy-start | bytes 1540
  2.7 38.3 %all-to-all-start = ((bf16[16,32,1024]{2,1,0:T(8,128)(2,1)}), bf16[16,32,1024]{2,1,0:T(8,128)(2,1)S(1)}, u32[]{:S(2)}, u32[]{:S(2)}) async-start(bf16[16,32,1024]{2,1,0:T(8,128)(2,1)} %bitcast.4), calls=%async_computation | async-start | bytes 2097152 | tf_op jit(solution)/shard_map/all_to_all | solution.py:252
  15.9 32.7 %copy-start.14 = (bf16[1152,128]{1,0:T(8,128)(2,1)S(1)}, bf16[1152,128]{1,0:T(8,128)(2,1)}, u32[]{:S(2)}) copy-start(bf16[1152,128]{1,0:T(8,128)(2,1)} %get-tuple-element.15) | copy-start | bytes 884740
  15.9 17.3 %collective-permute-start = (bf16[1040,128]{1,0:T(8,128)(2,1)}, bf16[1040,128]{1,0:T(8,128)(2,1)}, u32[]{:S(2)}, u32[]{:S(2)}) collective-permute-start(bf16[1040,128]{1,0:T(8,128)(2,1)} %get-tuple-element.11), channel_id=1, source_target_pairs={{16,0},{32,16},{48,32},{64,48},{80,64},{96,80},{112,96},{128,112},... | collective-permute-start | bytes 798728 | tf_op jit(solution)/shard_map/ppermute | solution.py:266
  41.0 37.4 %copy-start.1 = (bf16[16,32,1024]{2,1,0:T(8,128)(2,1)}, bf16[16,32,1024]{2,1,0:T(8,128)(2,1)S(1)}, u32[]{:S(2)}) copy-start(bf16[16,32,1024]{2,1,0:T(8,128)(2,1)S(1)} %all-to-all-done.own_ref) | copy-start | bytes 3145732
  41.0 37.4 %collective-permute-start.1 = (bf16[16,32,1024]{2,1,0:T(8,128)(2,1)S(1)}, bf16[16,32,1024]{2,1,0:T(8,128)(2,1)}, u32[]{:S(2)}, u32[]{:S(2)}) collective-permute-start(bf16[16,32,1024]{2,1,0:T(8,128)(2,1)S(1)} %all-to-all-done.own_ref), channel_id=1, source_target_pairs={{0,1},{1,0},{2,3},{3,2},{4,5},{5,4},{6,7},{7,6},{8,9},{9,8},{10,11... | collective-permute-start | bytes 3145736 | tf_op jit(solution)/shard_map/ppermute | solution.py:277
  44.7 33.6 %all-to-all-start.1 = ((bf16[16,128,128]{2,1,0:T(8,128)(2,1)}), bf16[16,128,128]{2,1,0:T(8,128)(2,1)S(1)}, u32[]{:S(2)}, u32[]{:S(2)}) async-start(bf16[16,128,128]{2,1,0:T(8,128)(2,1)} %pad_maximum_fusion.1.xd_ref), calls=%async_computation.1 | async-start | bytes 1048576 | tf_op jit(solution)/shard_map/all_to_all | solution.py:280
  48.6 17.3 %collective-permute-start.2 = (bf16[1152,128]{1,0:T(8,128)(2,1)S(1)}, bf16[1152,128]{1,0:T(8,128)(2,1)S(1)}, u32[]{:S(2)}, u32[]{:S(2)}) collective-permute-start(bf16[1152,128]{1,0:T(8,128)(2,1)S(1)} %copy-done.14), channel_id=1, source_target_pairs={{16,0},{17,1},{18,2},{19,3},{20,4},{21,5},{22,6},{23,7},{8,8},{9,9... | collective-permute-start | bytes 884744 | tf_op jit(solution)/shard_map/ppermute | solution.py:270
  65.8 67.7 %copy-start.7 = (bf16[1152,128]{1,0:T(8,128)(2,1)}, bf16[1152,128]{1,0:T(8,128)(2,1)S(1)}, u32[]{:S(2)}) copy-start(bf16[1152,128]{1,0:T(8,128)(2,1)S(1)} %collective-permute-done.2.refs_0_) | copy-start | bytes 884740
  65.8 10.6 %collective-permute-start.3 = (bf16[1152,128]{1,0:T(8,128)(2,1)S(1)}, bf16[1152,128]{1,0:T(8,128)(2,1)S(1)}, u32[]{:S(2)}, u32[]{:S(2)}) collective-permute-start(bf16[1152,128]{1,0:T(8,128)(2,1)S(1)} %collective-permute-done.2.refs_0_), channel_id=1, source_target_pairs={{0,2},{2,4},{4,6},{6,8},{8,10},{10,12},{12,14},{14,0},{1,3},{3,5},... | collective-permute-start | bytes 884744 | tf_op jit(solution)/shard_map/ppermute | solution.py:228
  68.9 22.4 %collective-permute-start.4 = (bf16[1152,128]{1,0:T(8,128)(2,1)S(1)}, bf16[1152,128]{1,0:T(8,128)(2,1)S(1)}, u32[]{:S(2)}, u32[]{:S(2)}) collective-permute-start(bf16[1152,128]{1,0:T(8,128)(2,1)S(1)} %collective-permute-done.2.refs_0_), channel_id=1, source_target_pairs={{2,0},{4,2},{6,4},{8,6},{10,8},{12,10},{14,12},{0,14},{3,1},{5,3},... | collective-permute-start | bytes 884744 | tf_op jit(solution)/shard_map/ppermute | solution.py:231
  76.4 57.1 %copy-start.8 = (bf16[1152,128]{1,0:T(8,128)(2,1)}, bf16[1152,128]{1,0:T(8,128)(2,1)S(1)}, u32[]{:S(2)}) copy-start(bf16[1152,128]{1,0:T(8,128)(2,1)S(1)} %collective-permute-done.3.refs_1_) | copy-start | bytes 884740
  76.4 20.2 %collective-permute-start.5 = (bf16[1152,128]{1,0:T(8,128)(2,1)S(1)}, bf16[1152,128]{1,0:T(8,128)(2,1)S(1)}, u32[]{:S(2)}, u32[]{:S(2)}) collective-permute-start(bf16[1152,128]{1,0:T(8,128)(2,1)S(1)} %collective-permute-done.3.refs_1_), channel_id=1, source_target_pairs={{0,2},{2,4},{4,6},{6,8},{8,10},{10,12},{12,14},{14,0},{1,3},{3,5},... | collective-permute-start | bytes 884744 | tf_op jit(solution)/shard_map/ppermute | solution.py:228
  78.3 0.8 copy-start.2
  83.8 66.3 %all-to-all-start.2 = ((bf16[16,64,640]{2,1,0:T(8,128)(2,1)}), bf16[16,64,640]{2,1,0:T(8,128)(2,1)S(1)}, u32[]{:S(2)}, u32[]{:S(2)}) async-start(bf16[16,64,640]{2,1,0:T(8,128)(2,1)} %bitcast.7), calls=%async_computation.2 | async-start | bytes 2621440 | tf_op jit(solution)/shard_map/all_to_all | solution.py:291
  91.4 42.2 %copy-start.9 = (bf16[1152,128]{1,0:T(8,128)(2,1)}, bf16[1152,128]{1,0:T(8,128)(2,1)S(1)}, u32[]{:S(2)}) copy-start(bf16[1152,128]{1,0:T(8,128)(2,1)S(1)} %collective-permute-done.4.refs_2_) | copy-start | bytes 884740
  91.4 35.9 %collective-permute-start.6 = (bf16[1152,128]{1,0:T(8,128)(2,1)S(1)}, bf16[1152,128]{1,0:T(8,128)(2,1)S(1)}, u32[]{:S(2)}, u32[]{:S(2)}) collective-permute-start(bf16[1152,128]{1,0:T(8,128)(2,1)S(1)} %collective-permute-done.4.refs_2_), channel_id=1, source_target_pairs={{2,0},{4,2},{6,4},{8,6},{10,8},{12,10},{14,12},{0,14},{3,1},{5,3},... | collective-permute-start | bytes 884744 | tf_op jit(solution)/shard_map/ppermute | solution.py:231
  96.6 37.0 %copy-start.10 = (bf16[1152,128]{1,0:T(8,128)(2,1)}, bf16[1152,128]{1,0:T(8,128)(2,1)S(1)}, u32[]{:S(2)}) copy-start(bf16[1152,128]{1,0:T(8,128)(2,1)S(1)} %collective-permute-done.5.refs_3_) | copy-start | bytes 884740
  96.6 35.0 %collective-permute-start.7 = (bf16[1152,128]{1,0:T(8,128)(2,1)S(1)}, bf16[1152,128]{1,0:T(8,128)(2,1)S(1)}, u32[]{:S(2)}, u32[]{:S(2)}) collective-permute-start(bf16[1152,128]{1,0:T(8,128)(2,1)S(1)} %collective-permute-done.5.refs_3_), channel_id=1, source_target_pairs={{0,2},{2,4},{4,6},{6,8},{8,10},{10,12},{12,14},{14,0},{1,3},{3,5},... | collective-permute-start | bytes 884744 | tf_op jit(solution)/shard_map/ppermute | solution.py:228
  127.3 10.2 %copy-start.11 = (bf16[1152,128]{1,0:T(8,128)(2,1)}, bf16[1152,128]{1,0:T(8,128)(2,1)S(1)}, u32[]{:S(2)}) copy-start(bf16[1152,128]{1,0:T(8,128)(2,1)S(1)} %collective-permute-done.6.refs_4_) | copy-start | bytes 884740
  127.3 10.2 %collective-permute-start.8 = (bf16[1152,128]{1,0:T(8,128)(2,1)S(1)}, bf16[1152,128]{1,0:T(8,128)(2,1)S(1)}, u32[]{:S(2)}, u32[]{:S(2)}) collective-permute-start(bf16[1152,128]{1,0:T(8,128)(2,1)S(1)} %collective-permute-done.6.refs_4_), channel_id=1, source_target_pairs={{2,0},{4,2},{6,4},{8,6},{10,8},{12,10},{14,12},{0,14},{3,1},{5,3},... | collective-permute-start | bytes 884744 | tf_op jit(solution)/shard_map/ppermute | solution.py:231
  131.6 18.5 %copy-start.4 = (bf16[1152,128]{1,0:T(8,128)(2,1)}, bf16[1152,128]{1,0:T(8,128)(2,1)S(1)}, u32[]{:S(2)}) copy-start(bf16[1152,128]{1,0:T(8,128)(2,1)S(1)} %collective-permute-done.7.refs_5_) | copy-start | bytes 884740
  131.6 10.8 %collective-permute-start.9 = (bf16[1152,128]{1,0:T(8,128)(2,1)S(1)}, bf16[1152,128]{1,0:T(8,128)(2,1)S(1)}, u32[]{:S(2)}, u32[]{:S(2)}) collective-permute-start(bf16[1152,128]{1,0:T(8,128)(2,1)S(1)} %collective-permute-done.7.refs_5_), channel_id=1, source_target_pairs={{0,2},{2,4},{4,6},{6,8},{8,10},{10,12},{12,14},{14,0},{1,3},{3,5},... | collective-permute-start | bytes 884744 | tf_op jit(solution)/shard_map/ppermute | solution.py:228
  134.3 14.7 %collective-permute-start.10 = (bf16[5760,128]{1,0:T(8,128)(2,1)}, bf16[5760,128]{1,0:T(8,128)(2,1)S(1)}, u32[]{:S(2)}, u32[]{:S(2)}) collective-permute-start(bf16[5760,128]{1,0:T(8,128)(2,1)} %constant_dynamic-update-slice_fusion), channel_id=1, source_target_pairs={{0,1},{1,0},{2,3},{3,2},{4,5},{5,4},{6,7},{7,6},{8,9},{9,8},{10,11... | collective-permute-start | bytes 4423688 | tf_op jit(solution)/shard_map/ppermute | solution.py:272
  137.6 12.6 %copy-start.5 = (bf16[1152,128]{1,0:T(8,128)(2,1)}, bf16[1152,128]{1,0:T(8,128)(2,1)S(1)}, u32[]{:S(2)}) copy-start(bf16[1152,128]{1,0:T(8,128)(2,1)S(1)} %collective-permute-done.8.refs_6_) | copy-start | bytes 884740
  142.4 0.7 copy-start.6
  144.1 6.0 %collective-permute-start.11 = (bf16[3456,128]{1,0:T(8,128)(2,1)}, bf16[3456,128]{1,0:T(8,128)(2,1)}, u32[]{:S(2)}, u32[]{:S(2)}) collective-permute-start(bf16[3456,128]{1,0:T(8,128)(2,1)} %pad_maximum_fusion), channel_id=1, source_target_pairs={{0,1},{1,0},{2,3},{3,2},{4,5},{5,4},{6,7},{7,6},{8,9},{9,8},{10,11... | collective-permute-start | bytes 2654216 | tf_op jit(solution)/shard_map/ppermute | solution.py:273
  149.0 1.2 copy-start.3
  150.1 1.1 copy-start
  164.9 35.1 %collective-permute-start.12 = (bf16[1552,128]{1,0:T(8,128)(2,1)}, bf16[1552,128]{1,0:T(8,128)(2,1)S(1)}, u32[]{:S(2)}, u32[]{:S(2)}) collective-permute-start(bf16[1552,128]{1,0:T(8,128)(2,1)} %get-tuple-element.17), channel_id=1, source_target_pairs={{0,16},{16,32},{32,48},{48,64},{64,80},{80,96},{96,112},{112,128},... | collective-permute-start | bytes 1191944 | tf_op jit(solution)/shard_map/ppermute | solution.py:320
  199.9 0.7 copy-start.12

commit v4 on v2

--- a/solution.py
+++ b/solution.py
@@ -33,48 +33,58 @@
             send_ref[2 * hours * i : 2 * hours * (i + 1), :] = pair
         else:
             keep_ref[i - half] = pair
-    base = 2 * hours * half
-    extra = slots_ref.shape[0]
-    send_ref[base : base + extra, :] = slots_ref[...]
+    send_ref[2 * hours * half :, :] = slots_ref[...]
     for k in range(width):
-        flipped = blocks_ref[k].T
-        own_ref[k * n : (k + 1) * n, :] = flipped
-        send_ref[base + extra + k * n : base + extra + (k + 1) * n, :] = flipped
-
-
-def temporal_kernel(core_ref, own_ref, other_ref, v_ref, w_ref, shift_ref):
-    groups, part, hours = own_ref.shape
-    n = v_ref.shape[2]
-    core = core_ref[0]
-    row = lax.broadcasted_iota(jnp.int32, (part, n), 0)
-    lane = lax.broadcasted_iota(jnp.int32, (part, n), 1)
-    diagonal = jnp.zeros((part, n), F32)
-    for t in range(groups):
-        first_row = 2 * part * t
-        lanes = slice(first_row // n * n, first_row // n * n + n)
-        for ref, which in ((own_ref, core), (other_ref, 1 - core)):
-            at = row + (first_row % n + part * which)
-            diagonal = diagonal + jnp.where(lane == at, ref[t, :, lanes].astype(F32), 0.0)
-    c0 = jnp.sum(diagonal, axis=(0, 1), keepdims=True) / hours
+        own_ref[k * n : (k + 1) * n, :] = blocks_ref[k].T
+
+
+def chip_order(position, half):
+    away = [0]
+    for k in range(1, half // 2 + 1):
+        away += [k, half - k] if 2 * k < half else [k]
+    return [lax.rem(position // 2 + half - k, half) for k in away]
+
+
+def temporal_kernel(tm_ref, own_near, own_far, other_near, other_far, v_ref, w_ref, shift_ref):
+    groups, hours, _ = w_ref.shape
+    half, n = groups // 2, v_ref.shape[2]
+    count = groups * hours
+    core = lax.rem(tm_ref[0], 2)
+    chips = chip_order(tm_ref[0], half)
+    split = own_near.shape[0] // hours
+    row = lax.broadcasted_iota(jnp.int32, (hours, n), 0)
+    lane = lax.broadcasted_iota(jnp.int32, (hours, n), 1)
+    diagonal = jnp.zeros((hours, n), F32)
+    places = []
+    for which, refs in ((core, (own_near, own_far)), (1 - core, (other_near, other_far))):
+        for part, first in ((0, 0), (1, split)):
+            group = []
+            for k in range(refs[part].shape[0] // hours):
+                chip = chips[first + k]
+                tile = refs[part][k * hours : (k + 1) * hours, pl.ds(pl.multiple_of(chip * n, n), n)]
+                diagonal = diagonal + jnp.where(lane == row + hours * which, tile.astype(F32), 0.0)
+                group.append(2 * chip + which)
+            places.append((refs[part], group))
+    c0 = jnp.sum(diagonal, axis=(0, 1), keepdims=True) / count
     shift_ref[...] = jnp.broadcast_to(c0, shift_ref.shape)
 
-    mine = own_ref[...].reshape(groups * part, hours)
-    theirs = other_ref[...].reshape(groups * part, hours)
-
-    def power(v, base):
-        wide = v.shape[1]
-        by_core = jnp.stack([dot(mine, v).reshape(groups, part, wide), dot(theirs, v).reshape(groups, part, wide)], axis=1)
-        swapped = jnp.stack([by_core[:, 1], by_core[:, 0]], axis=1)
-        full = jnp.where(core == 0, by_core, swapped).reshape(hours, wide)
-        out = (full - c0 * v.astype(F32)).astype(BF16)
-        w_ref[:, base : base + wide] = out
-        return out
-
-    v = v_ref[...]
-    pairs = [v[:, k * 2 * part : (k + 1) * 2 * part].reshape(hours, n) for k in range(2)]
-    first = power(jnp.concatenate(pairs, axis=1), 0)
-    second = power(first, 2 * n)
-    power(second[:, :n], 4 * n)
+    def power(whole, piece, base):
+        wide = whole.shape[1]
+        for ref, group in places:
+            out = dot(ref[...], whole)
+            for k, t in enumerate(group):
+                value = out[k * hours : (k + 1) * hours] - c0 * piece(t).astype(F32)
+                w_ref[t, :, base : base + wide] = value.astype(BF16)
+
+    x = v_ref[:, 0:hours].reshape(count, n)
+    d = v_ref[:, hours : 2 * hours].reshape(count, n)
+    power(
+        jnp.concatenate([x, d], axis=1),
+        lambda t: jnp.concatenate([v_ref[t, 0:hours], v_ref[t, hours : 2 * hours]], axis=1),
+        0,
+    )
+    power(w_ref[:, :, 0 : 2 * n].reshape(count, 2 * n), lambda t: w_ref[t, :, 0 : 2 * n], 2 * n)
+    power(w_ref[:, :, 2 * n : 3 * n].reshape(count, n), lambda t: w_ref[t, :, 2 * n : 3 * n], 4 * n)
 
 
 def spatial_kernel(
@@ -210,6 +220,21 @@
     )
 
 
+def ring(row):
+    count = lax.axis_size(TM[0])
+    up = [(i, (i + 1) % count) for i in range(count)]
+    down = [(j, i) for i, j in up]
+    found = [row]
+    forward = backward = row
+    for k in range(1, count // 2 + 1):
+        forward = lax.ppermute(forward, TM[0], up)
+        found.append(forward)
+        if k < count // 2:
+            backward = lax.ppermute(backward, TM[0], down)
+            found.append(backward)
+    return found[:5], found[5:]
+
+
 def steps(right_side, initial, blocks, neighbour_blocks, temporal_cov):
     hours, sites = right_side.shape
     n = blocks.shape[2]
@@ -219,20 +244,20 @@
     slots = neighbour_blocks.shape[1]
     tm_count = lax.axis_size(TM)
     regions = lax.axis_size(REGION)
-    all_hours = temporal_cov.shape[1]
-    part = hours // 2
 
     local_slots = lax.rem(neighbour_blocks, rows)
     extra = jnp.pad(local_slots[:half].astype(BF16), ((0, 16 - half), (0, n - slots)))
     base = 2 * hours * half
-    halves = jnp.broadcast_to(temporal_cov.reshape(1, 2, part, all_hours), (tm_count // 2, 2, part, all_hours))
-    mine = lax.all_to_all(
-        halves.reshape(tm_count, part, all_hours), TM, split_axis=0, concat_axis=0, tiled=True
-    )
+    swap = [(0, 1), (1, 0)]
+    near, far = ring(temporal_cov)
+    own_near, own_far = jnp.concatenate(near, axis=0), jnp.concatenate(far, axis=0)
+    other_near = lax.ppermute(own_near, TM[1], swap)
+    other_far = lax.ppermute(own_far, TM[1], swap)
+    covariance = (own_near, own_far, other_near, other_far)
     packed, keep, own_blocks = pl.pallas_call(
         pack_kernel,
         out_shape=(
-            jax.ShapeDtypeStruct((base + 16 + width * n, n), BF16),
+            jax.ShapeDtypeStruct((base + 16, n), BF16),
             jax.ShapeDtypeStruct((half, 2 * hours, n), BF16),
             jax.ShapeDtypeStruct((width * n, n), BF16),
         ),
@@ -241,27 +266,27 @@
         name="pack",
     )(right_side, initial, blocks[0], extra)
     shifted = lax.ppermute(packed, REGION, [((r + 1) % regions, r) for r in range(regions)])
-    window_row = jnp.where(lax.axis_index(TM) < half, shifted[base + 16 :], own_blocks)
-    window_blocks = lax.all_gather(window_row[None], TM, axis=0, tiled=True)
+    pairs = [
+        (((r + (t < half)) % regions) * tm_count + t, r * tm_count + t) for r in range(regions) for t in range(tm_count)
+    ]
+    row = lax.ppermute(own_blocks, REGION_TM, pairs)
+    window_blocks = lax.all_gather(row[None], TM, axis=0, tiled=True)
     xd = jnp.concatenate([shifted[:base].reshape(half, 2 * hours, n), keep], axis=0)
-    window_slots = jnp.concatenate(
-        [shifted[base : base + half, :slots].astype(jnp.int32), local_slots[half:]], axis=0
-    )
-
-    theirs = lax.ppermute(mine, TM[1], [(0, 1), (1, 0)])
-    core = lax.axis_index(TM[1]).astype(jnp.int32).reshape(1)
+    window_slots = jnp.concatenate([shifted[base : base + half, :slots].astype(jnp.int32), local_slots[half:]], axis=0)
+
+    position = lax.axis_index(TM).astype(jnp.int32).reshape(1)
     arrived = lax.all_to_all(xd, TM, split_axis=0, concat_axis=0, tiled=True)
     powers, shift = pl.pallas_call(
         temporal_kernel,
         out_shape=(
-            jax.ShapeDtypeStruct((all_hours, 5 * n), BF16),
+            jax.ShapeDtypeStruct((tm_count, hours, 5 * n), BF16),
             jax.ShapeDtypeStruct((8, n), F32),
         ),
-        in_specs=[SMEM, VMEM, VMEM, VMEM],
+        in_specs=[SMEM] + [VMEM] * 5,
         out_specs=(VMEM, VMEM),
         name="temporal",
-    )(core, mine, theirs, arrived)
-    returned = lax.all_to_all(powers.reshape(tm_count, hours, 5 * n), TM, split_axis=0, concat_axis=0, tiled=True)
+    )(position, *covariance, arrived)
+    returned = lax.all_to_all(powers, TM, split_axis=0, concat_axis=0, tiled=True)
 
     low, high, gram, centre = pl.pallas_call(
         spatial_kernel,

time: 209 us -> 200 us (0.957)
  starting transfers between devices: 31.9 us -> 65.7 us
  blocking collectives: 50.9 us -> 27.3 us
  waiting for transfers between devices: 81.2 us -> 61.9 us
    ppermute x1 -> x10, starting transfers between devices: 1.91 us -> 40.1 us  [the longest x1 13.8 us: steps(): row = lax.ppermute(own_blocks, REGION_TM, pairs)]
    all_to_all x2, waiting for transfers between devices: 69.5 us -> 32.7 us  [the longest x1 32.6 us: steps(): lax.all_to_all(powers, TM, split_axis=0, concat_axis=0, tiled=True)]
    ppermute x1 -> x10, waiting for transfers between devices: 0.01 us -> 29.2 us  [the longest x4 19.7 us: ring(): forward = lax.ppermute(forward, TM[0], up)]
    all_to_all x1 -> x0, blocking collectives: 21.6 us -> none  [steps(): arrived = lax.all_to_all(xd, TM, split_axis=0, concat_axis=0, tiled=True)]
    ppermute x1, waiting for transfers between devices: 11.7 us -> 0.01 us  [steps(): lax.ppermute(packed, REGION, [((r + 1) % regions, r) for r in range(regio...]
    ppermute x1, starting transfers between devices: 13.7 us -> 7.32 us  [steps(): lax.ppermute(packed, REGION, [((r + 1) % regions, r) for r in range(regio...]
    unnamed x13 -> x27, local copies, waits for them, and re-layouts: 3.62 us -> 4.54 us
  transfers between devices with their start and end apart: 6 -> 15, of which waited for: 3 -> 7; matrix products, arithmetic and copies ran while one was open for 1% -> 1% of each run, Pallas kernels for 2% -> 3%
where the time goes in v4:
time: 200 us; the launch traced here: 199 us
  starting transfers between devices  65.7 us (33%)
  waiting for transfers between devices  61.9 us (31%)
  blocking collectives  27.3 us (14%)
  Pallas kernels  22.8 us (11%)
  between operations  14.3 us (7%)
  local copies, waits for them, and re-layouts  5.19 us (3%)
    all_to_all x1, waiting for transfers between devices, steps(): lax.all_to_all(powers, TM, split_axis=0, concat_axis=0, tiled=True)  32.6 us
    ppermute x4, waiting for transfers between devices, ring(): forward = lax.ppermute(forward, TM[0], up)  19.7 us
    all_to_all x1, blocking collectives, steps(): lax.all_to_all(spread, REGION, split_axis=0, concat_axis=0, tiled=True)  15.8 us
    ppermute x1, starting transfers between devices, steps(): row = lax.ppermute(own_blocks, REGION_TM, pairs)  13.8 us
    pallas_call x1, Pallas kernels, steps(): pl.pallas_call(spatial_kernel, out_shape=(jax.ShapeDtypeStruct((3 * half...  12.7 us
    ppermute x4, starting transfers between devices, ring(): forward = lax.ppermute(forward, TM[0], up)  12 us
    all_to_all x1, blocking collectives, steps(): over_tm = lax.all_to_all(gram, TM, split_axis=0, concat_axis=0, tiled=True)  11.6 us
    all_to_all x1, starting transfers between devices, steps(): arrived = lax.all_to_all(xd, TM, split_axis=0, concat_axis=0, tiled=True)  10.2 us
  transfers between devices with their start and end apart: 15, of which 7 were waited for; matrix products, arithmetic and copies ran while one was open for 1% of the time, Pallas kernels for 3%

profile of v4, /device:TPU:1, one launch (start us, length us, event | category | flops | bytes accessed | tf_op | source)
XLA Modules:
  0.0 198.7 jit_solution(6624585792386015097)
XLA Ops:
  7.2 0.8 copy.7
  8.6 2.3 %pack.1 = (bf16[1040,128]{1,0:T(8,128)(2,1)}, bf16[8,128,128]{2,1,0:T(8,128)(2,1)}, bf16[1152,128]{1,0:T(8,128)(2,1)}) custom-call(f32[64,2048]{1,0:T(8,128)} %right_ref.1, f32[64,2048]{1,0:T(8,128)} %x_ref.1, bf16[9,128,128]{2,1,0:T(8,128)(2,1)} %bitcast.6, bf16[16,128]{1,0:T(8,128)(2,1)} %pad.4.slots_ref), custom_call_target="tpu_custom_call" | custom-call | tf_op jit(solution)/shard_map/pack/pallas_call | solution.py:257
  10.9 13.8 %collective-permute-start.10 = (bf16[1152,128]{1,0:T(8,128)(2,1)}, bf16[1152,128]{1,0:T(8,128)(2,1)S(1)}, u32[]{:S(2)}, u32[]{:S(2)}) collective-permute-start(bf16[1152,128]{1,0:T(8,128)(2,1)} %get-tuple-element.15), channel_id=1, source_target_pairs={{16,0},{17,1},{18,2},{19,3},{20,4},{21,5},{22,6},{23,7},{8,8},{9,9... | collective-permute-start | bytes 884744 | tf_op jit(solution)/shard_map/ppermute | solution.py:272
  24.7 6.0 %collective-permute-done.10 = bf16[1152,128]{1,0:T(8,128)(2,1)S(1)} collective-permute-done((bf16[1152,128]{1,0:T(8,128)(2,1)}, bf16[1152,128]{1,0:T(8,128)(2,1)S(1)}, u32[]{:S(2)}, u32[]{:S(2)}) %collective-permute-start.10) | collective-permute-done | bytes 294944 | tf_op jit(solution)/shard_map/ppermute | solution.py:272
  30.7 0.7 copy-done.7
  31.4 7.3 %collective-permute-start = (bf16[1040,128]{1,0:T(8,128)(2,1)}, bf16[1040,128]{1,0:T(8,128)(2,1)S(1)}, u32[]{:S(2)}, u32[]{:S(2)}) collective-permute-start(bf16[1040,128]{1,0:T(8,128)(2,1)} %get-tuple-element.11), channel_id=1, source_target_pairs={{16,0},{32,16},{48,32},{64,48},{80,64},{96,80},{112,96},{128,112},... | collective-permute-start | bytes 798728 | tf_op jit(solution)/shard_map/ppermute | solution.py:268
  38.8 3.2 %collective-permute-start.1 = (bf16[64,1024]{1,0:T(8,128)(2,1)S(1)}, bf16[64,1024]{1,0:T(8,128)(2,1)S(1)}, u32[]{:S(2)}, u32[]{:S(2)}) collective-permute-start(bf16[64,1024]{1,0:T(8,128)(2,1)S(1)} %copy-done.9), channel_id=1, source_target_pairs={{0,2},{2,4},{4,6},{6,8},{8,10},{10,12},{12,14},{14,0},{1,3},{3,5},... | collective-permute-start | bytes 393224 | tf_op jit(solution)/shard_map/ppermute | solution.py:230
  42.0 3.3 %collective-permute-start.2 = (bf16[64,1024]{1,0:T(8,128)(2,1)S(1)}, bf16[64,1024]{1,0:T(8,128)(2,1)S(1)}, u32[]{:S(2)}, u32[]{:S(2)}) collective-permute-start(bf16[64,1024]{1,0:T(8,128)(2,1)S(1)} %copy-done.9), channel_id=1, source_target_pairs={{2,0},{4,2},{6,4},{8,6},{10,8},{12,10},{14,12},{0,14},{3,1},{5,3},... | collective-permute-start | bytes 393224 | tf_op jit(solution)/shard_map/ppermute | solution.py:233
  45.7 3.4 %collective-permute-start.3 = (bf16[64,1024]{1,0:T(8,128)(2,1)S(1)}, bf16[64,1024]{1,0:T(8,128)(2,1)S(1)}, u32[]{:S(2)}, u32[]{:S(2)}) collective-permute-start(bf16[64,1024]{1,0:T(8,128)(2,1)S(1)} %collective-permute-done.1), channel_id=1, source_target_pairs={{0,2},{2,4},{4,6},{6,8},{8,10},{10,12},{12,14},{14,0},{1,3},{3,5},... | collective-permute-start | bytes 393224 | tf_op jit(solution)/shard_map/ppermute | solution.py:230
  49.1 2.3 %collective-permute-done.2 = bf16[64,1024]{1,0:T(8,128)(2,1)S(1)} collective-permute-done((bf16[64,1024]{1,0:T(8,128)(2,1)S(1)}, bf16[64,1024]{1,0:T(8,128)(2,1)S(1)}, u32[]{:S(2)}, u32[]{:S(2)}) %collective-permute-start.2) | collective-permute-done | bytes 131104 | tf_op jit(solution)/shard_map/ppermute | solution.py:233
  51.3 1.9 collective-permute-start.4
  53.3 0.8 pad_maximum_fusion.xd_ref
  54.2 10.2 %all-to-all-start = ((bf16[16,128,128]{2,1,0:T(8,128)(2,1)}), bf16[16,128,128]{2,1,0:T(8,128)(2,1)S(1)}, u32[]{:S(2)}, u32[]{:S(2)}) async-start(bf16[16,128,128]{2,1,0:T(8,128)(2,1)} %pad_maximum_fusion.xd_ref), calls=%async_computation | async-start | bytes 1048576 | tf_op jit(solution)/shard_map/all_to_all | solution.py:278
  64.4 3.3 %collective-permute-start.5 = (bf16[64,1024]{1,0:T(8,128)(2,1)S(1)}, bf16[64,1024]{1,0:T(8,128)(2,1)S(1)}, u32[]{:S(2)}, u32[]{:S(2)}) collective-permute-start(bf16[64,1024]{1,0:T(8,128)(2,1)S(1)} %collective-permute-done.3), channel_id=1, source_target_pairs={{0,2},{2,4},{4,6},{6,8},{8,10},{10,12},{12,14},{14,0},{1,3},{3,5},... | collective-permute-start | bytes 393224 | tf_op jit(solution)/shard_map/ppermute | solution.py:230
  67.7 3.2 %collective-permute-start.6 = (bf16[64,1024]{1,0:T(8,128)(2,1)S(1)}, bf16[64,1024]{1,0:T(8,128)(2,1)S(1)}, u32[]{:S(2)}, u32[]{:S(2)}) collective-permute-start(bf16[64,1024]{1,0:T(8,128)(2,1)S(1)} %collective-permute-done.4), channel_id=1, source_target_pairs={{2,0},{4,2},{6,4},{8,6},{10,8},{12,10},{14,12},{0,14},{3,1},{5,3},... | collective-permute-start | bytes 393224 | tf_op jit(solution)/shard_map/ppermute | solution.py:233
  71.0 2.6 %collective-permute-start.8 = (bf16[320,1024]{1,0:T(8,128)(2,1)S(1)}, bf16[320,1024]{1,0:T(8,128)(2,1)S(1)}, u32[]{:S(2)}, u32[]{:S(2)}) collective-permute-start(bf16[320,1024]{1,0:T(8,128)(2,1)S(1)} %constant_dynamic-update-slice_fusion.own_near), channel_id=1, source_target_pairs={{0,1},{1,0},{2,3},{3,2},{4,5},{5,4},{6,7},{7,6},{8,9},{9,8},{10,11... | collective-permute-start | bytes 1966088 | tf_op jit(solution)/shard_map/ppermute | solution.py:254
  73.5 13.9 %collective-permute-done.5 = bf16[64,1024]{1,0:T(8,128)(2,1)S(1)} collective-permute-done((bf16[64,1024]{1,0:T(8,128)(2,1)S(1)}, bf16[64,1024]{1,0:T(8,128)(2,1)S(1)}, u32[]{:S(2)}, u32[]{:S(2)}) %collective-permute-start.5) | collective-permute-done | bytes 131104 | tf_op jit(solution)/shard_map/ppermute | solution.py:230
  87.5 2.2 %collective-permute-start.7 = (bf16[64,1024]{1,0:T(8,128)(2,1)S(1)}, bf16[64,1024]{1,0:T(8,128)(2,1)S(1)}, u32[]{:S(2)}, u32[]{:S(2)}) collective-permute-start(bf16[64,1024]{1,0:T(8,128)(2,1)S(1)} %collective-permute-done.5), channel_id=1, source_target_pairs={{0,2},{2,4},{4,6},{6,8},{8,10},{10,12},{12,14},{14,0},{1,3},{3,5},... | collective-permute-start | bytes 393224 | tf_op jit(solution)/shard_map/ppermute | solution.py:230
  89.7 5.3 %collective-permute-done.7 = bf16[64,1024]{1,0:T(8,128)(2,1)S(1)} collective-permute-done((bf16[64,1024]{1,0:T(8,128)(2,1)S(1)}, bf16[64,1024]{1,0:T(8,128)(2,1)S(1)}, u32[]{:S(2)}, u32[]{:S(2)}) %collective-permute-start.7) | collective-permute-done | bytes 131104 | tf_op jit(solution)/shard_map/ppermute | solution.py:230
  95.1 3.3 %collective-permute-start.9 = (bf16[192,1024]{1,0:T(8,128)(2,1)S(1)}, bf16[192,1024]{1,0:T(8,128)(2,1)S(1)}, u32[]{:S(2)}, u32[]{:S(2)}) collective-permute-start(bf16[192,1024]{1,0:T(8,128)(2,1)S(1)} %constant_dynamic-update-slice_fusion.5.own_far), channel_id=1, source_target_pairs={{0,1},{1,0},{2,3},{3,2},{4,5},{5,4},{6,7},{7,6},{8,9},{9,8},{10,11... | collective-permute-start | bytes 1179656 | tf_op jit(solution)/shard_map/ppermute | solution.py:255
  98.4 1.3 collective-permute-done.9.other_far
  99.8 0.7 copy-done.6
  100.9 5.0 %temporal.1 = (bf16[16,64,640]{2,1,0:T(8,128)(2,1)}, f32[8,128]{1,0:T(8,128)}) custom-call(s32[1]{0:T(128)} %bitcast.1.tm_ref, bf16[320,1024]{1,0:T(8,128)(2,1)} %copy-done.2, bf16[192,1024]{1,0:T(8,128)(2,1)} %copy-done.3, bf16[320,1024]{1,0:T(8,128)(2,1)} %copy-done.4, bf16[192,1024]{1,0:T(8,128)(2,1)} %copy-done.6, bf16[16,128,128]{2,1,0:T(8,128)(2,1)} %copy-done.1), custom_call_target="tpu_custom_call" | custom-call | tf_op jit(solution)/shard_map/temporal/pallas_call | solution.py:279
  105.9 6.1 %all-to-all-start.1 = ((bf16[16,64,640]{2,1,0:T(8,128)(2,1)}), bf16[16,64,640]{2,1,0:T(8,128)(2,1)S(1)}, u32[]{:S(2)}, u32[]{:S(2)}) async-start(bf16[16,64,640]{2,1,0:T(8,128)(2,1)} %get-tuple-element.13), calls=%async_computation.1 | async-start | bytes 2621440 | tf_op jit(solution)/shard_map/all_to_all | solution.py:289
  112.6 32.6 %all-to-all-done.1.g_ref = bf16[16,64,640]{2,1,0:T(8,128)(2,1)S(1)} async-done(((bf16[16,64,640]{2,1,0:T(8,128)(2,1)}), bf16[16,64,640]{2,1,0:T(8,128)(2,1)S(1)}, u32[]{:S(2)}, u32[]{:S(2)}) %all-to-all-start.1) | async-done | bytes 1310752 | tf_op jit(solution)/shard_map/all_to_all | solution.py:289
  145.3 1.1 copy-done
  146.3 12.7 %spatial.1 = (bf16[1552,128]{1,0:T(8,128)(2,1)}, f32[3,8,64,128]{3,2,1,0:T(8,128)}, f32[16,8,128]{2,1,0:T(8,128)}, f32[8,128]{1,0:T(8,128)}) custom-call(s32[16,8]{1,0:T(8,128)} %pad_add_fusion.slots_ref, bf16[16,64,640]{2,1,0:T(8,128)(2,1)} %copy-done, bf16[16,128,128]{2,1,0:T(8,128)(2,1)} %pad_maximum_fusion.xd_ref, f32[8,128]{1,0:T(8,128)} %get-tuple-element.14.shift_ref, ...), custom_call_target="tpu_custom_call" | custom-call | tf_op jit(solution)/shard_map/spatial/pallas_call | solution.py:291
  159.0 1.9 collective-permute-start.11
  160.9 11.6 %all_to_all.20 = f32[16,8,128]{2,1,0:T(8,128)S(1)} all-to-all(f32[16,8,128]{2,1,0:T(8,128)} %get-tuple-element.16), channel_id=1, replica_groups=mesh['region_0'=4,'region_1'=8,'tm_0'=8,'tm_1'=2] {'tm_0','tm_1'}, dimensions={0} | all-to-all | bytes 131072 | tf_op jit(solution)/shard_map/all_to_all | solution.py:317
  172.5 15.8 %all_to_all.21.gram_ref = f32[32,8,128]{2,1,0:T(8,128)} all-to-all(f32[32,8,128]{2,1,0:T(8,128)S(1)} %broadcast_in_dim.10), channel_id=1, replica_groups=mesh['region_0'=4,'region_1'=8,'tm_0'=8,'tm_1'=2] {'region_0','region_1'}, dimensions={0} | all-to-all | bytes 262144 | tf_op jit(solution)/shard_map/all_to_all | solution.py:319
  188.3 0.8 copy-done.5
  189.1 2.8 %finish.1 = (f32[64,2048]{1,0:T(8,128)}, f32[64,2048]{1,0:T(8,128)}) custom-call(f32[32,8,128]{2,1,0:T(8,128)} %all_to_all.21.gram_ref, f32[64,2048]{1,0:T(8,128)} %x_ref.1, bf16[1552,128]{1,0:T(8,128)(2,1)} %copy-done.5, f32[3,8,64,128]{3,2,1,0:T(8,128)} %get-tuple-element.18.high_ref, f32[8,128]{1,0:T(8,128)} %get-tuple-element.19.centre_ref), custom_call_target="tpu_custom_call" | custom-call | tf_op jit(solution)/shard_map/finish/pallas_call | solution.py:320
  (43 shorter events, 2.2 us)
Async XLA Ops:
  7.2 31.6 %copy-start.9 = (bf16[64,1024]{1,0:T(8,128)(2,1)S(1)}, bf16[64,1024]{1,0:T(8,128)(2,1)}, u32[]{:S(2)}) copy-start(bf16[64,1024]{1,0:T(8,128)(2,1)} %param.9) | copy-start | bytes 393220
  7.2 138.1 %all-gather.3.cloned.1.call-start = ((), (), s32[]{:S(2)}) async-start(), calls=%async_computation.4 | async-start | bytes 5013504 | tf_op jit(solution)/shard_map/all_gather | solution.py:273
  10.9 42.4 %copy-start.8 = (bf16[8,128,128]{2,1,0:T(8,128)(2,1)S(1)}, bf16[8,128,128]{2,1,0:T(8,128)(2,1)}, u32[]{:S(2)}) copy-start(bf16[8,128,128]{2,1,0:T(8,128)(2,1)} %get-tuple-element.12) | copy-start | bytes 786436
  10.9 19.8 %collective-permute-start.10 = (bf16[1152,128]{1,0:T(8,128)(2,1)}, bf16[1152,128]{1,0:T(8,128)(2,1)S(1)}, u32[]{:S(2)}, u32[]{:S(2)}) collective-permute-start(bf16[1152,128]{1,0:T(8,128)(2,1)} %get-tuple-element.15), channel_id=1, source_target_pairs={{16,0},{17,1},{18,2},{19,3},{20,4},{21,5},{22,6},{23,7},{8,8},{9,9... | collective-permute-start | bytes 884744 | tf_op jit(solution)/shard_map/ppermute | solution.py:272
  30.7 0.7 copy-start.7
  31.4 21.8 %collective-permute-start = (bf16[1040,128]{1,0:T(8,128)(2,1)}, bf16[1040,128]{1,0:T(8,128)(2,1)S(1)}, u32[]{:S(2)}, u32[]{:S(2)}) collective-permute-start(bf16[1040,128]{1,0:T(8,128)(2,1)} %get-tuple-element.11), channel_id=1, source_target_pairs={{16,0},{32,16},{48,32},{64,48},{80,64},{96,80},{112,96},{128,112},... | collective-permute-start | bytes 798728 | tf_op jit(solution)/shard_map/ppermute | solution.py:268
  38.8 6.9 %collective-permute-start.1 = (bf16[64,1024]{1,0:T(8,128)(2,1)S(1)}, bf16[64,1024]{1,0:T(8,128)(2,1)S(1)}, u32[]{:S(2)}, u32[]{:S(2)}) collective-permute-start(bf16[64,1024]{1,0:T(8,128)(2,1)S(1)} %copy-done.9), channel_id=1, source_target_pairs={{0,2},{2,4},{4,6},{6,8},{8,10},{10,12},{12,14},{14,0},{1,3},{3,5},... | collective-permute-start | bytes 393224 | tf_op jit(solution)/shard_map/ppermute | solution.py:230
  42.0 9.3 %collective-permute-start.2 = (bf16[64,1024]{1,0:T(8,128)(2,1)S(1)}, bf16[64,1024]{1,0:T(8,128)(2,1)S(1)}, u32[]{:S(2)}, u32[]{:S(2)}) collective-permute-start(bf16[64,1024]{1,0:T(8,128)(2,1)S(1)} %copy-done.9), channel_id=1, source_target_pairs={{2,0},{4,2},{6,4},{8,6},{10,8},{12,10},{14,12},{0,14},{3,1},{5,3},... | collective-permute-start | bytes 393224 | tf_op jit(solution)/shard_map/ppermute | solution.py:233
  45.7 18.7 %collective-permute-start.3 = (bf16[64,1024]{1,0:T(8,128)(2,1)S(1)}, bf16[64,1024]{1,0:T(8,128)(2,1)S(1)}, u32[]{:S(2)}, u32[]{:S(2)}) collective-permute-start(bf16[64,1024]{1,0:T(8,128)(2,1)S(1)} %collective-permute-done.1), channel_id=1, source_target_pairs={{0,2},{2,4},{4,6},{6,8},{8,10},{10,12},{12,14},{14,0},{1,3},{3,5},... | collective-permute-start | bytes 393224 | tf_op jit(solution)/shard_map/ppermute | solution.py:230
  51.3 16.3 %collective-permute-start.4 = (bf16[64,1024]{1,0:T(8,128)(2,1)S(1)}, bf16[64,1024]{1,0:T(8,128)(2,1)S(1)}, u32[]{:S(2)}, u32[]{:S(2)}) collective-permute-start(bf16[64,1024]{1,0:T(8,128)(2,1)S(1)} %collective-permute-done.2), channel_id=1, source_target_pairs={{2,0},{4,2},{6,4},{8,6},{10,8},{12,10},{14,12},{0,14},{3,1},{5,3},... | collective-permute-start | bytes 393224 | tf_op jit(solution)/shard_map/ppermute | solution.py:233
  54.2 45.6 %all-to-all-start = ((bf16[16,128,128]{2,1,0:T(8,128)(2,1)}), bf16[16,128,128]{2,1,0:T(8,128)(2,1)S(1)}, u32[]{:S(2)}, u32[]{:S(2)}) async-start(bf16[16,128,128]{2,1,0:T(8,128)(2,1)} %pad_maximum_fusion.xd_ref), calls=%async_computation | async-start | bytes 1048576 | tf_op jit(solution)/shard_map/all_to_all | solution.py:278
  64.4 23.1 %collective-permute-start.5 = (bf16[64,1024]{1,0:T(8,128)(2,1)S(1)}, bf16[64,1024]{1,0:T(8,128)(2,1)S(1)}, u32[]{:S(2)}, u32[]{:S(2)}) collective-permute-start(bf16[64,1024]{1,0:T(8,128)(2,1)S(1)} %collective-permute-done.3), channel_id=1, source_target_pairs={{0,2},{2,4},{4,6},{6,8},{8,10},{10,12},{12,14},{14,0},{1,3},{3,5},... | collective-permute-start | bytes 393224 | tf_op jit(solution)/shard_map/ppermute | solution.py:230
  67.7 22.0 %collective-permute-start.6 = (bf16[64,1024]{1,0:T(8,128)(2,1)S(1)}, bf16[64,1024]{1,0:T(8,128)(2,1)S(1)}, u32[]{:S(2)}, u32[]{:S(2)}) collective-permute-start(bf16[64,1024]{1,0:T(8,128)(2,1)S(1)} %collective-permute-done.4), channel_id=1, source_target_pairs={{2,0},{4,2},{6,4},{8,6},{10,8},{12,10},{14,12},{0,14},{3,1},{5,3},... | collective-permute-start | bytes 393224 | tf_op jit(solution)/shard_map/ppermute | solution.py:233
  71.0 28.8 %copy-start.2 = (bf16[320,1024]{1,0:T(8,128)(2,1)}, bf16[320,1024]{1,0:T(8,128)(2,1)S(1)}, u32[]{:S(2)}) copy-start(bf16[320,1024]{1,0:T(8,128)(2,1)S(1)} %constant_dynamic-update-slice_fusion.own_near) | copy-start | bytes 1966084
  71.0 28.8 %collective-permute-start.8 = (bf16[320,1024]{1,0:T(8,128)(2,1)S(1)}, bf16[320,1024]{1,0:T(8,128)(2,1)S(1)}, u32[]{:S(2)}, u32[]{:S(2)}) collective-permute-start(bf16[320,1024]{1,0:T(8,128)(2,1)S(1)} %constant_dynamic-update-slice_fusion.own_near), channel_id=1, source_target_pairs={{0,1},{1,0},{2,3},{3,2},{4,5},{5,4},{6,7},{7,6},{8,9},{9,8},{10,11... | collective-permute-start | bytes 1966088 | tf_op jit(solution)/shard_map/ppermute | solution.py:254
  87.5 7.6 %collective-permute-start.7 = (bf16[64,1024]{1,0:T(8,128)(2,1)S(1)}, bf16[64,1024]{1,0:T(8,128)(2,1)S(1)}, u32[]{:S(2)}, u32[]{:S(2)}) collective-permute-start(bf16[64,1024]{1,0:T(8,128)(2,1)S(1)} %collective-permute-done.5), channel_id=1, source_target_pairs={{0,2},{2,4},{4,6},{6,8},{8,10},{10,12},{12,14},{14,0},{1,3},{3,5},... | collective-permute-start | bytes 393224 | tf_op jit(solution)/shard_map/ppermute | solution.py:230
  95.0 4.7 %copy-start.3 = (bf16[192,1024]{1,0:T(8,128)(2,1)}, bf16[192,1024]{1,0:T(8,128)(2,1)S(1)}, u32[]{:S(2)}) copy-start(bf16[192,1024]{1,0:T(8,128)(2,1)S(1)} %constant_dynamic-update-slice_fusion.5.own_far) | copy-start | bytes 1179652
  95.1 4.7 %collective-permute-start.9 = (bf16[192,1024]{1,0:T(8,128)(2,1)S(1)}, bf16[192,1024]{1,0:T(8,128)(2,1)S(1)}, u32[]{:S(2)}, u32[]{:S(2)}) collective-permute-start(bf16[192,1024]{1,0:T(8,128)(2,1)S(1)} %constant_dynamic-update-slice_fusion.5.own_far), channel_id=1, source_target_pairs={{0,1},{1,0},{2,3},{3,2},{4,5},{5,4},{6,7},{7,6},{8,9},{9,8},{10,11... | collective-permute-start | bytes 1179656 | tf_op jit(solution)/shard_map/ppermute | solution.py:255
  99.7 0.8 copy-start.6
  99.7 1.0 copy-start.4
  99.7 1.1 copy-start.1
  105.9 39.4 %all-to-all-start.1 = ((bf16[16,64,640]{2,1,0:T(8,128)(2,1)}), bf16[16,64,640]{2,1,0:T(8,128)(2,1)S(1)}, u32[]{:S(2)}, u32[]{:S(2)}) async-start(bf16[16,64,640]{2,1,0:T(8,128)(2,1)} %get-tuple-element.13), calls=%async_computation.1 | async-start | bytes 2621440 | tf_op jit(solution)/shard_map/all_to_all | solution.py:289
  145.2 1.1 copy-start
  159.0 29.3 %collective-permute-start.11 = (bf16[1552,128]{1,0:T(8,128)(2,1)}, bf16[1552,128]{1,0:T(8,128)(2,1)S(1)}, u32[]{:S(2)}, u32[]{:S(2)}) collective-permute-start(bf16[1552,128]{1,0:T(8,128)(2,1)} %get-tuple-element.17), channel_id=1, source_target_pairs={{0,16},{16,32},{32,48},{48,64},{64,80},{80,96},{96,112},{112,128},... | collective-permute-start | bytes 1191944 | tf_op jit(solution)/shard_map/ppermute | solution.py:316
  188.3 0.8 copy-start.5
Sparse Core Ops, SparseCore 0:
  31.5 58.5 all-gather.2

commit v5 on v2

--- a/solution.py
+++ b/solution.py
@@ -19,6 +19,10 @@
 
 def dot(a, b):
     return jnp.dot(a, b, preferred_element_type=F32)
+
+
+def keep_in_vmem(value):
+    return pltpu.with_memory_space_constraint(value, pltpu.MemorySpace.VMEM)
 
 
 def pack_kernel(right_ref, initial_ref, blocks_ref, slots_ref, send_ref, keep_ref, own_ref):
@@ -33,13 +37,9 @@
             send_ref[2 * hours * i : 2 * hours * (i + 1), :] = pair
         else:
             keep_ref[i - half] = pair
-    base = 2 * hours * half
-    extra = slots_ref.shape[0]
-    send_ref[base : base + extra, :] = slots_ref[...]
+    send_ref[2 * hours * half :, :] = slots_ref[...]
     for k in range(width):
-        flipped = blocks_ref[k].T
-        own_ref[k * n : (k + 1) * n, :] = flipped
-        send_ref[base + extra + k * n : base + extra + (k + 1) * n, :] = flipped
+        own_ref[k * n : (k + 1) * n, :] = blocks_ref[k].T
 
 
 def temporal_kernel(core_ref, own_ref, other_ref, v_ref, w_ref, shift_ref):
@@ -232,7 +232,7 @@
     packed, keep, own_blocks = pl.pallas_call(
         pack_kernel,
         out_shape=(
-            jax.ShapeDtypeStruct((base + 16 + width * n, n), BF16),
+            jax.ShapeDtypeStruct((base + 16, n), BF16),
             jax.ShapeDtypeStruct((half, 2 * hours, n), BF16),
             jax.ShapeDtypeStruct((width * n, n), BF16),
         ),
@@ -241,8 +241,11 @@
         name="pack",
     )(right_side, initial, blocks[0], extra)
     shifted = lax.ppermute(packed, REGION, [((r + 1) % regions, r) for r in range(regions)])
-    window_row = jnp.where(lax.axis_index(TM) < half, shifted[base + 16 :], own_blocks)
-    window_blocks = lax.all_gather(window_row[None], TM, axis=0, tiled=True)
+    pairs = [
+        (((r + (t < half)) % regions) * tm_count + t, r * tm_count + t) for r in range(regions) for t in range(tm_count)
+    ]
+    row = lax.ppermute(own_blocks, REGION_TM, pairs)
+    window_blocks = lax.all_gather(row[None], TM, axis=0, tiled=True)
     xd = jnp.concatenate([shifted[:base].reshape(half, 2 * hours, n), keep], axis=0)
     window_slots = jnp.concatenate(
         [shifted[base : base + half, :slots].astype(jnp.int32), local_slots[half:]], axis=0
@@ -260,7 +263,7 @@
         in_specs=[SMEM, VMEM, VMEM, VMEM],
         out_specs=(VMEM, VMEM),
         name="temporal",
-    )(core, mine, theirs, arrived)
+    )(core, keep_in_vmem(mine), keep_in_vmem(theirs), keep_in_vmem(arrived))
     returned = lax.all_to_all(powers.reshape(tm_count, hours, 5 * n), TM, split_axis=0, concat_axis=0, tiled=True)
 
     low, high, gram, centre = pl.pallas_call(
@@ -286,7 +289,7 @@
             pltpu.SemaphoreType.DMA((rows,)),
         ],
         name="spatial",
-    )(window_slots, returned, xd, shift, window_blocks)
+    )(window_slots, keep_in_vmem(returned), keep_in_vmem(xd), shift, window_blocks)
 
     back = lax.ppermute(low, REGION, [(r, (r + 1) % regions) for r in range(regions)])
     over_tm = lax.all_to_all(gram, TM, split_axis=0, concat_axis=0, tiled=True)
@@ -301,7 +304,7 @@
         in_specs=[VMEM] * 5,
         out_specs=(VMEM, VMEM),
         name="finish",
-    )(over_region, initial, back, high, centre)
+    )(over_region, initial, keep_in_vmem(back), high, centre)
 
 
 def solution(mesh):

time: 209 us -> 195 us (0.933)
  blocking collectives: 50.9 us -> 29.2 us
  starting transfers between devices: 31.9 us -> 41 us
  waiting for transfers between devices: 81.2 us -> 85.1 us
  Pallas kernels: 22.6 us -> 20.3 us
  local copies, waits for them, and re-layouts: 5.38 us -> 3.27 us
    all_to_all x1 -> x0, blocking collectives: 21.6 us -> none  [steps(): arrived = lax.all_to_all(xd, TM, split_axis=0, concat_axis=0, tiled=True)]
    all_to_all x0 -> x1, waiting for transfers between devices: none -> 16.8 us  [steps(): arrived = lax.all_to_all(xd, TM, split_axis=0, concat_axis=0, tiled=True)]
    ppermute x0 -> x1, starting transfers between devices: none -> 13.7 us  [steps(): row = lax.ppermute(own_blocks, REGION_TM, pairs)]
    all_to_all x1, waiting for transfers between devices: 36.8 us -> 24 us  [steps(): lax.all_to_all(halves.reshape(tm_count, part, all_hours), TM, split_axis=...]
    ppermute x1, starting transfers between devices: 13.7 us -> 7.32 us  [steps(): lax.ppermute(packed, REGION, [((r + 1) % regions, r) for r in range(regio...]
    ppermute x1, waiting for transfers between devices: 11.7 us -> 5.63 us  [steps(): lax.ppermute(packed, REGION, [((r + 1) % regions, r) for r in range(regio...]
    ppermute x0 -> x1, waiting for transfers between devices: none -> 5.99 us  [steps(): row = lax.ppermute(own_blocks, REGION_TM, pairs)]
    all_to_all x0 -> x1, starting transfers between devices: none -> 4.93 us  [steps(): arrived = lax.all_to_all(xd, TM, split_axis=0, concat_axis=0, tiled=True)]
  transfers between devices with their start and end apart: 6 -> 8, of which waited for: 3 -> 5; matrix products, arithmetic and copies ran while one was open for 1% -> 1% of each run, Pallas kernels for 2% -> 2%
where the time goes in v5:
time: 195 us; the launch traced here: 194 us
  waiting for transfers between devices  85.1 us (44%)
  starting transfers between devices  41 us (21%)
  blocking collectives  29.2 us (15%)
  Pallas kernels  20.3 us (10%)
  between operations  14.1 us (7%)
  local copies, waits for them, and re-layouts  3.27 us (2%)
    all_to_all x1, waiting for transfers between devices, steps(): lax.all_to_all(powers.reshape(tm_count, hours, 5 * n), TM, split_axis=0,...  32.7 us
    all_to_all x1, waiting for transfers between devices, steps(): lax.all_to_all(halves.reshape(tm_count, part, all_hours), TM, split_axis=...  24 us
    all_to_all x1, blocking collectives, steps(): lax.all_to_all(spread, REGION, split_axis=0, concat_axis=0, tiled=True)  17.7 us
    all_to_all x1, waiting for transfers between devices, steps(): arrived = lax.all_to_all(xd, TM, split_axis=0, concat_axis=0, tiled=True)  16.8 us
    ppermute x1, starting transfers between devices, steps(): row = lax.ppermute(own_blocks, REGION_TM, pairs)  13.7 us
    pallas_call x1, Pallas kernels, steps(): pl.pallas_call(spatial_kernel, out_shape=(jax.ShapeDtypeStruct((3 * half...  12.2 us
    all_to_all x1, blocking collectives, steps(): over_tm = lax.all_to_all(gram, TM, split_axis=0, concat_axis=0, tiled=True)  11.6 us
    ppermute x1, starting transfers between devices, steps(): lax.ppermute(packed, REGION, [((r + 1) % regions, r) for r in range(regio...  7.32 us
  transfers between devices with their start and end apart: 8, of which 5 were waited for; matrix products, arithmetic and copies ran while one was open for 1% of the time, Pallas kernels for 2%

profile of v5, /device:TPU:1, one launch (start us, length us, event | category | flops | bytes accessed | tf_op | source)
XLA Modules:
  0.0 194.4 jit_solution(7113605270114771692)
XLA Ops:
  7.2 0.0 copy-start.2
  7.2 0.0 all-gather.3.cloned.1.call-start
  7.2 0.8 copy.7
  8.0 0.6 pad.4.slots_ref
  8.6 2.3 %pack.1 = (bf16[1040,128]{1,0:T(8,128)(2,1)}, bf16[8,128,128]{2,1,0:T(8,128)(2,1)}, bf16[1152,128]{1,0:T(8,128)(2,1)}) custom-call(f32[64,2048]{1,0:T(8,128)} %right_ref.1, f32[64,2048]{1,0:T(8,128)} %x_ref.1, bf16[9,128,128]{2,1,0:T(8,128)(2,1)} %bitcast.10, bf16[16,128]{1,0:T(8,128)(2,1)} %pad.4.slots_ref), custom_call_target="tpu_custom_call" | custom-call | tf_op jit(solution)/shard_map/pack/pallas_call | solution.py:232
  10.9 13.7 %collective-permute-start.2 = (bf16[1152,128]{1,0:T(8,128)(2,1)}, bf16[1152,128]{1,0:T(8,128)(2,1)S(1)}, u32[]{:S(2)}, u32[]{:S(2)}) collective-permute-start(bf16[1152,128]{1,0:T(8,128)(2,1)} %get-tuple-element.15), channel_id=1, source_target_pairs={{16,0},{17,1},{18,2},{19,3},{20,4},{21,5},{22,6},{23,7},{8,8},{9,9... | collective-permute-start | bytes 884744 | tf_op jit(solution)/shard_map/ppermute | solution.py:247
  24.6 6.0 %collective-permute-done.2 = bf16[1152,128]{1,0:T(8,128)(2,1)S(1)} collective-permute-done((bf16[1152,128]{1,0:T(8,128)(2,1)}, bf16[1152,128]{1,0:T(8,128)(2,1)S(1)}, u32[]{:S(2)}, u32[]{:S(2)}) %collective-permute-start.2) | collective-permute-done | bytes 294944 | tf_op jit(solution)/shard_map/ppermute | solution.py:247
  30.6 0.7 copy-done
  31.3 0.0 all-gather.3.cloned.1.call-update
  31.3 0.0 copy-done.2
  31.3 1.1 broadcast_in_dim.17
  32.4 6.5 %all-to-all-start = ((bf16[16,32,1024]{2,1,0:T(8,128)(2,1)}), bf16[16,32,1024]{2,1,0:T(8,128)(2,1)S(1)}, u32[]{:S(2)}, u32[]{:S(2)}) async-start(bf16[16,32,1024]{2,1,0:T(8,128)(2,1)} %bitcast.3), calls=%async_computation | async-start | bytes 2097152 | tf_op jit(solution)/shard_map/all_to_all | solution.py:229
  39.0 0.0 copy-done.3
  39.0 7.3 %collective-permute-start = (bf16[1040,128]{1,0:T(8,128)(2,1)S(1)}, bf16[1040,128]{1,0:T(8,128)(2,1)S(1)}, u32[]{:S(2)}, u32[]{:S(2)}) collective-permute-start(bf16[1040,128]{1,0:T(8,128)(2,1)S(1)} %copy-done.3), channel_id=1, source_target_pairs={{16,0},{32,16},{48,32},{64,48},{80,64},{96,80},{112,96},{128,112},... | collective-permute-start | bytes 798728 | tf_op jit(solution)/shard_map/ppermute | solution.py:243
  46.3 5.6 %collective-permute-done = bf16[1040,128]{1,0:T(8,128)(2,1)S(1)} collective-permute-done((bf16[1040,128]{1,0:T(8,128)(2,1)S(1)}, bf16[1040,128]{1,0:T(8,128)(2,1)S(1)}, u32[]{:S(2)}, u32[]{:S(2)}) %collective-permute-start) | collective-permute-done | bytes 266272 | tf_op jit(solution)/shard_map/ppermute | solution.py:243
  52.0 24.0 %all-to-all-done.own_ref = bf16[16,32,1024]{2,1,0:T(8,128)(2,1)S(1)} async-done(((bf16[16,32,1024]{2,1,0:T(8,128)(2,1)}), bf16[16,32,1024]{2,1,0:T(8,128)(2,1)S(1)}, u32[]{:S(2)}, u32[]{:S(2)}) %all-to-all-start) | async-done | bytes 1048608 | tf_op jit(solution)/shard_map/all_to_all | solution.py:229
  76.0 1.9 collective-permute-start.1
  77.9 0.0 copy-done.1
  77.9 0.8 pad_maximum_fusion.xd_ref
  78.8 4.9 %all-to-all-start.1 = ((bf16[16,128,128]{2,1,0:T(8,128)(2,1)}), bf16[16,128,128]{2,1,0:T(8,128)(2,1)S(1)}, u32[]{:S(2)}, u32[]{:S(2)}) async-start(bf16[16,128,128]{2,1,0:T(8,128)(2,1)} %pad_maximum_fusion.xd_ref), calls=%async_computation.1 | async-start | bytes 1048576 | tf_op jit(solution)/shard_map/all_to_all | solution.py:256
  83.7 16.8 %all-to-all-done.1.v_ref = bf16[16,128,128]{2,1,0:T(8,128)(2,1)S(1)} async-done(((bf16[16,128,128]{2,1,0:T(8,128)(2,1)}), bf16[16,128,128]{2,1,0:T(8,128)(2,1)S(1)}, u32[]{:S(2)}, u32[]{:S(2)}) %all-to-all-start.1) | async-done | bytes 524320 | tf_op jit(solution)/shard_map/all_to_all | solution.py:256
  100.5 0.0 collective-permute-done.1.other_ref
  100.5 3.0 %temporal.1 = (bf16[1024,640]{1,0:T(8,128)(2,1)}, f32[8,128]{1,0:T(8,128)}) custom-call(s32[1]{0:T(128)} %bitcast.1.core_ref, bf16[16,32,1024]{2,1,0:T(8,128)(2,1)S(1)} %all-to-all-done.own_ref, bf16[16,32,1024]{2,1,0:T(8,128)(2,1)S(1)} %collective-permute-done.1.other_ref, bf16[16,128,128]{2,1,0:T(8,128)(2,1)S(1)} %all-to-all-done.1.v_ref), custom_call_target="tpu_custom_call" | custom-call | tf_op jit(solution)/shard_map/temporal/pallas_call | solution.py:257
  103.5 4.7 %all-to-all-start.2 = ((bf16[16,64,640]{2,1,0:T(8,128)(2,1)}), bf16[16,64,640]{2,1,0:T(8,128)(2,1)S(1)}, u32[]{:S(2)}, u32[]{:S(2)}) async-start(bf16[16,64,640]{2,1,0:T(8,128)(2,1)} %bitcast.8), calls=%async_computation.2 | async-start | bytes 2621440 | tf_op jit(solution)/shard_map/all_to_all | solution.py:267
  108.2 0.6 pad_add_fusion.slots_ref
  108.8 32.7 %all-to-all-done.2.g_ref = bf16[16,64,640]{2,1,0:T(8,128)(2,1)S(1)} async-done(((bf16[16,64,640]{2,1,0:T(8,128)(2,1)}), bf16[16,64,640]{2,1,0:T(8,128)(2,1)S(1)}, u32[]{:S(2)}, u32[]{:S(2)}) %all-to-all-start.2) | async-done | bytes 1310752 | tf_op jit(solution)/shard_map/all_to_all | solution.py:267
  141.4 12.2 %spatial.1 = (bf16[1552,128]{1,0:T(8,128)(2,1)}, f32[3,8,64,128]{3,2,1,0:T(8,128)}, f32[16,8,128]{2,1,0:T(8,128)}, f32[8,128]{1,0:T(8,128)}) custom-call(s32[16,8]{1,0:T(8,128)} %pad_add_fusion.slots_ref, bf16[16,64,640]{2,1,0:T(8,128)(2,1)S(1)} %all-to-all-done.2.g_ref, bf16[16,128,128]{2,1,0:T(8,128)(2,1)} %pad_maximum_fusion.xd_ref, ...), custom_call_target="tpu_custom_call" | custom-call | tf_op jit(solution)/shard_map/spatial/pallas_call | solution.py:269
  153.7 1.9 collective-permute-start.3
  155.6 11.6 %all_to_all.25 = f32[16,8,128]{2,1,0:T(8,128)S(1)} all-to-all(f32[16,8,128]{2,1,0:T(8,128)} %get-tuple-element.16), channel_id=1, replica_groups=mesh['region_0'=4,'region_1'=8,'tm_0'=8,'tm_1'=2] {'tm_0','tm_1'}, dimensions={0} | all-to-all | bytes 131072 | tf_op jit(solution)/shard_map/all_to_all | solution.py:295
  167.2 17.7 %all_to_all.26.gram_ref = f32[32,8,128]{2,1,0:T(8,128)} all-to-all(f32[32,8,128]{2,1,0:T(8,128)S(1)} %broadcast_in_dim.19), channel_id=1, replica_groups=mesh['region_0'=4,'region_1'=8,'tm_0'=8,'tm_1'=2] {'region_0','region_1'}, dimensions={0} | all-to-all | bytes 262144 | tf_op jit(solution)/shard_map/all_to_all | solution.py:297
  184.9 0.0 collective-permute-done.3.low_ref
  184.9 2.7 %finish.1 = (f32[64,2048]{1,0:T(8,128)}, f32[64,2048]{1,0:T(8,128)}) custom-call(f32[32,8,128]{2,1,0:T(8,128)} %all_to_all.26.gram_ref, f32[64,2048]{1,0:T(8,128)} %x_ref.1, bf16[1552,128]{1,0:T(8,128)(2,1)S(1)} %collective-permute-done.3.low_ref, f32[3,8,64,128]{3,2,1,0:T(8,128)} %get-tuple-element.18.high_ref, f32[8,128]{1,0:T(8,128)} %get-tuple-element.19.centre_ref), custom_call_target="tpu_custom_call" | custom-call | tf_op jit(solution)/shard_map/finish/pallas_call | solution.py:298
  (10 shorter events, 0.1 us)
Async XLA Ops:
  7.2 24.1 %copy-start.2 = (bf16[64,1024]{1,0:T(8,128)(2,1)S(1)}, bf16[64,1024]{1,0:T(8,128)(2,1)}, u32[]{:S(2)}) copy-start(bf16[64,1024]{1,0:T(8,128)(2,1)} %param.9) | copy-start | bytes 393220
  7.2 134.2 %all-gather.3.cloned.1.call-start = ((), (), s32[]{:S(2)}) async-start(), calls=%async_computation.5 | async-start | bytes 5013504 | tf_op jit(solution)/shard_map/all_gather | solution.py:248
  10.9 19.7 %collective-permute-start.2 = (bf16[1152,128]{1,0:T(8,128)(2,1)}, bf16[1152,128]{1,0:T(8,128)(2,1)S(1)}, u32[]{:S(2)}, u32[]{:S(2)}) collective-permute-start(bf16[1152,128]{1,0:T(8,128)(2,1)} %get-tuple-element.15), channel_id=1, source_target_pairs={{16,0},{17,1},{18,2},{19,3},{20,4},{21,5},{22,6},{23,7},{8,8},{9,9... | collective-permute-start | bytes 884744 | tf_op jit(solution)/shard_map/ppermute | solution.py:247
  30.6 0.7 copy-start
  32.4 6.6 %copy-start.3 = (bf16[1040,128]{1,0:T(8,128)(2,1)S(1)}, bf16[1040,128]{1,0:T(8,128)(2,1)}, u32[]{:S(2)}) copy-start(bf16[1040,128]{1,0:T(8,128)(2,1)} %get-tuple-element.11) | copy-start | bytes 798724
  32.4 45.5 %copy-start.1 = (bf16[8,128,128]{2,1,0:T(8,128)(2,1)S(1)}, bf16[8,128,128]{2,1,0:T(8,128)(2,1)}, u32[]{:S(2)}) copy-start(bf16[8,128,128]{2,1,0:T(8,128)(2,1)} %get-tuple-element.12) | copy-start | bytes 786436
  32.4 43.6 %all-to-all-start = ((bf16[16,32,1024]{2,1,0:T(8,128)(2,1)}), bf16[16,32,1024]{2,1,0:T(8,128)(2,1)S(1)}, u32[]{:S(2)}, u32[]{:S(2)}) async-start(bf16[16,32,1024]{2,1,0:T(8,128)(2,1)} %bitcast.3), calls=%async_computation | async-start | bytes 2097152 | tf_op jit(solution)/shard_map/all_to_all | solution.py:229
  39.0 13.0 %collective-permute-start = (bf16[1040,128]{1,0:T(8,128)(2,1)S(1)}, bf16[1040,128]{1,0:T(8,128)(2,1)S(1)}, u32[]{:S(2)}, u32[]{:S(2)}) collective-permute-start(bf16[1040,128]{1,0:T(8,128)(2,1)S(1)} %copy-done.3), channel_id=1, source_target_pairs={{16,0},{32,16},{48,32},{64,48},{80,64},{96,80},{112,96},{128,112},... | collective-permute-start | bytes 798728 | tf_op jit(solution)/shard_map/ppermute | solution.py:243
  76.0 24.5 %collective-permute-start.1 = (bf16[16,32,1024]{2,1,0:T(8,128)(2,1)S(1)}, bf16[16,32,1024]{2,1,0:T(8,128)(2,1)S(1)}, u32[]{:S(2)}, u32[]{:S(2)}) collective-permute-start(bf16[16,32,1024]{2,1,0:T(8,128)(2,1)S(1)} %all-to-all-done.own_ref), channel_id=1, source_target_pairs={{0,1},{1,0},{2,3},{3,2},{4,5},{5,4},{6,7},{7,6},{8,9},{9,8},{10,11... | collective-permute-start | bytes 3145736 | tf_op jit(solution)/shard_map/ppermute | solution.py:254
  78.8 21.7 %all-to-all-start.1 = ((bf16[16,128,128]{2,1,0:T(8,128)(2,1)}), bf16[16,128,128]{2,1,0:T(8,128)(2,1)S(1)}, u32[]{:S(2)}, u32[]{:S(2)}) async-start(bf16[16,128,128]{2,1,0:T(8,128)(2,1)} %pad_maximum_fusion.xd_ref), calls=%async_computation.1 | async-start | bytes 1048576 | tf_op jit(solution)/shard_map/all_to_all | solution.py:256
  103.5 37.9 %all-to-all-start.2 = ((bf16[16,64,640]{2,1,0:T(8,128)(2,1)}), bf16[16,64,640]{2,1,0:T(8,128)(2,1)S(1)}, u32[]{:S(2)}, u32[]{:S(2)}) async-start(bf16[16,64,640]{2,1,0:T(8,128)(2,1)} %bitcast.8), calls=%async_computation.2 | async-start | bytes 2621440 | tf_op jit(solution)/shard_map/all_to_all | solution.py:267
  153.7 31.2 %collective-permute-start.3 = (bf16[1552,128]{1,0:T(8,128)(2,1)}, bf16[1552,128]{1,0:T(8,128)(2,1)S(1)}, u32[]{:S(2)}, u32[]{:S(2)}) collective-permute-start(bf16[1552,128]{1,0:T(8,128)(2,1)} %get-tuple-element.17), channel_id=1, source_target_pairs={{0,16},{16,32},{32,48},{48,64},{64,80},{80,96},{96,112},{112,128},... | collective-permute-start | bytes 1191944 | tf_op jit(solution)/shard_map/ppermute | solution.py:294
Sparse Core Ops, SparseCore 0:
  31.4 65.3 all-gather.2

commit v6 on v5

--- a/solution.py
+++ b/solution.py
@@ -12,7 +12,7 @@
 REGION_TM = ("region_0", "region_1", "tm_0", "tm_1")
 F32 = jnp.float32
 BF16 = jnp.bfloat16
-UNROLL = 2
+UNROLL = 8
 VMEM = pl.BlockSpec(memory_space=pltpu.MemorySpace.VMEM)
 SMEM = pl.BlockSpec(memory_space=pltpu.MemorySpace.SMEM)
 
@@ -25,8 +25,7 @@
     return pltpu.with_memory_space_constraint(value, pltpu.MemorySpace.VMEM)
 
 
-def pack_kernel(right_ref, initial_ref, blocks_ref, slots_ref, send_ref, keep_ref, own_ref):
-    hours = right_ref.shape[0]
+def pack_kernel(right_ref, initial_ref, blocks_ref, send_ref, keep_ref, own_ref):
     width, n = blocks_ref.shape[0], blocks_ref.shape[1]
     half = keep_ref.shape[0]
     for i in range(2 * half):
@@ -34,40 +33,52 @@
         x = initial_ref[:, lanes]
         pair = jnp.concatenate([x.astype(BF16), (right_ref[:, lanes] - x).astype(BF16)], axis=0)
         if i < half:
-            send_ref[2 * hours * i : 2 * hours * (i + 1), :] = pair
+            send_ref[i] = pair
         else:
             keep_ref[i - half] = pair
-    send_ref[2 * hours * half :, :] = slots_ref[...]
     for k in range(width):
         own_ref[k * n : (k + 1) * n, :] = blocks_ref[k].T
 
 
-def temporal_kernel(core_ref, own_ref, other_ref, v_ref, w_ref, shift_ref):
-    groups, part, hours = own_ref.shape
+def spread_kernel(chip_ref, rows_ref, out_ref):
+    groups, part, wide = out_ref.shape
+    chips = groups // 2
+    n = rows_ref.shape[1] // chips
+    for k in range(wide // n):
+        start = pl.multiple_of(lax.rem(chip_ref[0] + k, chips) * n, n)
+        for core in range(2):
+            tile = rows_ref[core * part : (core + 1) * part, pl.ds(start, n)]
+            for chip in range(chips):
+                out_ref[2 * chip + core, :, k * n : (k + 1) * n] = tile
+
+
+def temporal_kernel(core_ref, own_ref, other_ref, v_ref, w_ref, shift_ref, c_buf):
+    groups, part, wide = own_ref.shape
+    chips = groups // 2
     n = v_ref.shape[2]
+    hours = chips * n
     core = core_ref[0]
-    row = lax.broadcasted_iota(jnp.int32, (part, n), 0)
-    lane = lax.broadcasted_iota(jnp.int32, (part, n), 1)
-    diagonal = jnp.zeros((part, n), F32)
     for t in range(groups):
-        first_row = 2 * part * t
-        lanes = slice(first_row // n * n, first_row // n * n + n)
         for ref, which in ((own_ref, core), (other_ref, 1 - core)):
-            at = row + (first_row % n + part * which)
-            diagonal = diagonal + jnp.where(lane == at, ref[t, :, lanes].astype(F32), 0.0)
+            rows = pl.ds(pl.multiple_of(2 * part * t + part * which, part), part)
+            for k in range(wide // n):
+                block = (t // 2 + k) % chips
+                c_buf[rows, block * n : (block + 1) * n] = ref[t, :, k * n : (k + 1) * n]
+    for i in range(chips):
+        for k in range(1, chips // 2):
+            j = (i + k) % chips
+            c_buf[j * n : (j + 1) * n, i * n : (i + 1) * n] = c_buf[i * n : (i + 1) * n, j * n : (j + 1) * n].T
+    eye = lax.broadcasted_iota(jnp.int32, (n, n), 0) == lax.broadcasted_iota(jnp.int32, (n, n), 1)
+    diagonal = jnp.zeros((n, n), F32)
+    for i in range(chips):
+        tile = c_buf[i * n : (i + 1) * n, i * n : (i + 1) * n].astype(F32)
+        diagonal = diagonal + jnp.where(eye, tile, 0.0)
     c0 = jnp.sum(diagonal, axis=(0, 1), keepdims=True) / hours
     shift_ref[...] = jnp.broadcast_to(c0, shift_ref.shape)
 
-    mine = own_ref[...].reshape(groups * part, hours)
-    theirs = other_ref[...].reshape(groups * part, hours)
-
     def power(v, base):
-        wide = v.shape[1]
-        by_core = jnp.stack([dot(mine, v).reshape(groups, part, wide), dot(theirs, v).reshape(groups, part, wide)], axis=1)
-        swapped = jnp.stack([by_core[:, 1], by_core[:, 0]], axis=1)
-        full = jnp.where(core == 0, by_core, swapped).reshape(hours, wide)
-        out = (full - c0 * v.astype(F32)).astype(BF16)
-        w_ref[:, base : base + wide] = out
+        out = (dot(c_buf[...], v) - c0 * v.astype(F32)).astype(BF16)
+        w_ref[:, base : base + v.shape[1]] = out
         return out
 
     v = v_ref[...]
@@ -216,43 +227,46 @@
     width = blocks.shape[1]
     rows = neighbour_blocks.shape[0]
     half = rows // 2
-    slots = neighbour_blocks.shape[1]
     tm_count = lax.axis_size(TM)
     regions = lax.axis_size(REGION)
     all_hours = temporal_cov.shape[1]
     part = hours // 2
 
-    local_slots = lax.rem(neighbour_blocks, rows)
-    extra = jnp.pad(local_slots[:half].astype(BF16), ((0, 16 - half), (0, n - slots)))
-    base = 2 * hours * half
-    halves = jnp.broadcast_to(temporal_cov.reshape(1, 2, part, all_hours), (tm_count // 2, 2, part, all_hours))
-    mine = lax.all_to_all(
-        halves.reshape(tm_count, part, all_hours), TM, split_axis=0, concat_axis=0, tiled=True
-    )
+    core = lax.axis_index(TM[1]).astype(jnp.int32).reshape(1)
+    chip = lax.axis_index(TM[0]).astype(jnp.int32).reshape(1)
+    chips = tm_count // 2
+    spread_rows = pl.pallas_call(
+        spread_kernel,
+        out_shape=jax.ShapeDtypeStruct((tm_count, part, (chips // 2 + 1) * (all_hours // chips)), BF16),
+        in_specs=[SMEM, VMEM],
+        out_specs=VMEM,
+        name="spread",
+    )(chip, temporal_cov)
+    mine = lax.all_to_all(spread_rows, TM, split_axis=0, concat_axis=0, tiled=True)
     packed, keep, own_blocks = pl.pallas_call(
         pack_kernel,
         out_shape=(
-            jax.ShapeDtypeStruct((base + 16, n), BF16),
+            jax.ShapeDtypeStruct((half, 2 * hours, n), BF16),
             jax.ShapeDtypeStruct((half, 2 * hours, n), BF16),
             jax.ShapeDtypeStruct((width * n, n), BF16),
         ),
-        in_specs=[VMEM] * 4,
+        in_specs=[VMEM] * 3,
         out_specs=(VMEM,) * 3,
         name="pack",
-    )(right_side, initial, blocks[0], extra)
-    shifted = lax.ppermute(packed, REGION, [((r + 1) % regions, r) for r in range(regions)])
+    )(right_side, initial, blocks[0])
+    from_next = [((r + 1) % regions, r) for r in range(regions)]
+    shifted = lax.ppermute(packed, REGION, from_next)
     pairs = [
         (((r + (t < half)) % regions) * tm_count + t, r * tm_count + t) for r in range(regions) for t in range(tm_count)
     ]
     row = lax.ppermute(own_blocks, REGION_TM, pairs)
     window_blocks = lax.all_gather(row[None], TM, axis=0, tiled=True)
-    xd = jnp.concatenate([shifted[:base].reshape(half, 2 * hours, n), keep], axis=0)
-    window_slots = jnp.concatenate(
-        [shifted[base : base + half, :slots].astype(jnp.int32), local_slots[half:]], axis=0
-    )
+    xd = jnp.concatenate([shifted, keep], axis=0)
+    local_slots = lax.rem(neighbour_blocks, rows)
+    next_slots = lax.ppermute(local_slots[:half], REGION, from_next)
+    window_slots = jnp.concatenate([next_slots, local_slots[half:]], axis=0)
 
     theirs = lax.ppermute(mine, TM[1], [(0, 1), (1, 0)])
-    core = lax.axis_index(TM[1]).astype(jnp.int32).reshape(1)
     arrived = lax.all_to_all(xd, TM, split_axis=0, concat_axis=0, tiled=True)
     powers, shift = pl.pallas_call(
         temporal_kernel,
@@ -262,6 +276,7 @@
         ),
         in_specs=[SMEM, VMEM, VMEM, VMEM],
         out_specs=(VMEM, VMEM),
+        scratch_shapes=[pltpu.VMEM((all_hours, all_hours), BF16)],
         name="temporal",
     )(core, keep_in_vmem(mine), keep_in_vmem(theirs), keep_in_vmem(arrived))
     returned = lax.all_to_all(powers.reshape(tm_count, hours, 5 * n), TM, split_axis=0, concat_axis=0, tiled=True)
@@ -304,7 +319,7 @@
         in_specs=[VMEM] * 5,
         out_specs=(VMEM, VMEM),
         name="finish",
-    )(over_region, initial, keep_in_vmem(back), high, centre)
+    )(over_region, keep_in_vmem(initial), keep_in_vmem(back), high, centre)
 
 
 def solution(mesh):

time: 195 us -> 183 us (0.938)
  waiting for transfers between devices: 85.1 us -> 67.8 us
  starting transfers between devices: 41 us -> 46.8 us
    all_to_all x1, waiting for transfers between devices: 24 us -> 11.1 us  [steps(): lax.all_to_all(spread_rows, TM, split_axis=0, concat_axis=0, tiled=True)]
    all_to_all x1, waiting for transfers between devices: 32.7 us -> 24.5 us  [steps(): lax.all_to_all(powers.reshape(tm_count, hours, 5 * n), TM, split_axis=0,...]
    ppermute x1 -> x2, starting transfers between devices: 7.32 us -> 14.6 us  [the longest x1 7.32 us: steps(): shifted = lax.ppermute(packed, REGION, from_next)]
    all_to_all x1, waiting for transfers between devices: 16.8 us -> 19.9 us  [steps(): arrived = lax.all_to_all(xd, TM, split_axis=0, concat_axis=0, tiled=True)]
    pallas_call x1 -> x2, Pallas kernels: 2.26 us -> 4.15 us  [the longest x1 2.26 us: steps(): pl.pallas_call(pack_kernel, out_shape=(jax.ShapeDtypeStruct((half, 2 * ho...]
    ppermute x1 -> x2, waiting for transfers between devices: 5.63 us -> 6.27 us  [the longest x1 5.54 us: steps(): shifted = lax.ppermute(packed, REGION, from_next)]
  transfers between devices with their start and end apart: 8 -> 9, of which waited for: 5 -> 6; matrix products, arithmetic and copies ran while one was open for 1% -> 1% of each run, Pallas kernels for 2% -> 3%
where the time goes in v6:
time: 183 us; the launch traced here: 182 us
  waiting for transfers between devices  67.8 us (37%)
  starting transfers between devices  46.8 us (26%)
  blocking collectives  29.1 us (16%)
  Pallas kernels  21.1 us (12%)
  between operations  14.1 us (8%)
  local copies, waits for them, and re-layouts  2.26 us (1%)
    all_to_all x1, waiting for transfers between devices, steps(): lax.all_to_all(powers.reshape(tm_count, hours, 5 * n), TM, split_axis=0,...  24.5 us
    all_to_all x1, waiting for transfers between devices, steps(): arrived = lax.all_to_all(xd, TM, split_axis=0, concat_axis=0, tiled=True)  19.9 us
    all_to_all x1, blocking collectives, steps(): lax.all_to_all(spread, REGION, split_axis=0, concat_axis=0, tiled=True)  17.6 us
    ppermute x1, starting transfers between devices, steps(): row = lax.ppermute(own_blocks, REGION_TM, pairs)  13.8 us
    all_to_all x1, blocking collectives, steps(): over_tm = lax.all_to_all(gram, TM, split_axis=0, concat_axis=0, tiled=True)  11.6 us
    all_to_all x1, waiting for transfers between devices, steps(): lax.all_to_all(spread_rows, TM, split_axis=0, concat_axis=0, tiled=True)  11.1 us
    pallas_call x1, Pallas kernels, steps(): pl.pallas_call(spatial_kernel, out_shape=(jax.ShapeDtypeStruct((3 * half...  10.4 us
    ppermute x1, starting transfers between devices, steps(): shifted = lax.ppermute(packed, REGION, from_next)  7.32 us
  transfers between devices with their start and end apart: 9, of which 6 were waited for; matrix products, arithmetic and copies ran while one was open for 1% of the time, Pallas kernels for 3%

profile of v6, /device:TPU:1, one launch (start us, length us, event | category | flops | bytes accessed | tf_op | source)
XLA Modules:
  0.0 181.9 jit_solution(11715860031119055167)
XLA Ops:
  7.2 0.0 all-gather.3.cloned.1.call-start
  7.2 2.3 %pack.1 = (bf16[8,128,128]{2,1,0:T(8,128)(2,1)}, bf16[8,128,128]{2,1,0:T(8,128)(2,1)}, bf16[1152,128]{1,0:T(8,128)(2,1)}) custom-call(f32[64,2048]{1,0:T(8,128)} %right_ref.1, f32[64,2048]{1,0:T(8,128)} %x_ref.1, bf16[9,128,128]{2,1,0:T(8,128)(2,1)} %bitcast.7), custom_call_target="tpu_custom_call" | custom-call | tf_op jit(solution)/shard_map/pack/pallas_call | solution.py:246
  9.5 13.8 %collective-permute-start.3 = (bf16[1152,128]{1,0:T(8,128)(2,1)}, bf16[1152,128]{1,0:T(8,128)(2,1)S(1)}, u32[]{:S(2)}, u32[]{:S(2)}) collective-permute-start(bf16[1152,128]{1,0:T(8,128)(2,1)} %get-tuple-element.15), channel_id=1, source_target_pairs={{16,0},{17,1},{18,2},{19,3},{20,4},{21,5},{22,6},{23,7},{8,8},{9,9... | collective-permute-start | bytes 884744 | tf_op jit(solution)/shard_map/ppermute | solution.py:262
  23.3 6.0 %collective-permute-done.3 = bf16[1152,128]{1,0:T(8,128)(2,1)S(1)} collective-permute-done((bf16[1152,128]{1,0:T(8,128)(2,1)}, bf16[1152,128]{1,0:T(8,128)(2,1)S(1)}, u32[]{:S(2)}, u32[]{:S(2)}) %collective-permute-start.3) | collective-permute-done | bytes 294944 | tf_op jit(solution)/shard_map/ppermute | solution.py:262
  29.3 0.7 copy-done.1
  30.0 0.0 all-gather.3.cloned.1.call-update
  30.0 0.0 copy-start.2
  30.0 1.9 %spread.1 = bf16[16,32,640]{2,1,0:T(8,128)(2,1)} custom-call(s32[1]{0:T(128)} %bitcast.1.chip_ref, bf16[64,1024]{1,0:T(8,128)(2,1)} %rows_ref.1), custom_call_target="tpu_custom_call" | custom-call | tf_op jit(solution)/shard_map/spread/pallas_call | solution.py:238
  31.9 6.4 %all-to-all-start = ((bf16[16,32,640]{2,1,0:T(8,128)(2,1)}), bf16[16,32,640]{2,1,0:T(8,128)(2,1)S(1)}, u32[]{:S(2)}, u32[]{:S(2)}) async-start(bf16[16,32,640]{2,1,0:T(8,128)(2,1)} %spread.1), calls=%async_computation | async-start | bytes 1310720 | tf_op jit(solution)/shard_map/all_to_all | solution.py:245
  38.3 0.0 copy-done.4
  38.3 7.3 %collective-permute-start.2 = (bf16[8,128,128]{2,1,0:T(8,128)(2,1)S(1)}, bf16[8,128,128]{2,1,0:T(8,128)(2,1)S(1)}, u32[]{:S(2)}, u32[]{:S(2)}) collective-permute-start(bf16[8,128,128]{2,1,0:T(8,128)(2,1)S(1)} %copy-done.4), channel_id=1, source_target_pairs={{16,0},{32,16},{48,32},{64,48},{80,64},{96,80},{112,96},{128,112},... | collective-permute-start | bytes 786440 | tf_op jit(solution)/shard_map/ppermute | solution.py:258
  45.7 5.5 %collective-permute-done.2 = bf16[8,128,128]{2,1,0:T(8,128)(2,1)S(1)} collective-permute-done((bf16[8,128,128]{2,1,0:T(8,128)(2,1)S(1)}, bf16[8,128,128]{2,1,0:T(8,128)(2,1)S(1)}, u32[]{:S(2)}, u32[]{:S(2)}) %collective-permute-start.2) | collective-permute-done | bytes 262176 | tf_op jit(solution)/shard_map/ppermute | solution.py:258
  51.2 0.7 constant_dynamic-update-slice_fusion.1
  51.9 0.7 constant_dynamic-update-slice_fusion.xd_ref
  52.6 11.1 %all-to-all-done.own_ref = bf16[16,32,640]{2,1,0:T(8,128)(2,1)S(1)} async-done(((bf16[16,32,640]{2,1,0:T(8,128)(2,1)}), bf16[16,32,640]{2,1,0:T(8,128)(2,1)S(1)}, u32[]{:S(2)}, u32[]{:S(2)}) %all-to-all-start) | async-done | bytes 655392 | tf_op jit(solution)/shard_map/all_to_all | solution.py:245
  63.7 4.0 %all-to-all-start.1 = ((bf16[16,128,128]{2,1,0:T(8,128)(2,1)}), bf16[16,128,128]{2,1,0:T(8,128)(2,1)S(1)}, u32[]{:S(2)}, u32[]{:S(2)}) async-start(bf16[16,128,128]{2,1,0:T(8,128)(2,1)} %constant_dynamic-update-slice_fusion.xd_ref), calls=%async_computation.1 | async-start | bytes 1048576 | tf_op jit(solution)/shard_map/all_to_all | solution.py:270
  67.7 2.0 %collective-permute-start.1 = (bf16[16,32,640]{2,1,0:T(8,128)(2,1)S(1)}, bf16[16,32,640]{2,1,0:T(8,128)(2,1)S(1)}, u32[]{:S(2)}, u32[]{:S(2)}) collective-permute-start(bf16[16,32,640]{2,1,0:T(8,128)(2,1)S(1)} %all-to-all-done.own_ref), channel_id=1, source_target_pairs={{0,1},{1,0},{2,3},{3,2},{4,5},{5,4},{6,7},{7,6},{8,9},{9,8},{10,11... | collective-permute-start | bytes 1966088 | tf_op jit(solution)/shard_map/ppermute | solution.py:269
  69.7 19.9 %all-to-all-done.1.v_ref = bf16[16,128,128]{2,1,0:T(8,128)(2,1)S(1)} async-done(((bf16[16,128,128]{2,1,0:T(8,128)(2,1)}), bf16[16,128,128]{2,1,0:T(8,128)(2,1)S(1)}, u32[]{:S(2)}, u32[]{:S(2)}) %all-to-all-start.1) | async-done | bytes 524320 | tf_op jit(solution)/shard_map/all_to_all | solution.py:270
  89.6 0.0 collective-permute-done.1.other_ref
  89.6 4.0 %temporal.1 = (bf16[1024,640]{1,0:T(8,128)(2,1)}, f32[8,128]{1,0:T(8,128)}) custom-call(s32[1]{0:T(128)} %bitcast.core_ref, bf16[16,32,640]{2,1,0:T(8,128)(2,1)S(1)} %all-to-all-done.own_ref, bf16[16,32,640]{2,1,0:T(8,128)(2,1)S(1)} %collective-permute-done.1.other_ref, bf16[16,128,128]{2,1,0:T(8,128)(2,1)S(1)} %all-to-all-done.1.v_ref), custom_call_target="tpu_custom_call" | custom-call | tf_op jit(solution)/shard_map/temporal/pallas_call | solution.py:271
  93.7 4.0 %all-to-all-start.2 = ((bf16[16,64,640]{2,1,0:T(8,128)(2,1)}), bf16[16,64,640]{2,1,0:T(8,128)(2,1)S(1)}, u32[]{:S(2)}, u32[]{:S(2)}) async-start(bf16[16,64,640]{2,1,0:T(8,128)(2,1)} %bitcast.6), calls=%async_computation.2 | async-start | bytes 2621440 | tf_op jit(solution)/shard_map/all_to_all | solution.py:282
  97.7 0.1 copy.7
  97.8 7.3 %collective-permute-start = (s32[8,8]{1,0:T(8,128)S(1)}, s32[8,8]{1,0:T(8,128)S(1)}, u32[]{:S(2)}, u32[]{:S(2)}) collective-permute-start(s32[8,8]{1,0:T(8,128)S(1)} %get-tuple-element.20), channel_id=1, source_target_pairs={{16,0},{32,16},{48,32},{64,48},{80,64},{96,80},{112,96},{128,112},... | collective-permute-start | bytes 776 | tf_op jit(solution)/shard_map/ppermute | solution.py:266
  105.1 0.7 collective-permute-done
  105.8 0.6 pad_add_fusion.slots_ref
  106.4 24.5 %all-to-all-done.2.g_ref = bf16[16,64,640]{2,1,0:T(8,128)(2,1)S(1)} async-done(((bf16[16,64,640]{2,1,0:T(8,128)(2,1)}), bf16[16,64,640]{2,1,0:T(8,128)(2,1)S(1)}, u32[]{:S(2)}, u32[]{:S(2)}) %all-to-all-start.2) | async-done | bytes 1310752 | tf_op jit(solution)/shard_map/all_to_all | solution.py:282
  131.0 10.4 %spatial.1 = (bf16[1552,128]{1,0:T(8,128)(2,1)}, f32[3,8,64,128]{3,2,1,0:T(8,128)}, f32[16,8,128]{2,1,0:T(8,128)}, f32[8,128]{1,0:T(8,128)}) custom-call(s32[16,8]{1,0:T(8,128)} %pad_add_fusion.slots_ref, bf16[16,64,640]{2,1,0:T(8,128)(2,1)S(1)} %all-to-all-done.2.g_ref, bf16[16,128,128]{2,1,0:T(8,128)(2,1)} %constant_dynamic-update-slice_fusion.xd_ref, ...), custom_call_target="tpu_custom_call" | custom-call | tf_op jit(solution)/shard_map/spatial/pallas_call | solution.py:284
  141.4 1.9 %collective-permute-start.4 = (bf16[1552,128]{1,0:T(8,128)(2,1)}, bf16[1552,128]{1,0:T(8,128)(2,1)S(1)}, u32[]{:S(2)}, u32[]{:S(2)}) collective-permute-start(bf16[1552,128]{1,0:T(8,128)(2,1)} %get-tuple-element.17), channel_id=1, source_target_pairs={{0,16},{16,32},{32,48},{48,64},{64,80},{80,96},{96,112},{112,128},... | collective-permute-start | bytes 1191944 | tf_op jit(solution)/shard_map/ppermute | solution.py:309
  143.3 11.6 %all_to_all.25 = f32[16,8,128]{2,1,0:T(8,128)S(1)} all-to-all(f32[16,8,128]{2,1,0:T(8,128)} %get-tuple-element.16), channel_id=1, replica_groups=mesh['region_0'=4,'region_1'=8,'tm_0'=8,'tm_1'=2] {'tm_0','tm_1'}, dimensions={0} | all-to-all | bytes 131072 | tf_op jit(solution)/shard_map/all_to_all | solution.py:310
  154.9 17.6 %all_to_all.26.gram_ref = f32[32,8,128]{2,1,0:T(8,128)} all-to-all(f32[32,8,128]{2,1,0:T(8,128)S(1)} %broadcast_in_dim.10), channel_id=1, replica_groups=mesh['region_0'=4,'region_1'=8,'tm_0'=8,'tm_1'=2] {'region_0','region_1'}, dimensions={0} | all-to-all | bytes 262144 | tf_op jit(solution)/shard_map/all_to_all | solution.py:312
  172.5 0.0 collective-permute-done.4.low_ref
  172.5 2.5 %finish.1 = (f32[64,2048]{1,0:T(8,128)}, f32[64,2048]{1,0:T(8,128)}) custom-call(f32[32,8,128]{2,1,0:T(8,128)} %all_to_all.26.gram_ref, f32[64,2048]{1,0:T(8,128)S(1)} %copy-done, bf16[1552,128]{1,0:T(8,128)(2,1)S(1)} %collective-permute-done.4.low_ref, f32[3,8,64,128]{3,2,1,0:T(8,128)} %get-tuple-element.18.high_ref, f32[8,128]{1,0:T(8,128)} %get-tuple-element.19.centre_ref), custom_call_target="tpu_custom_call" | custom-call | tf_op jit(solution)/shard_map/finish/pallas_call | solution.py:313
  (12 shorter events, 0.1 us)
Async XLA Ops:
  7.2 123.8 %all-gather.3.cloned.1.call-start = ((), (), s32[]{:S(2)}) async-start(), calls=%async_computation.5 | async-start | bytes 5013504 | tf_op jit(solution)/shard_map/all_gather | solution.py:263
  9.5 28.9 %copy-start.4 = (bf16[8,128,128]{2,1,0:T(8,128)(2,1)S(1)}, bf16[8,128,128]{2,1,0:T(8,128)(2,1)}, u32[]{:S(2)}) copy-start(bf16[8,128,128]{2,1,0:T(8,128)(2,1)} %get-tuple-element.11) | copy-start | bytes 786436
  9.5 19.8 %collective-permute-start.3 = (bf16[1152,128]{1,0:T(8,128)(2,1)}, bf16[1152,128]{1,0:T(8,128)(2,1)S(1)}, u32[]{:S(2)}, u32[]{:S(2)}) collective-permute-start(bf16[1152,128]{1,0:T(8,128)(2,1)} %get-tuple-element.15), channel_id=1, source_target_pairs={{16,0},{17,1},{18,2},{19,3},{20,4},{21,5},{22,6},{23,7},{8,8},{9,9... | collective-permute-start | bytes 884744 | tf_op jit(solution)/shard_map/ppermute | solution.py:262
  29.3 0.7 copy-start.1
  30.0 21.9 %copy-start.2 = (bf16[8,128,128]{2,1,0:T(8,128)(2,1)S(1)}, bf16[8,128,128]{2,1,0:T(8,128)(2,1)}, u32[]{:S(2)}) copy-start(bf16[8,128,128]{2,1,0:T(8,128)(2,1)} %get-tuple-element.12) | copy-start | bytes 786436
  31.9 31.8 %all-to-all-start = ((bf16[16,32,640]{2,1,0:T(8,128)(2,1)}), bf16[16,32,640]{2,1,0:T(8,128)(2,1)S(1)}, u32[]{:S(2)}, u32[]{:S(2)}) async-start(bf16[16,32,640]{2,1,0:T(8,128)(2,1)} %spread.1), calls=%async_computation | async-start | bytes 1310720 | tf_op jit(solution)/shard_map/all_to_all | solution.py:245
  38.3 12.9 %collective-permute-start.2 = (bf16[8,128,128]{2,1,0:T(8,128)(2,1)S(1)}, bf16[8,128,128]{2,1,0:T(8,128)(2,1)S(1)}, u32[]{:S(2)}, u32[]{:S(2)}) collective-permute-start(bf16[8,128,128]{2,1,0:T(8,128)(2,1)S(1)} %copy-done.4), channel_id=1, source_target_pairs={{16,0},{32,16},{48,32},{64,48},{80,64},{96,80},{112,96},{128,112},... | collective-permute-start | bytes 786440 | tf_op jit(solution)/shard_map/ppermute | solution.py:258
  63.7 25.9 %all-to-all-start.1 = ((bf16[16,128,128]{2,1,0:T(8,128)(2,1)}), bf16[16,128,128]{2,1,0:T(8,128)(2,1)S(1)}, u32[]{:S(2)}, u32[]{:S(2)}) async-start(bf16[16,128,128]{2,1,0:T(8,128)(2,1)} %constant_dynamic-update-slice_fusion.xd_ref), calls=%async_computation.1 | async-start | bytes 1048576 | tf_op jit(solution)/shard_map/all_to_all | solution.py:270
  67.7 21.9 %collective-permute-start.1 = (bf16[16,32,640]{2,1,0:T(8,128)(2,1)S(1)}, bf16[16,32,640]{2,1,0:T(8,128)(2,1)S(1)}, u32[]{:S(2)}, u32[]{:S(2)}) collective-permute-start(bf16[16,32,640]{2,1,0:T(8,128)(2,1)S(1)} %all-to-all-done.own_ref), channel_id=1, source_target_pairs={{0,1},{1,0},{2,3},{3,2},{4,5},{5,4},{6,7},{7,6},{8,9},{9,8},{10,11... | collective-permute-start | bytes 1966088 | tf_op jit(solution)/shard_map/ppermute | solution.py:269
  93.7 4.0 %copy-start.3 = (s32[16,8]{0,1:T(8,128)S(1)}, s32[16,8]{0,1:T(8,128)}, u32[]{:S(2)}) copy-start(s32[16,8]{0,1:T(8,128)} %param.8) | copy-start | bytes 1540
  93.7 37.3 %all-to-all-start.2 = ((bf16[16,64,640]{2,1,0:T(8,128)(2,1)}), bf16[16,64,640]{2,1,0:T(8,128)(2,1)S(1)}, u32[]{:S(2)}, u32[]{:S(2)}) async-start(bf16[16,64,640]{2,1,0:T(8,128)(2,1)} %bitcast.6), calls=%async_computation.2 | async-start | bytes 2621440 | tf_op jit(solution)/shard_map/all_to_all | solution.py:282
  97.8 8.0 %collective-permute-start = (s32[8,8]{1,0:T(8,128)S(1)}, s32[8,8]{1,0:T(8,128)S(1)}, u32[]{:S(2)}, u32[]{:S(2)}) collective-permute-start(s32[8,8]{1,0:T(8,128)S(1)} %get-tuple-element.20), channel_id=1, source_target_pairs={{16,0},{32,16},{48,32},{64,48},{80,64},{96,80},{112,96},{128,112},... | collective-permute-start | bytes 776 | tf_op jit(solution)/shard_map/ppermute | solution.py:266
  131.0 41.5 %copy-start = (f32[64,2048]{1,0:T(8,128)S(1)}, f32[64,2048]{1,0:T(8,128)}, u32[]{:S(2)}) copy-start(f32[64,2048]{1,0:T(8,128)} %x_ref.1) | copy-start | bytes 1572868
  141.4 31.1 %collective-permute-start.4 = (bf16[1552,128]{1,0:T(8,128)(2,1)}, bf16[1552,128]{1,0:T(8,128)(2,1)S(1)}, u32[]{:S(2)}, u32[]{:S(2)}) collective-permute-start(bf16[1552,128]{1,0:T(8,128)(2,1)} %get-tuple-element.17), channel_id=1, source_target_pairs={{0,16},{16,32},{32,48},{48,64},{64,80},{80,96},{96,112},{112,128},... | collective-permute-start | bytes 1191944 | tf_op jit(solution)/shard_map/ppermute | solution.py:309
Sparse Core Ops, SparseCore 0:
  30.1 63.2 all-gather.2

commit v7 on v6

--- a/solution.py
+++ b/solution.py
@@ -25,9 +25,8 @@
     return pltpu.with_memory_space_constraint(value, pltpu.MemorySpace.VMEM)
 
 
-def pack_kernel(right_ref, initial_ref, blocks_ref, send_ref, keep_ref, own_ref):
-    width, n = blocks_ref.shape[0], blocks_ref.shape[1]
-    half = keep_ref.shape[0]
+def pack_kernel(right_ref, initial_ref, send_ref, field_ref):
+    half, _, n = send_ref.shape
     for i in range(2 * half):
         lanes = slice(i * n, (i + 1) * n)
         x = initial_ref[:, lanes]
@@ -35,9 +34,20 @@
         if i < half:
             send_ref[i] = pair
         else:
-            keep_ref[i - half] = pair
-    for k in range(width):
-        own_ref[k * n : (k + 1) * n, :] = blocks_ref[k].T
+            field_ref[i] = pair
+
+
+def merge_kernel(field_ref, arrived_ref, out_ref, sem):
+    del field_ref
+    copy = pltpu.make_async_copy(arrived_ref, out_ref.at[0 : arrived_ref.shape[0]], sem)
+    copy.start()
+    copy.wait()
+
+
+def flip_kernel(blocks_ref, out_ref):
+    n = blocks_ref.shape[1]
+    for k in range(blocks_ref.shape[0]):
+        out_ref[k * n : (k + 1) * n, :] = blocks_ref[k].T
 
 
 def spread_kernel(chip_ref, rows_ref, out_ref):
@@ -232,6 +242,10 @@
     all_hours = temporal_cov.shape[1]
     part = hours // 2
 
+    pairs = [
+        (((r + (t < half)) % regions) * tm_count + t, r * tm_count + t) for r in range(regions) for t in range(tm_count)
+    ]
+    row = lax.ppermute(blocks[0], REGION_TM, pairs)
     core = lax.axis_index(TM[1]).astype(jnp.int32).reshape(1)
     chip = lax.axis_index(TM[0]).astype(jnp.int32).reshape(1)
     chips = tm_count // 2
@@ -243,25 +257,35 @@
         name="spread",
     )(chip, temporal_cov)
     mine = lax.all_to_all(spread_rows, TM, split_axis=0, concat_axis=0, tiled=True)
-    packed, keep, own_blocks = pl.pallas_call(
+    packed, field = pl.pallas_call(
         pack_kernel,
         out_shape=(
             jax.ShapeDtypeStruct((half, 2 * hours, n), BF16),
-            jax.ShapeDtypeStruct((half, 2 * hours, n), BF16),
-            jax.ShapeDtypeStruct((width * n, n), BF16),
-        ),
-        in_specs=[VMEM] * 3,
-        out_specs=(VMEM,) * 3,
+            jax.ShapeDtypeStruct((rows, 2 * hours, n), BF16),
+        ),
+        in_specs=[VMEM] * 2,
+        out_specs=(VMEM, VMEM),
         name="pack",
-    )(right_side, initial, blocks[0])
+    )(right_side, initial)
     from_next = [((r + 1) % regions, r) for r in range(regions)]
     shifted = lax.ppermute(packed, REGION, from_next)
-    pairs = [
-        (((r + (t < half)) % regions) * tm_count + t, r * tm_count + t) for r in range(regions) for t in range(tm_count)
-    ]
-    row = lax.ppermute(own_blocks, REGION_TM, pairs)
-    window_blocks = lax.all_gather(row[None], TM, axis=0, tiled=True)
-    xd = jnp.concatenate([shifted, keep], axis=0)
+    flipped = pl.pallas_call(
+        flip_kernel,
+        out_shape=jax.ShapeDtypeStruct((width * n, n), BF16),
+        in_specs=[VMEM],
+        out_specs=VMEM,
+        name="flip",
+    )(keep_in_vmem(row))
+    window_blocks = lax.all_gather(flipped[None], TM, axis=0, tiled=True)
+    xd = pl.pallas_call(
+        merge_kernel,
+        out_shape=jax.ShapeDtypeStruct((rows, 2 * hours, n), BF16),
+        in_specs=[pl.BlockSpec(memory_space=pl.ANY), VMEM],
+        out_specs=pl.BlockSpec(memory_space=pl.ANY),
+        scratch_shapes=[pltpu.SemaphoreType.DMA],
+        input_output_aliases={0: 0},
+        name="merge",
+    )(field, keep_in_vmem(shifted))
     local_slots = lax.rem(neighbour_blocks, rows)
     next_slots = lax.ppermute(local_slots[:half], REGION, from_next)
     window_slots = jnp.concatenate([next_slots, local_slots[half:]], axis=0)

time: 183 us -> 180 us (0.984)
  local copies, waits for them, and re-layouts: 2.26 us -> 0.1 us
  transfers between devices with their start and end apart: 9 -> 9, of which waited for: 6 -> 6; matrix products, arithmetic and copies ran while one was open for 1% -> 0% of each run, Pallas kernels for 3% -> 5%
where the time goes in v7:
time: 180 us; the launch traced here: 179 us
  waiting for transfers between devices  66.4 us (37%)
  starting transfers between devices  46.7 us (26%)
  blocking collectives  29.1 us (16%)
  Pallas kernels  22.3 us (12%)
  between operations  14.1 us (8%)
    all_to_all x1, waiting for transfers between devices, steps(): lax.all_to_all(powers.reshape(tm_count, hours, 5 * n), TM, split_axis=0,...  24.6 us
    all_to_all x1, waiting for transfers between devices, steps(): arrived = lax.all_to_all(xd, TM, split_axis=0, concat_axis=0, tiled=True)  19.9 us
    all_to_all x1, blocking collectives, steps(): lax.all_to_all(spread, REGION, split_axis=0, concat_axis=0, tiled=True)  17.5 us
    ppermute x1, starting transfers between devices, steps(): row = lax.ppermute(blocks[0], REGION_TM, pairs)  13.7 us
    all_to_all x1, blocking collectives, steps(): over_tm = lax.all_to_all(gram, TM, split_axis=0, concat_axis=0, tiled=True)  11.6 us
    pallas_call x1, Pallas kernels, steps(): pl.pallas_call(spatial_kernel, out_shape=(jax.ShapeDtypeStruct((3 * half...  10.3 us
    all_to_all x1, waiting for transfers between devices, steps(): lax.all_to_all(spread_rows, TM, split_axis=0, concat_axis=0, tiled=True)  9.36 us
    ppermute x1, starting transfers between devices, steps(): shifted = lax.ppermute(packed, REGION, from_next)  7.31 us
  transfers between devices with their start and end apart: 9, of which 6 were waited for; matrix products, arithmetic and copies ran while one was open for 0% of the time, Pallas kernels for 5%

profile of v7, /device:TPU:1, one launch (start us, length us, event | category | flops | bytes accessed | tf_op | source)
XLA Modules:
  0.0 179.4 jit_solution(12058730420790632175)
XLA Ops:
  7.2 0.0 all-gather.3.cloned.1.call-start
  7.2 13.7 %collective-permute-start.3 = (bf16[9,128,128]{2,1,0:T(8,128)(2,1)}, bf16[9,128,128]{2,1,0:T(8,128)(2,1)S(1)}, u32[]{:S(2)}, u32[]{:S(2)}) collective-permute-start(bf16[9,128,128]{2,1,0:T(8,128)(2,1)} %bitcast.7), channel_id=1, source_target_pairs={{16,0},{17,1},{18,2},{19,3},{20,4},{21,5},{22,6},{23,7},{8,8},{9,9... | collective-permute-start | bytes 884744 | tf_op jit(solution)/shard_map/ppermute | solution.py:248
  20.9 6.0 %collective-permute-done.3.blocks_ref = bf16[9,128,128]{2,1,0:T(8,128)(2,1)S(1)} collective-permute-done((bf16[9,128,128]{2,1,0:T(8,128)(2,1)}, bf16[9,128,128]{2,1,0:T(8,128)(2,1)S(1)}, u32[]{:S(2)}, u32[]{:S(2)}) %collective-permute-start.3) | collective-permute-done | bytes 294944 | tf_op jit(solution)/shard_map/ppermute | solution.py:248
  26.9 0.9 flip.1
  27.7 0.0 all-gather.3.cloned.1.call-update
  27.8 1.8 %spread.1 = bf16[16,32,640]{2,1,0:T(8,128)(2,1)} custom-call(s32[1]{0:T(128)} %bitcast.1.chip_ref, bf16[64,1024]{1,0:T(8,128)(2,1)} %rows_ref.1), custom_call_target="tpu_custom_call" | custom-call | tf_op jit(solution)/shard_map/spread/pallas_call | solution.py:252
  29.6 6.4 %all-to-all-start = ((bf16[16,32,640]{2,1,0:T(8,128)(2,1)}), bf16[16,32,640]{2,1,0:T(8,128)(2,1)S(1)}, u32[]{:S(2)}, u32[]{:S(2)}) async-start(bf16[16,32,640]{2,1,0:T(8,128)(2,1)} %spread.1), calls=%async_computation | async-start | bytes 1310720 | tf_op jit(solution)/shard_map/all_to_all | solution.py:259
  36.0 2.1 %pack.1 = (bf16[8,128,128]{2,1,0:T(8,128)(2,1)}, bf16[16,128,128]{2,1,0:T(8,128)(2,1)}) custom-call(f32[64,2048]{1,0:T(8,128)} %right_ref.1, f32[64,2048]{1,0:T(8,128)} %x_ref.1), custom_call_target="tpu_custom_call" | custom-call | tf_op jit(solution)/shard_map/pack/pallas_call | solution.py:260
  38.1 7.3 %collective-permute-start.2 = (bf16[8,128,128]{2,1,0:T(8,128)(2,1)}, bf16[8,128,128]{2,1,0:T(8,128)(2,1)S(1)}, u32[]{:S(2)}, u32[]{:S(2)}) collective-permute-start(bf16[8,128,128]{2,1,0:T(8,128)(2,1)} %get-tuple-element.11), channel_id=1, source_target_pairs={{16,0},{32,16},{48,32},{64,48},{80,64},{96,80},{112,96},{128,112},... | collective-permute-start | bytes 786440 | tf_op jit(solution)/shard_map/ppermute | solution.py:271
  45.5 5.9 %collective-permute-done.2.arrived_ref = bf16[8,128,128]{2,1,0:T(8,128)(2,1)S(1)} collective-permute-done((bf16[8,128,128]{2,1,0:T(8,128)(2,1)}, bf16[8,128,128]{2,1,0:T(8,128)(2,1)S(1)}, u32[]{:S(2)}, u32[]{:S(2)}) %collective-permute-start.2) | collective-permute-done | bytes 262176 | tf_op jit(solution)/shard_map/ppermute | solution.py:271
  51.3 0.7 merge.1.xd_ref
  52.0 9.4 %all-to-all-done.own_ref = bf16[16,32,640]{2,1,0:T(8,128)(2,1)S(1)} async-done(((bf16[16,32,640]{2,1,0:T(8,128)(2,1)}), bf16[16,32,640]{2,1,0:T(8,128)(2,1)S(1)}, u32[]{:S(2)}, u32[]{:S(2)}) %all-to-all-start) | async-done | bytes 655392 | tf_op jit(solution)/shard_map/all_to_all | solution.py:259
  61.4 4.0 %all-to-all-start.1 = ((bf16[16,128,128]{2,1,0:T(8,128)(2,1)}), bf16[16,128,128]{2,1,0:T(8,128)(2,1)S(1)}, u32[]{:S(2)}, u32[]{:S(2)}) async-start(bf16[16,128,128]{2,1,0:T(8,128)(2,1)} %merge.1.xd_ref), calls=%async_computation.1 | async-start | bytes 1048576 | tf_op jit(solution)/shard_map/all_to_all | solution.py:294
  65.4 2.0 %collective-permute-start.1 = (bf16[16,32,640]{2,1,0:T(8,128)(2,1)S(1)}, bf16[16,32,640]{2,1,0:T(8,128)(2,1)S(1)}, u32[]{:S(2)}, u32[]{:S(2)}) collective-permute-start(bf16[16,32,640]{2,1,0:T(8,128)(2,1)S(1)} %all-to-all-done.own_ref), channel_id=1, source_target_pairs={{0,1},{1,0},{2,3},{3,2},{4,5},{5,4},{6,7},{7,6},{8,9},{9,8},{10,11... | collective-permute-start | bytes 1966088 | tf_op jit(solution)/shard_map/ppermute | solution.py:293
  67.4 19.9 %all-to-all-done.1.v_ref = bf16[16,128,128]{2,1,0:T(8,128)(2,1)S(1)} async-done(((bf16[16,128,128]{2,1,0:T(8,128)(2,1)}), bf16[16,128,128]{2,1,0:T(8,128)(2,1)S(1)}, u32[]{:S(2)}, u32[]{:S(2)}) %all-to-all-start.1) | async-done | bytes 524320 | tf_op jit(solution)/shard_map/all_to_all | solution.py:294
  87.3 0.0 collective-permute-done.1.other_ref
  87.3 4.0 %temporal.1 = (bf16[1024,640]{1,0:T(8,128)(2,1)}, f32[8,128]{1,0:T(8,128)}) custom-call(s32[1]{0:T(128)} %bitcast.core_ref, bf16[16,32,640]{2,1,0:T(8,128)(2,1)S(1)} %all-to-all-done.own_ref, bf16[16,32,640]{2,1,0:T(8,128)(2,1)S(1)} %collective-permute-done.1.other_ref, bf16[16,128,128]{2,1,0:T(8,128)(2,1)S(1)} %all-to-all-done.1.v_ref), custom_call_target="tpu_custom_call" | custom-call | tf_op jit(solution)/shard_map/temporal/pallas_call | solution.py:295
  91.4 4.0 %all-to-all-start.2 = ((bf16[16,64,640]{2,1,0:T(8,128)(2,1)}), bf16[16,64,640]{2,1,0:T(8,128)(2,1)S(1)}, u32[]{:S(2)}, u32[]{:S(2)}) async-start(bf16[16,64,640]{2,1,0:T(8,128)(2,1)} %bitcast.6), calls=%async_computation.2 | async-start | bytes 2621440 | tf_op jit(solution)/shard_map/all_to_all | solution.py:306
  95.4 0.0 copy-done.2
  95.4 0.1 copy.8
  95.5 7.3 %collective-permute-start = (s32[8,8]{1,0:T(8,128)S(1)}, s32[8,8]{1,0:T(8,128)S(1)}, u32[]{:S(2)}, u32[]{:S(2)}) collective-permute-start(s32[8,8]{1,0:T(8,128)S(1)} %get-tuple-element.18), channel_id=1, source_target_pairs={{16,0},{32,16},{48,32},{64,48},{80,64},{96,80},{112,96},{128,112},... | collective-permute-start | bytes 776 | tf_op jit(solution)/shard_map/ppermute | solution.py:290
  102.8 0.7 collective-permute-done
  103.5 0.6 pad_add_fusion.slots_ref
  104.1 24.6 %all-to-all-done.2.g_ref = bf16[16,64,640]{2,1,0:T(8,128)(2,1)S(1)} async-done(((bf16[16,64,640]{2,1,0:T(8,128)(2,1)}), bf16[16,64,640]{2,1,0:T(8,128)(2,1)S(1)}, u32[]{:S(2)}, u32[]{:S(2)}) %all-to-all-start.2) | async-done | bytes 1310752 | tf_op jit(solution)/shard_map/all_to_all | solution.py:306
  128.7 0.0 copy-done
  128.7 10.3 %spatial.1 = (bf16[1552,128]{1,0:T(8,128)(2,1)}, f32[3,8,64,128]{3,2,1,0:T(8,128)}, f32[16,8,128]{2,1,0:T(8,128)}, f32[8,128]{1,0:T(8,128)}) custom-call(s32[16,8]{1,0:T(8,128)} %pad_add_fusion.slots_ref, bf16[16,64,640]{2,1,0:T(8,128)(2,1)S(1)} %all-to-all-done.2.g_ref, bf16[16,128,128]{2,1,0:T(8,128)(2,1)S(1)} %copy-done, ...), custom_call_target="tpu_custom_call" | custom-call | tf_op jit(solution)/shard_map/spatial/pallas_call | solution.py:308
  138.9 1.9 %collective-permute-start.4 = (bf16[1552,128]{1,0:T(8,128)(2,1)}, bf16[1552,128]{1,0:T(8,128)(2,1)S(1)}, u32[]{:S(2)}, u32[]{:S(2)}) collective-permute-start(bf16[1552,128]{1,0:T(8,128)(2,1)} %get-tuple-element.15), channel_id=1, source_target_pairs={{0,16},{16,32},{32,48},{48,64},{64,80},{80,96},{96,112},{112,128},... | collective-permute-start | bytes 1191944 | tf_op jit(solution)/shard_map/ppermute | solution.py:333
  140.9 11.6 %all_to_all.25 = f32[16,8,128]{2,1,0:T(8,128)S(1)} all-to-all(f32[16,8,128]{2,1,0:T(8,128)} %get-tuple-element.14), channel_id=1, replica_groups=mesh['region_0'=4,'region_1'=8,'tm_0'=8,'tm_1'=2] {'tm_0','tm_1'}, dimensions={0} | all-to-all | bytes 131072 | tf_op jit(solution)/shard_map/all_to_all | solution.py:334
  152.4 17.5 %all_to_all.26.gram_ref = f32[32,8,128]{2,1,0:T(8,128)} all-to-all(f32[32,8,128]{2,1,0:T(8,128)S(1)} %broadcast_in_dim.10), channel_id=1, replica_groups=mesh['region_0'=4,'region_1'=8,'tm_0'=8,'tm_1'=2] {'region_0','region_1'}, dimensions={0} | all-to-all | bytes 262144 | tf_op jit(solution)/shard_map/all_to_all | solution.py:336
  170.0 0.0 collective-permute-done.4.low_ref
  170.0 0.0 copy-done.1
  170.0 2.5 %finish.1 = (f32[64,2048]{1,0:T(8,128)}, f32[64,2048]{1,0:T(8,128)}) custom-call(f32[32,8,128]{2,1,0:T(8,128)} %all_to_all.26.gram_ref, f32[64,2048]{1,0:T(8,128)S(1)} %copy-done.1, bf16[1552,128]{1,0:T(8,128)(2,1)S(1)} %collective-permute-done.4.low_ref, f32[3,8,64,128]{3,2,1,0:T(8,128)} %get-tuple-element.16.high_ref, f32[8,128]{1,0:T(8,128)} %get-tuple-element.17.centre_ref), custom_call_target="tpu_custom_call" | custom-call | tf_op jit(solution)/shard_map/finish/pallas_call | solution.py:337
  (8 shorter events, 0.1 us)
Async XLA Ops:
  7.2 121.5 %all-gather.3.cloned.1.call-start = ((), (), s32[]{:S(2)}) async-start(), calls=%async_computation.5 | async-start | bytes 5013504 | tf_op jit(solution)/shard_map/all_gather | solution.py:279
  7.2 19.7 %collective-permute-start.3 = (bf16[9,128,128]{2,1,0:T(8,128)(2,1)}, bf16[9,128,128]{2,1,0:T(8,128)(2,1)S(1)}, u32[]{:S(2)}, u32[]{:S(2)}) collective-permute-start(bf16[9,128,128]{2,1,0:T(8,128)(2,1)} %bitcast.7), channel_id=1, source_target_pairs={{16,0},{17,1},{18,2},{19,3},{20,4},{21,5},{22,6},{23,7},{8,8},{9,9... | collective-permute-start | bytes 884744 | tf_op jit(solution)/shard_map/ppermute | solution.py:248
  29.6 31.8 %all-to-all-start = ((bf16[16,32,640]{2,1,0:T(8,128)(2,1)}), bf16[16,32,640]{2,1,0:T(8,128)(2,1)S(1)}, u32[]{:S(2)}, u32[]{:S(2)}) async-start(bf16[16,32,640]{2,1,0:T(8,128)(2,1)} %spread.1), calls=%async_computation | async-start | bytes 1310720 | tf_op jit(solution)/shard_map/all_to_all | solution.py:259
  38.1 13.2 %collective-permute-start.2 = (bf16[8,128,128]{2,1,0:T(8,128)(2,1)}, bf16[8,128,128]{2,1,0:T(8,128)(2,1)S(1)}, u32[]{:S(2)}, u32[]{:S(2)}) collective-permute-start(bf16[8,128,128]{2,1,0:T(8,128)(2,1)} %get-tuple-element.11), channel_id=1, source_target_pairs={{16,0},{32,16},{48,32},{64,48},{80,64},{96,80},{112,96},{128,112},... | collective-permute-start | bytes 786440 | tf_op jit(solution)/shard_map/ppermute | solution.py:271
  61.4 25.9 %all-to-all-start.1 = ((bf16[16,128,128]{2,1,0:T(8,128)(2,1)}), bf16[16,128,128]{2,1,0:T(8,128)(2,1)S(1)}, u32[]{:S(2)}, u32[]{:S(2)}) async-start(bf16[16,128,128]{2,1,0:T(8,128)(2,1)} %merge.1.xd_ref), calls=%async_computation.1 | async-start | bytes 1048576 | tf_op jit(solution)/shard_map/all_to_all | solution.py:294
  65.4 21.9 %collective-permute-start.1 = (bf16[16,32,640]{2,1,0:T(8,128)(2,1)S(1)}, bf16[16,32,640]{2,1,0:T(8,128)(2,1)S(1)}, u32[]{:S(2)}, u32[]{:S(2)}) collective-permute-start(bf16[16,32,640]{2,1,0:T(8,128)(2,1)S(1)} %all-to-all-done.own_ref), channel_id=1, source_target_pairs={{0,1},{1,0},{2,3},{3,2},{4,5},{5,4},{6,7},{7,6},{8,9},{9,8},{10,11... | collective-permute-start | bytes 1966088 | tf_op jit(solution)/shard_map/ppermute | solution.py:293
  91.4 4.0 %copy-start.2 = (s32[16,8]{0,1:T(8,128)S(1)}, s32[16,8]{0,1:T(8,128)}, u32[]{:S(2)}) copy-start(s32[16,8]{0,1:T(8,128)} %param.8) | copy-start | bytes 1540
  91.4 37.3 %copy-start = (bf16[16,128,128]{2,1,0:T(8,128)(2,1)S(1)}, bf16[16,128,128]{2,1,0:T(8,128)(2,1)}, u32[]{:S(2)}) copy-start(bf16[16,128,128]{2,1,0:T(8,128)(2,1)} %merge.1.xd_ref) | copy-start | bytes 1572868
  91.4 37.3 %all-to-all-start.2 = ((bf16[16,64,640]{2,1,0:T(8,128)(2,1)}), bf16[16,64,640]{2,1,0:T(8,128)(2,1)S(1)}, u32[]{:S(2)}, u32[]{:S(2)}) async-start(bf16[16,64,640]{2,1,0:T(8,128)(2,1)} %bitcast.6), calls=%async_computation.2 | async-start | bytes 2621440 | tf_op jit(solution)/shard_map/all_to_all | solution.py:306
  95.5 8.0 %collective-permute-start = (s32[8,8]{1,0:T(8,128)S(1)}, s32[8,8]{1,0:T(8,128)S(1)}, u32[]{:S(2)}, u32[]{:S(2)}) collective-permute-start(s32[8,8]{1,0:T(8,128)S(1)} %get-tuple-element.18), channel_id=1, source_target_pairs={{16,0},{32,16},{48,32},{64,48},{80,64},{96,80},{112,96},{128,112},... | collective-permute-start | bytes 776 | tf_op jit(solution)/shard_map/ppermute | solution.py:290
  128.7 41.3 %copy-start.1 = (f32[64,2048]{1,0:T(8,128)S(1)}, f32[64,2048]{1,0:T(8,128)}, u32[]{:S(2)}) copy-start(f32[64,2048]{1,0:T(8,128)} %x_ref.1) | copy-start | bytes 1572868
  138.9 31.1 %collective-permute-start.4 = (bf16[1552,128]{1,0:T(8,128)(2,1)}, bf16[1552,128]{1,0:T(8,128)(2,1)S(1)}, u32[]{:S(2)}, u32[]{:S(2)}) collective-permute-start(bf16[1552,128]{1,0:T(8,128)(2,1)} %get-tuple-element.15), channel_id=1, source_target_pairs={{0,16},{16,32},{32,48},{48,64},{64,80},{80,96},{96,112},{112,128},... | collective-permute-start | bytes 1191944 | tf_op jit(solution)/shard_map/ppermute | solution.py:333
Sparse Core Ops, SparseCore 0:
  27.9 63.2 all-gather.2

commit v8 on v7

--- a/solution.py
+++ b/solution.py
@@ -62,11 +62,11 @@
                 out_ref[2 * chip + core, :, k * n : (k + 1) * n] = tile
 
 
-def temporal_kernel(core_ref, own_ref, other_ref, v_ref, w_ref, shift_ref, c_buf):
+def square_kernel(core_ref, own_ref, other_ref, c_buf, shift_ref):
     groups, part, wide = own_ref.shape
     chips = groups // 2
-    n = v_ref.shape[2]
-    hours = chips * n
+    hours = c_buf.shape[0]
+    n = hours // chips
     core = core_ref[0]
     for t in range(groups):
         for ref, which in ((own_ref, core), (other_ref, 1 - core)):
@@ -86,13 +86,19 @@
     c0 = jnp.sum(diagonal, axis=(0, 1), keepdims=True) / hours
     shift_ref[...] = jnp.broadcast_to(c0, shift_ref.shape)
 
+
+def temporal_kernel(c_ref, shift_ref, v_ref, w_ref):
+    _, both, n = v_ref.shape
+    hours = c_ref.shape[0]
+    c0 = shift_ref[0:1, 0:1]
+
     def power(v, base):
-        out = (dot(c_buf[...], v) - c0 * v.astype(F32)).astype(BF16)
+        out = (dot(c_ref[...], v) - c0 * v.astype(F32)).astype(BF16)
         w_ref[:, base : base + v.shape[1]] = out
         return out
 
     v = v_ref[...]
-    pairs = [v[:, k * 2 * part : (k + 1) * 2 * part].reshape(hours, n) for k in range(2)]
+    pairs = [v[:, k * both // 2 : (k + 1) * both // 2].reshape(hours, n) for k in range(2)]
     first = power(jnp.concatenate(pairs, axis=1), 0)
     second = power(first, 2 * n)
     power(second[:, :n], 4 * n)
@@ -254,6 +260,7 @@
         out_shape=jax.ShapeDtypeStruct((tm_count, part, (chips // 2 + 1) * (all_hours // chips)), BF16),
         in_specs=[SMEM, VMEM],
         out_specs=VMEM,
+        compiler_params=pltpu.CompilerParams(vmem_limit_bytes=8 * 2**20),
         name="spread",
     )(chip, temporal_cov)
     mine = lax.all_to_all(spread_rows, TM, split_axis=0, concat_axis=0, tiled=True)
@@ -265,6 +272,7 @@
         ),
         in_specs=[VMEM] * 2,
         out_specs=(VMEM, VMEM),
+        compiler_params=pltpu.CompilerParams(vmem_limit_bytes=8 * 2**20),
         name="pack",
     )(right_side, initial)
     from_next = [((r + 1) % regions, r) for r in range(regions)]
@@ -274,6 +282,7 @@
         out_shape=jax.ShapeDtypeStruct((width * n, n), BF16),
         in_specs=[VMEM],
         out_specs=VMEM,
+        compiler_params=pltpu.CompilerParams(vmem_limit_bytes=8 * 2**20),
         name="flip",
     )(keep_in_vmem(row))
     window_blocks = lax.all_gather(flipped[None], TM, axis=0, tiled=True)
@@ -284,6 +293,7 @@
         out_specs=pl.BlockSpec(memory_space=pl.ANY),
         scratch_shapes=[pltpu.SemaphoreType.DMA],
         input_output_aliases={0: 0},
+        compiler_params=pltpu.CompilerParams(vmem_limit_bytes=8 * 2**20),
         name="merge",
     )(field, keep_in_vmem(shifted))
     local_slots = lax.rem(neighbour_blocks, rows)
@@ -292,17 +302,24 @@
 
     theirs = lax.ppermute(mine, TM[1], [(0, 1), (1, 0)])
     arrived = lax.all_to_all(xd, TM, split_axis=0, concat_axis=0, tiled=True)
-    powers, shift = pl.pallas_call(
+    covariance, shift = pl.pallas_call(
+        square_kernel,
+        out_shape=(
+            jax.ShapeDtypeStruct((all_hours, all_hours), BF16),
+            jax.ShapeDtypeStruct((8, n), F32),
+        ),
+        in_specs=[SMEM, VMEM, VMEM],
+        out_specs=(VMEM, VMEM),
+        compiler_params=pltpu.CompilerParams(vmem_limit_bytes=8 * 2**20),
+        name="square",
+    )(core, keep_in_vmem(mine), keep_in_vmem(theirs))
+    powers = pl.pallas_call(
         temporal_kernel,
-        out_shape=(
-            jax.ShapeDtypeStruct((all_hours, 5 * n), BF16),
-            jax.ShapeDtypeStruct((8, n), F32),
-        ),
-        in_specs=[SMEM, VMEM, VMEM, VMEM],
-        out_specs=(VMEM, VMEM),
-        scratch_shapes=[pltpu.VMEM((all_hours, all_hours), BF16)],
+        out_shape=jax.ShapeDtypeStruct((all_hours, 5 * n), BF16),
+        in_specs=[VMEM] * 3,
+        out_specs=VMEM,
         name="temporal",
-    )(core, keep_in_vmem(mine), keep_in_vmem(theirs), keep_in_vmem(arrived))
+    )(covariance, shift, keep_in_vmem(arrived))
     returned = lax.all_to_all(powers.reshape(tm_count, hours, 5 * n), TM, split_axis=0, concat_axis=0, tiled=True)
 
     low, high, gram, centre = pl.pallas_call(
@@ -313,7 +330,7 @@
             jax.ShapeDtypeStruct((tm_count, 8, n), F32),
             jax.ShapeDtypeStruct((8, n), F32),
         ),
-        in_specs=[SMEM, VMEM, VMEM, VMEM, pl.BlockSpec(memory_space=pl.ANY)],
+        in_specs=[SMEM, VMEM, VMEM, VMEM, pl.BlockSpec(memory_space=pltpu.MemorySpace.HBM)],
         out_specs=(VMEM,) * 4,
         scratch_shapes=[
             pltpu.VMEM((rows, width * n, n), BF16),

time: 180 us -> 182 us (1.011)
  local copies, waits for them, and re-layouts: 0.1 us -> 2.95 us
    all_to_all x1, waiting for transfers between devices: 19.9 us -> 15.5 us  [steps(): arrived = lax.all_to_all(xd, TM, split_axis=0, concat_axis=0, tiled=True)]
    unnamed x7 -> x13, local copies, waits for them, and re-layouts: 0.08 us -> 2.93 us
    ppermute x1, waiting for transfers between devices: 0.01 us -> 1.96 us  [steps(): theirs = lax.ppermute(mine, TM[1], [(0, 1), (1, 0)])]
    pallas_call x1 -> x2, Pallas kernels: 4.03 us -> 5.9 us  [the longest x1 5.46 us: steps(): pl.pallas_call(temporal_kernel, out_shape=jax.ShapeDtypeStruct((all_hours...]
  transfers between devices with their start and end apart: 9 -> 9, of which waited for: 6 -> 7; matrix products, arithmetic and copies ran while one was open for 0% -> 0% of each run, Pallas kernels for 5% -> 5%
where the time goes in v8:
time: 182 us; the launch traced here: 181 us
  waiting for transfers between devices  65.2 us (36%)
  starting transfers between devices  46.9 us (26%)
  blocking collectives  29.1 us (16%)
  Pallas kernels  22.1 us (12%)
  between operations  14.2 us (8%)
  local copies, waits for them, and re-layouts  2.95 us (2%)
    all_to_all x1, waiting for transfers between devices, steps(): lax.all_to_all(powers.reshape(tm_count, hours, 5 * n), TM, split_axis=0,...  24.5 us
    all_to_all x1, blocking collectives, steps(): lax.all_to_all(spread, REGION, split_axis=0, concat_axis=0, tiled=True)  17.6 us
    all_to_all x1, waiting for transfers between devices, steps(): arrived = lax.all_to_all(xd, TM, split_axis=0, concat_axis=0, tiled=True)  15.5 us
    ppermute x1, starting transfers between devices, steps(): row = lax.ppermute(blocks[0], REGION_TM, pairs)  13.8 us
    all_to_all x1, blocking collectives, steps(): over_tm = lax.all_to_all(gram, TM, split_axis=0, concat_axis=0, tiled=True)  11.6 us
    all_to_all x1, waiting for transfers between devices, steps(): lax.all_to_all(spread_rows, TM, split_axis=0, concat_axis=0, tiled=True)  10.9 us
    pallas_call x1, Pallas kernels, steps(): pl.pallas_call(spatial_kernel, out_shape=(jax.ShapeDtypeStruct((3 * half...  10.4 us
    ppermute x1, starting transfers between devices, steps(): shifted = lax.ppermute(packed, REGION, from_next)  7.31 us
  transfers between devices with their start and end apart: 9, of which 7 were waited for; matrix products, arithmetic and copies ran while one was open for 0% of the time, Pallas kernels for 5%

profile of v8, /device:TPU:1, one launch (start us, length us, event | category | flops | bytes accessed | tf_op | source)
XLA Modules:
  0.0 181.1 jit_solution(1807662270557524843)
XLA Ops:
  7.2 0.0 all-gather.3.cloned.1.call-start
  7.2 13.8 %collective-permute-start.3 = (bf16[9,128,128]{2,1,0:T(8,128)(2,1)}, bf16[9,128,128]{2,1,0:T(8,128)(2,1)S(1)}, u32[]{:S(2)}, u32[]{:S(2)}) collective-permute-start(bf16[9,128,128]{2,1,0:T(8,128)(2,1)} %bitcast.7), channel_id=1, source_target_pairs={{16,0},{17,1},{18,2},{19,3},{20,4},{21,5},{22,6},{23,7},{8,8},{9,9... | collective-permute-start | bytes 884744 | tf_op jit(solution)/shard_map/ppermute | solution.py:254
  21.0 6.0 %collective-permute-done.3.blocks_ref = bf16[9,128,128]{2,1,0:T(8,128)(2,1)S(1)} collective-permute-done((bf16[9,128,128]{2,1,0:T(8,128)(2,1)}, bf16[9,128,128]{2,1,0:T(8,128)(2,1)S(1)}, u32[]{:S(2)}, u32[]{:S(2)}) %collective-permute-start.3) | collective-permute-done | bytes 294944 | tf_op jit(solution)/shard_map/ppermute | solution.py:254
  27.0 0.9 flip.1
  27.9 0.0 all-gather.3.cloned.1.call-update
  27.9 0.9 copy-done.3
  28.8 0.9 spread.1
  29.8 6.4 %all-to-all-start = ((bf16[16,32,640]{2,1,0:T(8,128)(2,1)}), bf16[16,32,640]{2,1,0:T(8,128)(2,1)S(1)}, u32[]{:S(2)}, u32[]{:S(2)}) async-start(bf16[16,32,640]{2,1,0:T(8,128)(2,1)} %spread.1), calls=%async_computation | async-start | bytes 1310720 | tf_op jit(solution)/shard_map/all_to_all | solution.py:266
  36.2 0.8 pack.1
  37.0 7.3 %collective-permute-start.2 = (bf16[8,128,128]{2,1,0:T(8,128)(2,1)S(1)}, bf16[8,128,128]{2,1,0:T(8,128)(2,1)S(1)}, u32[]{:S(2)}, u32[]{:S(2)}) collective-permute-start(bf16[8,128,128]{2,1,0:T(8,128)(2,1)S(1)} %get-tuple-element.13), channel_id=1, source_target_pairs={{16,0},{32,16},{48,32},{64,48},{80,64},{96,80},{112,96},{128,112},... | collective-permute-start | bytes 786440 | tf_op jit(solution)/shard_map/ppermute | solution.py:279
  44.4 5.5 %collective-permute-done.2.arrived_ref = bf16[8,128,128]{2,1,0:T(8,128)(2,1)S(1)} collective-permute-done((bf16[8,128,128]{2,1,0:T(8,128)(2,1)S(1)}, bf16[8,128,128]{2,1,0:T(8,128)(2,1)S(1)}, u32[]{:S(2)}, u32[]{:S(2)}) %collective-permute-start.2) | collective-permute-done | bytes 262176 | tf_op jit(solution)/shard_map/ppermute | solution.py:279
  49.9 0.7 merge.1.xd_ref
  50.6 10.9 %all-to-all-done.own_ref = bf16[16,32,640]{2,1,0:T(8,128)(2,1)S(1)} async-done(((bf16[16,32,640]{2,1,0:T(8,128)(2,1)}), bf16[16,32,640]{2,1,0:T(8,128)(2,1)S(1)}, u32[]{:S(2)}, u32[]{:S(2)}) %all-to-all-start) | async-done | bytes 655392 | tf_op jit(solution)/shard_map/all_to_all | solution.py:266
  61.5 4.0 %all-to-all-start.1 = ((bf16[16,128,128]{2,1,0:T(8,128)(2,1)}), bf16[16,128,128]{2,1,0:T(8,128)(2,1)S(1)}, u32[]{:S(2)}, u32[]{:S(2)}) async-start(bf16[16,128,128]{2,1,0:T(8,128)(2,1)} %merge.1.xd_ref), calls=%async_computation.1 | async-start | bytes 1048576 | tf_op jit(solution)/shard_map/all_to_all | solution.py:304
  65.6 2.0 %collective-permute-start.1 = (bf16[16,32,640]{2,1,0:T(8,128)(2,1)S(1)}, bf16[16,32,640]{2,1,0:T(8,128)(2,1)S(1)}, u32[]{:S(2)}, u32[]{:S(2)}) collective-permute-start(bf16[16,32,640]{2,1,0:T(8,128)(2,1)S(1)} %all-to-all-done.own_ref), channel_id=1, source_target_pairs={{0,1},{1,0},{2,3},{3,2},{4,5},{5,4},{6,7},{7,6},{8,9},{9,8},{10,11... | collective-permute-start | bytes 1966088 | tf_op jit(solution)/shard_map/ppermute | solution.py:303
  67.6 2.0 %collective-permute-done.1.other_ref = bf16[16,32,640]{2,1,0:T(8,128)(2,1)S(1)} collective-permute-done((bf16[16,32,640]{2,1,0:T(8,128)(2,1)S(1)}, bf16[16,32,640]{2,1,0:T(8,128)(2,1)S(1)}, u32[]{:S(2)}, u32[]{:S(2)}) %collective-permute-start.1) | collective-permute-done | bytes 655392 | tf_op jit(solution)/shard_map/ppermute | solution.py:303
  69.5 0.4 square.1
  70.0 1.3 copy-done.1
  71.3 0.6 copy-done.4
  71.9 15.5 %all-to-all-done.1.v_ref = bf16[16,128,128]{2,1,0:T(8,128)(2,1)S(1)} async-done(((bf16[16,128,128]{2,1,0:T(8,128)(2,1)}), bf16[16,128,128]{2,1,0:T(8,128)(2,1)S(1)}, u32[]{:S(2)}, u32[]{:S(2)}) %all-to-all-start.1) | async-done | bytes 524320 | tf_op jit(solution)/shard_map/all_to_all | solution.py:304
  87.4 5.5 %temporal.1 = bf16[1024,640]{1,0:T(8,128)(2,1)} custom-call(bf16[1024,1024]{1,0:T(8,128)(2,1)} %copy-done.1, f32[8,128]{1,0:T(8,128)} %copy-done.4, bf16[16,128,128]{2,1,0:T(8,128)(2,1)S(1)} %all-to-all-done.1.v_ref), custom_call_target="tpu_custom_call" | custom-call | tf_op jit(solution)/shard_map/temporal/pallas_call | solution.py:316
  92.9 4.1 %all-to-all-start.2 = ((bf16[16,64,640]{2,1,0:T(8,128)(2,1)}), bf16[16,64,640]{2,1,0:T(8,128)(2,1)S(1)}, u32[]{:S(2)}, u32[]{:S(2)}) async-start(bf16[16,64,640]{2,1,0:T(8,128)(2,1)} %bitcast.5), calls=%async_computation.2 | async-start | bytes 2621440 | tf_op jit(solution)/shard_map/all_to_all | solution.py:323
  97.0 0.1 copy.8
  97.1 7.3 %collective-permute-start = (s32[8,8]{1,0:T(8,128)S(1)}, s32[8,8]{1,0:T(8,128)S(1)}, u32[]{:S(2)}, u32[]{:S(2)}) collective-permute-start(s32[8,8]{1,0:T(8,128)S(1)} %get-tuple-element.18), channel_id=1, source_target_pairs={{16,0},{32,16},{48,32},{64,48},{80,64},{96,80},{112,96},{128,112},... | collective-permute-start | bytes 776 | tf_op jit(solution)/shard_map/ppermute | solution.py:300
  104.4 0.7 collective-permute-done
  105.1 0.6 pad_add_fusion.slots_ref
  105.7 24.5 %all-to-all-done.2.g_ref = bf16[16,64,640]{2,1,0:T(8,128)(2,1)S(1)} async-done(((bf16[16,64,640]{2,1,0:T(8,128)(2,1)}), bf16[16,64,640]{2,1,0:T(8,128)(2,1)S(1)}, u32[]{:S(2)}, u32[]{:S(2)}) %all-to-all-start.2) | async-done | bytes 1310752 | tf_op jit(solution)/shard_map/all_to_all | solution.py:323
  130.2 10.4 %spatial.1 = (bf16[1552,128]{1,0:T(8,128)(2,1)}, f32[3,8,64,128]{3,2,1,0:T(8,128)}, f32[16,8,128]{2,1,0:T(8,128)}, f32[8,128]{1,0:T(8,128)}) custom-call(s32[16,8]{1,0:T(8,128)} %pad_add_fusion.slots_ref, bf16[16,64,640]{2,1,0:T(8,128)(2,1)S(1)} %all-to-all-done.2.g_ref, bf16[16,128,128]{2,1,0:T(8,128)(2,1)} %merge.1.xd_ref, f32[8,128]{1,0:T(8,128)} %copy-done.4, ...), custom_call_target="tpu_custom_call" | custom-call | tf_op jit(solution)/shard_map/spatial/pallas_call | solution.py:325
  140.6 1.9 %collective-permute-start.4 = (bf16[1552,128]{1,0:T(8,128)(2,1)}, bf16[1552,128]{1,0:T(8,128)(2,1)S(1)}, u32[]{:S(2)}, u32[]{:S(2)}) collective-permute-start(bf16[1552,128]{1,0:T(8,128)(2,1)} %get-tuple-element.15), channel_id=1, source_target_pairs={{0,16},{16,32},{32,48},{48,64},{64,80},{80,96},{96,112},{112,128},... | collective-permute-start | bytes 1191944 | tf_op jit(solution)/shard_map/ppermute | solution.py:350
  142.5 11.6 %all_to_all.25 = f32[16,8,128]{2,1,0:T(8,128)S(1)} all-to-all(f32[16,8,128]{2,1,0:T(8,128)} %get-tuple-element.14), channel_id=1, replica_groups=mesh['region_0'=4,'region_1'=8,'tm_0'=8,'tm_1'=2] {'tm_0','tm_1'}, dimensions={0} | all-to-all | bytes 131072 | tf_op jit(solution)/shard_map/all_to_all | solution.py:351
  154.1 17.6 %all_to_all.26.gram_ref = f32[32,8,128]{2,1,0:T(8,128)} all-to-all(f32[32,8,128]{2,1,0:T(8,128)S(1)} %broadcast_in_dim.10), channel_id=1, replica_groups=mesh['region_0'=4,'region_1'=8,'tm_0'=8,'tm_1'=2] {'region_0','region_1'}, dimensions={0} | all-to-all | bytes 262144 | tf_op jit(solution)/shard_map/all_to_all | solution.py:353
  171.7 2.5 %finish.1 = (f32[64,2048]{1,0:T(8,128)}, f32[64,2048]{1,0:T(8,128)}) custom-call(f32[32,8,128]{2,1,0:T(8,128)} %all_to_all.26.gram_ref, f32[64,2048]{1,0:T(8,128)S(1)} %copy-done, bf16[1552,128]{1,0:T(8,128)(2,1)S(1)} %collective-permute-done.4.low_ref, f32[3,8,64,128]{3,2,1,0:T(8,128)} %get-tuple-element.16.high_ref, f32[8,128]{1,0:T(8,128)} %get-tuple-element.17.centre_ref), custom_call_target="tpu_custom_call" | custom-call | tf_op jit(solution)/shard_map/finish/pallas_call | solution.py:354
  (15 shorter events, 0.1 us)
Async XLA Ops:
  7.2 29.0 %copy-start.2 = (f32[64,2048]{1,0:T(8,128)S(1)}, f32[64,2048]{1,0:T(8,128)}, u32[]{:S(2)}) copy-start(f32[64,2048]{1,0:T(8,128)} %right_ref.1) | copy-start | bytes 1572868
  7.2 29.0 %copy-start = (f32[64,2048]{1,0:T(8,128)S(1)}, f32[64,2048]{1,0:T(8,128)}, u32[]{:S(2)}) copy-start(f32[64,2048]{1,0:T(8,128)} %x_ref.1) | copy-start | bytes 1572868
  7.2 123.0 %all-gather.3.cloned.1.call-start = ((), (), s32[]{:S(2)}) async-start(), calls=%async_computation.5 | async-start | bytes 5013504 | tf_op jit(solution)/shard_map/all_gather | solution.py:288
  7.2 19.8 %collective-permute-start.3 = (bf16[9,128,128]{2,1,0:T(8,128)(2,1)}, bf16[9,128,128]{2,1,0:T(8,128)(2,1)S(1)}, u32[]{:S(2)}, u32[]{:S(2)}) collective-permute-start(bf16[9,128,128]{2,1,0:T(8,128)(2,1)} %bitcast.7), channel_id=1, source_target_pairs={{16,0},{17,1},{18,2},{19,3},{20,4},{21,5},{22,6},{23,7},{8,8},{9,9... | collective-permute-start | bytes 884744 | tf_op jit(solution)/shard_map/ppermute | solution.py:254
  27.9 0.9 copy-start.3
  29.8 31.8 %all-to-all-start = ((bf16[16,32,640]{2,1,0:T(8,128)(2,1)}), bf16[16,32,640]{2,1,0:T(8,128)(2,1)S(1)}, u32[]{:S(2)}, u32[]{:S(2)}) async-start(bf16[16,32,640]{2,1,0:T(8,128)(2,1)} %spread.1), calls=%async_computation | async-start | bytes 1310720 | tf_op jit(solution)/shard_map/all_to_all | solution.py:266
  37.0 12.9 %collective-permute-start.2 = (bf16[8,128,128]{2,1,0:T(8,128)(2,1)S(1)}, bf16[8,128,128]{2,1,0:T(8,128)(2,1)S(1)}, u32[]{:S(2)}, u32[]{:S(2)}) collective-permute-start(bf16[8,128,128]{2,1,0:T(8,128)(2,1)S(1)} %get-tuple-element.13), channel_id=1, source_target_pairs={{16,0},{32,16},{48,32},{64,48},{80,64},{96,80},{112,96},{128,112},... | collective-permute-start | bytes 786440 | tf_op jit(solution)/shard_map/ppermute | solution.py:279
  61.5 25.9 %all-to-all-start.1 = ((bf16[16,128,128]{2,1,0:T(8,128)(2,1)}), bf16[16,128,128]{2,1,0:T(8,128)(2,1)S(1)}, u32[]{:S(2)}, u32[]{:S(2)}) async-start(bf16[16,128,128]{2,1,0:T(8,128)(2,1)} %merge.1.xd_ref), calls=%async_computation.1 | async-start | bytes 1048576 | tf_op jit(solution)/shard_map/all_to_all | solution.py:304
  65.6 4.0 %collective-permute-start.1 = (bf16[16,32,640]{2,1,0:T(8,128)(2,1)S(1)}, bf16[16,32,640]{2,1,0:T(8,128)(2,1)S(1)}, u32[]{:S(2)}, u32[]{:S(2)}) collective-permute-start(bf16[16,32,640]{2,1,0:T(8,128)(2,1)S(1)} %all-to-all-done.own_ref), channel_id=1, source_target_pairs={{0,1},{1,0},{2,3},{3,2},{4,5},{5,4},{6,7},{7,6},{8,9},{9,8},{10,11... | collective-permute-start | bytes 1966088 | tf_op jit(solution)/shard_map/ppermute | solution.py:303
  70.0 1.4 copy-start.1
  71.3 0.6 copy-start.4
  92.9 4.1 %copy-start.5 = (s32[16,8]{0,1:T(8,128)S(1)}, s32[16,8]{0,1:T(8,128)}, u32[]{:S(2)}) copy-start(s32[16,8]{0,1:T(8,128)} %param.8) | copy-start | bytes 1540
  92.9 37.3 %all-to-all-start.2 = ((bf16[16,64,640]{2,1,0:T(8,128)(2,1)}), bf16[16,64,640]{2,1,0:T(8,128)(2,1)S(1)}, u32[]{:S(2)}, u32[]{:S(2)}) async-start(bf16[16,64,640]{2,1,0:T(8,128)(2,1)} %bitcast.5), calls=%async_computation.2 | async-start | bytes 2621440 | tf_op jit(solution)/shard_map/all_to_all | solution.py:323
  97.1 8.0 %collective-permute-start = (s32[8,8]{1,0:T(8,128)S(1)}, s32[8,8]{1,0:T(8,128)S(1)}, u32[]{:S(2)}, u32[]{:S(2)}) collective-permute-start(s32[8,8]{1,0:T(8,128)S(1)} %get-tuple-element.18), channel_id=1, source_target_pairs={{16,0},{32,16},{48,32},{64,48},{80,64},{96,80},{112,96},{128,112},... | collective-permute-start | bytes 776 | tf_op jit(solution)/shard_map/ppermute | solution.py:300
  140.6 31.1 %collective-permute-start.4 = (bf16[1552,128]{1,0:T(8,128)(2,1)}, bf16[1552,128]{1,0:T(8,128)(2,1)S(1)}, u32[]{:S(2)}, u32[]{:S(2)}) collective-permute-start(bf16[1552,128]{1,0:T(8,128)(2,1)} %get-tuple-element.15), channel_id=1, source_target_pairs={{0,16},{16,32},{32,48},{48,64},{64,80},{80,96},{96,112},{112,128},... | collective-permute-start | bytes 1191944 | tf_op jit(solution)/shard_map/ppermute | solution.py:350
Sparse Core Ops, SparseCore 0:
  28.0 63.1 all-gather.2

commit v9 on v7

--- a/solution.py
+++ b/solution.py
@@ -254,6 +254,7 @@
         out_shape=jax.ShapeDtypeStruct((tm_count, part, (chips // 2 + 1) * (all_hours // chips)), BF16),
         in_specs=[SMEM, VMEM],
         out_specs=VMEM,
+        compiler_params=pltpu.CompilerParams(vmem_limit_bytes=8 * 2**20),
         name="spread",
     )(chip, temporal_cov)
     mine = lax.all_to_all(spread_rows, TM, split_axis=0, concat_axis=0, tiled=True)
@@ -265,6 +266,7 @@
         ),
         in_specs=[VMEM] * 2,
         out_specs=(VMEM, VMEM),
+        compiler_params=pltpu.CompilerParams(vmem_limit_bytes=8 * 2**20),
         name="pack",
     )(right_side, initial)
     from_next = [((r + 1) % regions, r) for r in range(regions)]
@@ -274,6 +276,7 @@
         out_shape=jax.ShapeDtypeStruct((width * n, n), BF16),
         in_specs=[VMEM],
         out_specs=VMEM,
+        compiler_params=pltpu.CompilerParams(vmem_limit_bytes=8 * 2**20),
         name="flip",
     )(keep_in_vmem(row))
     window_blocks = lax.all_gather(flipped[None], TM, axis=0, tiled=True)
@@ -284,6 +287,7 @@
         out_specs=pl.BlockSpec(memory_space=pl.ANY),
         scratch_shapes=[pltpu.SemaphoreType.DMA],
         input_output_aliases={0: 0},
+        compiler_params=pltpu.CompilerParams(vmem_limit_bytes=8 * 2**20),
         name="merge",
     )(field, keep_in_vmem(shifted))
     local_slots = lax.rem(neighbour_blocks, rows)
@@ -313,7 +317,7 @@
             jax.ShapeDtypeStruct((tm_count, 8, n), F32),
             jax.ShapeDtypeStruct((8, n), F32),
         ),
-        in_specs=[SMEM, VMEM, VMEM, VMEM, pl.BlockSpec(memory_space=pl.ANY)],
+        in_specs=[SMEM, VMEM, VMEM, VMEM, pl.BlockSpec(memory_space=pltpu.MemorySpace.HBM)],
         out_specs=(VMEM,) * 4,
         scratch_shapes=[
             pltpu.VMEM((rows, width * n, n), BF16),

time: 180 us -> 180 us (level)
  Pallas kernels: 22.3 us -> 20.3 us
  transfers between devices with their start and end apart: 9 -> 9, of which waited for: 6 -> 6; matrix products, arithmetic and copies ran while one was open for 0% -> 0% of each run, Pallas kernels for 5% -> 4%
where the time goes in v9:
time: 180 us
  waiting for transfers between devices  67.8 us (38%)
  starting transfers between devices  46.6 us (26%)
  blocking collectives  29 us (16%)
  Pallas kernels  20.3 us (11%)
  between operations  14.1 us (8%)
    all_to_all x1, waiting for transfers between devices, steps(): lax.all_to_all(powers.reshape(tm_count, hours, 5 * n), TM, split_axis=0,...  24.7 us
    all_to_all x1, waiting for transfers between devices, steps(): arrived = lax.all_to_all(xd, TM, split_axis=0, concat_axis=0, tiled=True)  19.9 us
    all_to_all x1, blocking collectives, steps(): lax.all_to_all(spread, REGION, split_axis=0, concat_axis=0, tiled=True)  17.4 us
    ppermute x1, starting transfers between devices, steps(): row = lax.ppermute(blocks[0], REGION_TM, pairs)  13.7 us
    all_to_all x1, blocking collectives, steps(): over_tm = lax.all_to_all(gram, TM, split_axis=0, concat_axis=0, tiled=True)  11.6 us
    all_to_all x1, waiting for transfers between devices, steps(): lax.all_to_all(spread_rows, TM, split_axis=0, concat_axis=0, tiled=True)  10.9 us
    pallas_call x1, Pallas kernels, steps(): pl.pallas_call(spatial_kernel, out_shape=(jax.ShapeDtypeStruct((3 * half...  10.4 us
    ppermute x1, starting transfers between devices, steps(): shifted = lax.ppermute(packed, REGION, from_next)  7.31 us
  transfers between devices with their start and end apart: 9, of which 6 were waited for; matrix products, arithmetic and copies ran while one was open for 0% of the time, Pallas kernels for 4%

profile of v9, /device:TPU:1, one launch (start us, length us, event | category | flops | bytes accessed | tf_op | source)
XLA Modules:
  0.0 179.5 jit_solution(4598070990932540300)
XLA Ops:
  7.2 0.0 all-gather.3.cloned.1.call-start
  7.2 13.7 %collective-permute-start.3 = (bf16[9,128,128]{2,1,0:T(8,128)(2,1)}, bf16[9,128,128]{2,1,0:T(8,128)(2,1)S(1)}, u32[]{:S(2)}, u32[]{:S(2)}) collective-permute-start(bf16[9,128,128]{2,1,0:T(8,128)(2,1)} %bitcast.7), channel_id=1, source_target_pairs={{16,0},{17,1},{18,2},{19,3},{20,4},{21,5},{22,6},{23,7},{8,8},{9,9... | collective-permute-start | bytes 884744 | tf_op jit(solution)/shard_map/ppermute | solution.py:248
  20.9 6.0 %collective-permute-done.3.blocks_ref = bf16[9,128,128]{2,1,0:T(8,128)(2,1)S(1)} collective-permute-done((bf16[9,128,128]{2,1,0:T(8,128)(2,1)}, bf16[9,128,128]{2,1,0:T(8,128)(2,1)S(1)}, u32[]{:S(2)}, u32[]{:S(2)}) %collective-permute-start.3) | collective-permute-done | bytes 294944 | tf_op jit(solution)/shard_map/ppermute | solution.py:248
  26.9 0.9 flip.1
  27.7 0.0 all-gather.3.cloned.1.call-update
  27.8 0.0 copy-start.3
  27.8 1.0 copy-done.3
  28.8 0.9 spread.1
  29.7 6.4 %all-to-all-start = ((bf16[16,32,640]{2,1,0:T(8,128)(2,1)}), bf16[16,32,640]{2,1,0:T(8,128)(2,1)S(1)}, u32[]{:S(2)}, u32[]{:S(2)}) async-start(bf16[16,32,640]{2,1,0:T(8,128)(2,1)} %spread.1), calls=%async_computation | async-start | bytes 1310720 | tf_op jit(solution)/shard_map/all_to_all | solution.py:260
  36.1 0.0 copy-done
  36.1 0.8 pack.1
  37.0 7.3 %collective-permute-start.2 = (bf16[8,128,128]{2,1,0:T(8,128)(2,1)S(1)}, bf16[8,128,128]{2,1,0:T(8,128)(2,1)S(1)}, u32[]{:S(2)}, u32[]{:S(2)}) collective-permute-start(bf16[8,128,128]{2,1,0:T(8,128)(2,1)S(1)} %get-tuple-element.11), channel_id=1, source_target_pairs={{16,0},{32,16},{48,32},{64,48},{80,64},{96,80},{112,96},{128,112},... | collective-permute-start | bytes 786440 | tf_op jit(solution)/shard_map/ppermute | solution.py:273
  44.3 5.5 %collective-permute-done.2.arrived_ref = bf16[8,128,128]{2,1,0:T(8,128)(2,1)S(1)} collective-permute-done((bf16[8,128,128]{2,1,0:T(8,128)(2,1)S(1)}, bf16[8,128,128]{2,1,0:T(8,128)(2,1)S(1)}, u32[]{:S(2)}, u32[]{:S(2)}) %collective-permute-start.2) | collective-permute-done | bytes 262176 | tf_op jit(solution)/shard_map/ppermute | solution.py:273
  49.8 0.7 merge.1.xd_ref
  50.6 10.9 %all-to-all-done.own_ref = bf16[16,32,640]{2,1,0:T(8,128)(2,1)S(1)} async-done(((bf16[16,32,640]{2,1,0:T(8,128)(2,1)}), bf16[16,32,640]{2,1,0:T(8,128)(2,1)S(1)}, u32[]{:S(2)}, u32[]{:S(2)}) %all-to-all-start) | async-done | bytes 655392 | tf_op jit(solution)/shard_map/all_to_all | solution.py:260
  61.5 4.0 %all-to-all-start.1 = ((bf16[16,128,128]{2,1,0:T(8,128)(2,1)}), bf16[16,128,128]{2,1,0:T(8,128)(2,1)S(1)}, u32[]{:S(2)}, u32[]{:S(2)}) async-start(bf16[16,128,128]{2,1,0:T(8,128)(2,1)} %merge.1.xd_ref), calls=%async_computation.1 | async-start | bytes 1048576 | tf_op jit(solution)/shard_map/all_to_all | solution.py:298
  65.5 2.0 %collective-permute-start.1 = (bf16[16,32,640]{2,1,0:T(8,128)(2,1)S(1)}, bf16[16,32,640]{2,1,0:T(8,128)(2,1)S(1)}, u32[]{:S(2)}, u32[]{:S(2)}) collective-permute-start(bf16[16,32,640]{2,1,0:T(8,128)(2,1)S(1)} %all-to-all-done.own_ref), channel_id=1, source_target_pairs={{0,1},{1,0},{2,3},{3,2},{4,5},{5,4},{6,7},{7,6},{8,9},{9,8},{10,11... | collective-permute-start | bytes 1966088 | tf_op jit(solution)/shard_map/ppermute | solution.py:297
  67.5 19.9 %all-to-all-done.1.v_ref = bf16[16,128,128]{2,1,0:T(8,128)(2,1)S(1)} async-done(((bf16[16,128,128]{2,1,0:T(8,128)(2,1)}), bf16[16,128,128]{2,1,0:T(8,128)(2,1)S(1)}, u32[]{:S(2)}, u32[]{:S(2)}) %all-to-all-start.1) | async-done | bytes 524320 | tf_op jit(solution)/shard_map/all_to_all | solution.py:298
  87.4 0.0 collective-permute-done.1.other_ref
  87.4 4.0 %temporal.1 = (bf16[1024,640]{1,0:T(8,128)(2,1)}, f32[8,128]{1,0:T(8,128)}) custom-call(s32[1]{0:T(128)} %bitcast.core_ref, bf16[16,32,640]{2,1,0:T(8,128)(2,1)S(1)} %all-to-all-done.own_ref, bf16[16,32,640]{2,1,0:T(8,128)(2,1)S(1)} %collective-permute-done.1.other_ref, bf16[16,128,128]{2,1,0:T(8,128)(2,1)S(1)} %all-to-all-done.1.v_ref), custom_call_target="tpu_custom_call" | custom-call | tf_op jit(solution)/shard_map/temporal/pallas_call | solution.py:299
  91.5 4.0 %all-to-all-start.2 = ((bf16[16,64,640]{2,1,0:T(8,128)(2,1)}), bf16[16,64,640]{2,1,0:T(8,128)(2,1)S(1)}, u32[]{:S(2)}, u32[]{:S(2)}) async-start(bf16[16,64,640]{2,1,0:T(8,128)(2,1)} %bitcast.6), calls=%async_computation.2 | async-start | bytes 2621440 | tf_op jit(solution)/shard_map/all_to_all | solution.py:310
  95.5 0.1 copy.8
  95.6 7.2 %collective-permute-start = (s32[8,8]{1,0:T(8,128)S(1)}, s32[8,8]{1,0:T(8,128)S(1)}, u32[]{:S(2)}, u32[]{:S(2)}) collective-permute-start(s32[8,8]{1,0:T(8,128)S(1)} %get-tuple-element.18), channel_id=1, source_target_pairs={{16,0},{32,16},{48,32},{64,48},{80,64},{96,80},{112,96},{128,112},... | collective-permute-start | bytes 776 | tf_op jit(solution)/shard_map/ppermute | solution.py:294
  102.8 0.7 collective-permute-done
  103.5 0.6 pad_add_fusion.slots_ref
  104.1 24.7 %all-to-all-done.2.g_ref = bf16[16,64,640]{2,1,0:T(8,128)(2,1)S(1)} async-done(((bf16[16,64,640]{2,1,0:T(8,128)(2,1)}), bf16[16,64,640]{2,1,0:T(8,128)(2,1)S(1)}, u32[]{:S(2)}, u32[]{:S(2)}) %all-to-all-start.2) | async-done | bytes 1310752 | tf_op jit(solution)/shard_map/all_to_all | solution.py:310
  128.8 10.4 %spatial.1 = (bf16[1552,128]{1,0:T(8,128)(2,1)}, f32[3,8,64,128]{3,2,1,0:T(8,128)}, f32[16,8,128]{2,1,0:T(8,128)}, f32[8,128]{1,0:T(8,128)}) custom-call(s32[16,8]{1,0:T(8,128)} %pad_add_fusion.slots_ref, bf16[16,64,640]{2,1,0:T(8,128)(2,1)S(1)} %all-to-all-done.2.g_ref, bf16[16,128,128]{2,1,0:T(8,128)(2,1)} %merge.1.xd_ref, ...), custom_call_target="tpu_custom_call" | custom-call | tf_op jit(solution)/shard_map/spatial/pallas_call | solution.py:312
  139.2 1.9 %collective-permute-start.4 = (bf16[1552,128]{1,0:T(8,128)(2,1)}, bf16[1552,128]{1,0:T(8,128)(2,1)S(1)}, u32[]{:S(2)}, u32[]{:S(2)}) collective-permute-start(bf16[1552,128]{1,0:T(8,128)(2,1)} %get-tuple-element.15), channel_id=1, source_target_pairs={{0,16},{16,32},{32,48},{48,64},{64,80},{80,96},{96,112},{112,128},... | collective-permute-start | bytes 1191944 | tf_op jit(solution)/shard_map/ppermute | solution.py:337
  141.1 11.6 %all_to_all.25 = f32[16,8,128]{2,1,0:T(8,128)S(1)} all-to-all(f32[16,8,128]{2,1,0:T(8,128)} %get-tuple-element.14), channel_id=1, replica_groups=mesh['region_0'=4,'region_1'=8,'tm_0'=8,'tm_1'=2] {'tm_0','tm_1'}, dimensions={0} | all-to-all | bytes 131072 | tf_op jit(solution)/shard_map/all_to_all | solution.py:338
  152.7 17.4 %all_to_all.26.gram_ref = f32[32,8,128]{2,1,0:T(8,128)} all-to-all(f32[32,8,128]{2,1,0:T(8,128)S(1)} %broadcast_in_dim.10), channel_id=1, replica_groups=mesh['region_0'=4,'region_1'=8,'tm_0'=8,'tm_1'=2] {'region_0','region_1'}, dimensions={0} | all-to-all | bytes 262144 | tf_op jit(solution)/shard_map/all_to_all | solution.py:340
  170.2 0.0 collective-permute-done.4.low_ref
  170.2 2.5 %finish.1 = (f32[64,2048]{1,0:T(8,128)}, f32[64,2048]{1,0:T(8,128)}) custom-call(f32[32,8,128]{2,1,0:T(8,128)} %all_to_all.26.gram_ref, f32[64,2048]{1,0:T(8,128)S(1)} %copy-done.1, bf16[1552,128]{1,0:T(8,128)(2,1)S(1)} %collective-permute-done.4.low_ref, f32[3,8,64,128]{3,2,1,0:T(8,128)} %get-tuple-element.16.high_ref, f32[8,128]{1,0:T(8,128)} %get-tuple-element.17.centre_ref), custom_call_target="tpu_custom_call" | custom-call | tf_op jit(solution)/shard_map/finish/pallas_call | solution.py:341
  (12 shorter events, 0.1 us)
Async XLA Ops:
  7.2 121.6 %all-gather.3.cloned.1.call-start = ((), (), s32[]{:S(2)}) async-start(), calls=%async_computation.5 | async-start | bytes 5013504 | tf_op jit(solution)/shard_map/all_gather | solution.py:282
  7.2 19.7 %collective-permute-start.3 = (bf16[9,128,128]{2,1,0:T(8,128)(2,1)}, bf16[9,128,128]{2,1,0:T(8,128)(2,1)S(1)}, u32[]{:S(2)}, u32[]{:S(2)}) collective-permute-start(bf16[9,128,128]{2,1,0:T(8,128)(2,1)} %bitcast.7), channel_id=1, source_target_pairs={{16,0},{17,1},{18,2},{19,3},{20,4},{21,5},{22,6},{23,7},{8,8},{9,9... | collective-permute-start | bytes 884744 | tf_op jit(solution)/shard_map/ppermute | solution.py:248
  27.7 8.4 %copy-start = (f32[64,2048]{1,0:T(8,128)S(1)}, f32[64,2048]{1,0:T(8,128)}, u32[]{:S(2)}) copy-start(f32[64,2048]{1,0:T(8,128)} %x_ref.1) | copy-start | bytes 1572868
  27.7 8.4 %copy-start.2 = (f32[64,2048]{1,0:T(8,128)S(1)}, f32[64,2048]{1,0:T(8,128)}, u32[]{:S(2)}) copy-start(f32[64,2048]{1,0:T(8,128)} %right_ref.1) | copy-start | bytes 1572868
  27.8 1.0 copy-start.3
  29.7 31.8 %all-to-all-start = ((bf16[16,32,640]{2,1,0:T(8,128)(2,1)}), bf16[16,32,640]{2,1,0:T(8,128)(2,1)S(1)}, u32[]{:S(2)}, u32[]{:S(2)}) async-start(bf16[16,32,640]{2,1,0:T(8,128)(2,1)} %spread.1), calls=%async_computation | async-start | bytes 1310720 | tf_op jit(solution)/shard_map/all_to_all | solution.py:260
  37.0 12.9 %collective-permute-start.2 = (bf16[8,128,128]{2,1,0:T(8,128)(2,1)S(1)}, bf16[8,128,128]{2,1,0:T(8,128)(2,1)S(1)}, u32[]{:S(2)}, u32[]{:S(2)}) collective-permute-start(bf16[8,128,128]{2,1,0:T(8,128)(2,1)S(1)} %get-tuple-element.11), channel_id=1, source_target_pairs={{16,0},{32,16},{48,32},{64,48},{80,64},{96,80},{112,96},{128,112},... | collective-permute-start | bytes 786440 | tf_op jit(solution)/shard_map/ppermute | solution.py:273
  61.5 25.9 %all-to-all-start.1 = ((bf16[16,128,128]{2,1,0:T(8,128)(2,1)}), bf16[16,128,128]{2,1,0:T(8,128)(2,1)S(1)}, u32[]{:S(2)}, u32[]{:S(2)}) async-start(bf16[16,128,128]{2,1,0:T(8,128)(2,1)} %merge.1.xd_ref), calls=%async_computation.1 | async-start | bytes 1048576 | tf_op jit(solution)/shard_map/all_to_all | solution.py:298
  65.5 21.9 %collective-permute-start.1 = (bf16[16,32,640]{2,1,0:T(8,128)(2,1)S(1)}, bf16[16,32,640]{2,1,0:T(8,128)(2,1)S(1)}, u32[]{:S(2)}, u32[]{:S(2)}) collective-permute-start(bf16[16,32,640]{2,1,0:T(8,128)(2,1)S(1)} %all-to-all-done.own_ref), channel_id=1, source_target_pairs={{0,1},{1,0},{2,3},{3,2},{4,5},{5,4},{6,7},{7,6},{8,9},{9,8},{10,11... | collective-permute-start | bytes 1966088 | tf_op jit(solution)/shard_map/ppermute | solution.py:297
  91.5 4.0 %copy-start.4 = (s32[16,8]{0,1:T(8,128)S(1)}, s32[16,8]{0,1:T(8,128)}, u32[]{:S(2)}) copy-start(s32[16,8]{0,1:T(8,128)} %param.8) | copy-start | bytes 1540
  91.5 37.3 %all-to-all-start.2 = ((bf16[16,64,640]{2,1,0:T(8,128)(2,1)}), bf16[16,64,640]{2,1,0:T(8,128)(2,1)S(1)}, u32[]{:S(2)}, u32[]{:S(2)}) async-start(bf16[16,64,640]{2,1,0:T(8,128)(2,1)} %bitcast.6), calls=%async_computation.2 | async-start | bytes 2621440 | tf_op jit(solution)/shard_map/all_to_all | solution.py:310
  95.6 7.9 %collective-permute-start = (s32[8,8]{1,0:T(8,128)S(1)}, s32[8,8]{1,0:T(8,128)S(1)}, u32[]{:S(2)}, u32[]{:S(2)}) collective-permute-start(s32[8,8]{1,0:T(8,128)S(1)} %get-tuple-element.18), channel_id=1, source_target_pairs={{16,0},{32,16},{48,32},{64,48},{80,64},{96,80},{112,96},{128,112},... | collective-permute-start | bytes 776 | tf_op jit(solution)/shard_map/ppermute | solution.py:294
  128.8 41.4 %copy-start.1 = (f32[64,2048]{1,0:T(8,128)S(1)}, f32[64,2048]{1,0:T(8,128)}, u32[]{:S(2)}) copy-start(f32[64,2048]{1,0:T(8,128)} %x_ref.1) | copy-start | bytes 1572868
  139.2 31.0 %collective-permute-start.4 = (bf16[1552,128]{1,0:T(8,128)(2,1)}, bf16[1552,128]{1,0:T(8,128)(2,1)S(1)}, u32[]{:S(2)}, u32[]{:S(2)}) collective-permute-start(bf16[1552,128]{1,0:T(8,128)(2,1)} %get-tuple-element.15), channel_id=1, source_target_pairs={{0,16},{16,32},{32,48},{48,64},{64,80},{80,96},{96,112},{112,128},... | collective-permute-start | bytes 1191944 | tf_op jit(solution)/shard_map/ppermute | solution.py:337
Sparse Core Ops, SparseCore 0:
  27.9 63.2 all-gather.2
